TPU v7x, 128 devices: a whole 4x4x4 slice. The times are simulated.
128 devices in a mesh: lev: 4 (over x), lat: 32 (over y, z, core).
Axes of the slice: x: 4, y: 4, z: 4, core: 2. Of those that a mesh axis runs over, the one named last changes fastest.
Arguments:
- grid_values: bfloat16 [64, 1280, 2560], P(None, 'lat', 'lev'), may hold values from -6 to 6
- basis_table: bfloat16 [640, 640, 1281], P(None, ('lev', 'lat')), may hold values from -6 to 6
- damping_rates: float32 [64], replicated, may hold values from 0.5 to 8
- pair_table: int32 [640], replicated, may hold values from 0 to 639, each once
Outputs:
- coefficients: bfloat16 [160, 4, 2, 64, 1281], P('lat', None, None, 'lev')
Inputs may be any that keep to these rules, and one draw needn't show every extreme that they name: `pair_table`: each pair index appears in exactly one slot; the pair p stands for the wavenumbers p and 1279 - p.
All inputs are finite; a program needn't handle non-finite values.
Results may differ from a plain program's by a relative error of at most 0.0062.
Values may be sent and summed in bfloat16 or wider, within the bound.
No kernel may reach another device: no remote copies, remote signals or barrier semaphores. Data moves between devices by JAX's collectives and lax.ppermute only.
A program may use at most 128 MiB of HBM per device.

v0:
```python
import math

import jax
import jax.numpy as jnp
from jax import lax
from jax.sharding import PartitionSpec as P


def circle_rows(wave_numbers, lon_count):
    longitude = jnp.arange(lon_count, dtype=jnp.int32)
    phase = wave_numbers[..., None] * longitude % lon_count
    angle = phase.astype(jnp.float32) * (2.0 * math.pi / lon_count)
    return jnp.stack([jnp.cos(angle), -jnp.sin(angle)], axis=-2).astype(jnp.bfloat16)


def per_device(grid_values, basis_table, damping_rates, pair_table):
    lev_count = lax.axis_size("lev")
    lat_count = lax.axis_size("lat")
    dev_count = lev_count * lat_count
    level_block = grid_values.shape[0] // lev_count
    lat_band = grid_values.shape[1]
    lon_count = grid_values.shape[2] * lev_count
    pair_slots = basis_table.shape[1]
    col_count = basis_table.shape[2]
    wave_count = col_count - 1
    top_wave = wave_count - 1
    member_waves = jnp.stack([pair_table, top_wave - pair_table], axis=1)
    circle = circle_rows(jnp.arange(wave_count, dtype=jnp.int32), lon_count).reshape(
        2 * wave_count, lon_count
    )
    row_index = (member_waves[:, :, None] * 2 + jnp.arange(2, dtype=jnp.int32)).reshape(-1)
    widened = lax.all_to_all(grid_values, "lev", split_axis=0, concat_axis=2, tiled=True).astype(
        jnp.float32
    )
    squared = (widened * jnp.abs(widened)).astype(jnp.bfloat16)
    spectra = lax.dot_general(
        circle, squared, (((1,), (2,)), ((), ())), preferred_element_type=jnp.float32
    )
    spectra = jnp.take(spectra, row_index, axis=0)
    fourier = (spectra * (1.0 / lon_count)).astype(jnp.bfloat16)
    payload = fourier.reshape(dev_count, -1)
    received = lax.all_to_all(payload, ("lev", "lat"), split_axis=0, concat_axis=0, tiled=True)
    received = received.reshape(lev_count, lat_count, pair_slots, 2, 2, level_block, lat_band)
    half_bands = lat_count // 2
    north_rows = received[:, :half_bands]
    south_rows = received[:, half_bands:][:, ::-1, :, :, :, :, ::-1]
    basis_blocks = basis_table.reshape(half_bands, lat_band, pair_slots, col_count)
    north_prod = jnp.einsum(
        "vtkmrli,tikc->kvmrlc", north_rows, basis_blocks, preferred_element_type=jnp.float32
    )
    south_prod = jnp.einsum(
        "vtkmrli,tikc->kvmrlc", south_rows, basis_blocks, preferred_element_type=jnp.float32
    )
    flat_index = lax.axis_index("lev") * lat_count + lax.axis_index("lat")
    own_pairs = lax.dynamic_slice_in_dim(pair_table, flat_index * pair_slots, pair_slots)
    column_ids = jnp.arange(col_count, dtype=jnp.int32)
    second_member = column_ids[None, :] >= wave_count - own_pairs[:, None]
    degree = jnp.where(
        second_member, column_ids[None, :] - 1, own_pairs[:, None] + column_ids[None, :]
    )
    order_m = jnp.where(second_member, top_wave - own_pairs[:, None], own_pairs[:, None])
    parity_sign = jnp.where((degree - order_m) % 2 == 0, 1.0, -1.0).astype(jnp.float32)
    scaled = (degree * (degree + 1)).astype(jnp.float32) / float(top_wave * (top_wave + 1))
    member_mask = second_member[:, None, None, None, :]
    north_pick = jnp.where(member_mask, north_prod[:, :, 1], north_prod[:, :, 0])
    south_pick = jnp.where(member_mask, south_prod[:, :, 1], south_prod[:, :, 0])
    combined = north_pick + parity_sign[:, None, None, None, :] * south_pick
    rate_grid = damping_rates.reshape(lev_count, level_block)[None, :, None, :, None]
    factor = 1.0 / (1.0 + rate_grid * (scaled * scaled)[:, None, None, None, :])
    outgoing = (combined * factor).astype(jnp.bfloat16)
    return lax.all_to_all(outgoing, "lev", split_axis=1, concat_axis=1, tiled=True)


def solution(mesh):
    placed = (P(None, "lat", "lev"), P(None, ("lev", "lat"), None), P(), P())
    return jax.shard_map(
        per_device,
        mesh=mesh,
        in_specs=placed,
        out_specs=P("lat", None, None, "lev", None),
        check_vma=False,
    )
```

profile of v0, /device:TPU:0, one launch (start us, length us, event | category | flops | bytes accessed | tf_op | source)
XLA Modules:
  0.0 560.7 jit_solution(17677727837255381467)
XLA Ops:
  0.0 4.4 all-to-all-start
  4.4 55.2 %negate_convert_fusion = (bf16[1280,1,2560]{2,0,1:T(8,128)(2,1)}, bf16[1280,1,2560]{2,0,1:T(8,128)(2,1)}) fusion(), kind=kLoop, calls=%fused_computation.6 | loop fusion | flops 39321600 | bytes 13107200 | tf_op jit(solution)/shard_map/convert.3
  59.6 0.0 copy-done.2
  59.7 0.9 copy.44
  60.6 3.4 iota_add_fusion
  64.0 1.9 add.137
  65.9 1.9 add.133
  67.8 6.3 %pad_maximum_fusion = bf16[1280,2,2560]{2,0,1:T(8,128)(2,1)S(1)} fusion(bf16[1280,1,2560]{2,0,1:T(8,128)(2,1)} %get-tuple-element.11, bf16[1280,1,2560]{2,0,1:T(8,128)(2,1)} %get-tuple-element.12), kind=kLoop, calls=%fused_computation.5 | loop fusion | flops 6553600 | bytes 26214400 | tf_op jit(solution)/shard_map/stack | solution.py:13
  74.1 72.1 %copy.45 = bf16[1280,2,2560]{2,1,0:T(2,128)(2,1)} copy(bf16[1280,2,2560]{2,0,1:T(8,128)(2,1)S(1)} %pad_maximum_fusion) | data formatting | bytes 26214400 | tf_op jit(solution)/shard_map/stack | solution.py:13
  146.2 27.1 %reshape.328 = bf16[2560,2560,1]{1,0,2:T(8,128)(2,1)} reshape(bf16[1280,2,2560]{2,1,0:T(2,128)(2,1)} %copy.45) | data formatting | bytes 26214400 | tf_op jit(solution)/shard_map/convert_element_type | solution.py:13
  173.4 0.0 all-to-all-done
  173.4 0.0 copy-start
  173.4 0.8 fusion.22
  174.3 0.3 copy.67
  174.6 3.6 copy-done
  178.1 10.8 %fusion.31 = f32[2560,16,40]{0,2,1:T(8,128)} fusion(bf16[2560,2560,1]{1,0,2:T(8,128)(2,1)S(1)} %copy-done, bf16[16,40,2560]{2,1,0:T(8,128)(2,1)S(1)} %bitcast.62), kind=kOutput, calls=%fused_computation.57 | convolution fusion | flops 8388608000 | bytes 22937600 | tf_op jit(solution)/shard_map/dot_general | solution.py:36
  189.0 16.1 %copy.47 = f32[2560,16,40]{2,1,0:T(8,128)} copy(f32[2560,16,40]{0,2,1:T(8,128)} %fusion.31) | data formatting | bytes 13107200 | tf_op jit(solution)/shard_map/dot_general | solution.py:36
  205.0 18.0 %gather_fusion = f32[2560,16,40]{2,1,0:T(8,128)} fusion(f32[2560,16,40]{2,1,0:T(8,128)} %copy.47, s32[3072]{0:T(1024)S(1)} %pad_clamp_fusion), kind=kCustom, calls=%fused_computation | custom fusion | bytes 13117440 | tf_op jit(solution)/shard_map/jit(_take)/gather | solution.py:39
  223.0 12.9 %multiply_convert_fusion = bf16[2560,16,40]{2,1,0:T(8,128)(2,1)} fusion(f32[2560,16,40]{2,1,0:T(8,128)} %gather_fusion, pred[2560]{0:T(1024)(128)(4,1)S(1)} %compare_and_fusion), kind=kLoop, calls=%fused_computation.1 | loop fusion | flops 4915200 | bytes 9832960 | tf_op jit(solution)/shard_map/convert_element_type | solution.py:40
  236.0 25.7 %convert_element_type.80 = bf16[128,1,12800]{2,1,0:T(2,128)(2,1)} reshape(bf16[2560,16,40]{2,1,0:T(8,128)(2,1)} %multiply_convert_fusion) | data formatting | bytes 6553600 | tf_op jit(solution)/shard_map/convert_element_type | solution.py:40
  261.6 0.5 broadcast.291
  262.2 70.3 %reduce.3 = bf16[128,12800]{1,0:T(8,128)(2,1)S(1)} reduce(bf16[128,1,12800]{2,1,0:T(2,128)(2,1)} %convert_element_type.80, bf16[]{:T(256)} %broadcast.291), dimensions={1}, to_apply=%convert_element_type.80.reduce_sub_computation | reduce | bytes 6553602 | tf_op jit(solution)/shard_map/convert_element_type | solution.py:40
  332.4 0.0 copy-start.3
  332.4 2.5 reshape.335
  334.9 11.8 %all-to-all-start.1 = ((bf16[128,2,6400]{2,1,0:T(2,128)(2,1)}), bf16[128,2,6400]{2,1,0:T(2,128)(2,1)S(1)}, u32[]{:S(2)}, u32[]{:S(2)}) async-start(bf16[128,2,6400]{2,1,0:T(2,128)(2,1)} %reshape.335), calls=%async_computation.1 | async-start | bytes 6553600 | tf_op jit(solution)/shard_map/all_to_all | solution.py:42
  346.7 0.0 copy-done.3
  346.7 0.1 mul.149
  346.8 13.1 %copy.50 = bf16[640,5,1281]{2,0,1:T(8,128)(2,1)} copy(bf16[640,5,1281]{0,2,1:T(8,128)(2,1)} %param.5) | data formatting | bytes 16396800 | tf_op args[1]
  359.8 0.1 broadcast_subtract_fusion.1
  359.9 0.1 iota_compare_fusion
  360.0 0.1 fusion.28
  360.1 1.5 add_divide_fusion
  361.6 28.3 %all-to-all-done.1 = bf16[128,2,6400]{2,1,0:T(2,128)(2,1)S(1)} async-done(((bf16[128,2,6400]{2,1,0:T(2,128)(2,1)}), bf16[128,2,6400]{2,1,0:T(2,128)(2,1)S(1)}, u32[]{:S(2)}, u32[]{:S(2)}) %all-to-all-start.1) | async-done | bytes 3276832 | tf_op jit(solution)/shard_map/all_to_all | solution.py:42
  389.9 7.5 %reshape.336 = bf16[128,1,12800]{2,1,0:T(2,128)(2,1)} reshape(bf16[128,2,6400]{2,1,0:T(2,128)(2,1)S(1)} %all-to-all-done.1) | data formatting | bytes 6553600
  397.4 69.6 %reduce.1 = bf16[128,12800]{1,0:T(8,128)(2,1)S(1)} reduce(bf16[128,1,12800]{2,1,0:T(2,128)(2,1)} %reshape.336, bf16[]{:T(256)} %constant.82), dimensions={1}, to_apply=%all_to_all.15.reduce_sub_computation | reduce | bytes 6553602 | tf_op jit(solution)/shard_map/all_to_all | solution.py:42
  467.0 20.0 %reshape.317 = bf16[4,32,5,2,2,16,40]{6,5,4,3,2,1,0:T(8,128)(2,1)} reshape(bf16[128,12800]{1,0:T(8,128)(2,1)S(1)} %reduce.1) | data formatting | bytes 6553600 | tf_op jit(solution)/shard_map/reshape | solution.py:43
  487.0 11.3 %fusion.30 = (bf16[4,16,5,2,2,16,40]{6,5,4,3,2,1,0:T(8,128)(2,1)}, bf16[4,16,5,2,2,16,40]{6,5,4,3,2,1,0:T(8,128)(2,1)}) fusion(bf16[4,32,5,2,2,16,40]{6,5,4,3,2,1,0:T(8,128)(2,1)} %reshape.317), kind=kLoop, calls=%fused_computation.56 | loop fusion | bytes 6553600 | tf_op jit(solution)/shard_map/slice | solution.py:45
  498.3 13.7 %rev.3 = bf16[4,16,5,2,2,16,40]{6,5,4,3,2,1,0:T(8,128)(2,1)} reverse(bf16[4,16,5,2,2,16,40]{6,5,4,3,2,1,0:T(8,128)(2,1)} %get-tuple-element.8), dimensions={1,6} | reverse | bytes 3276800 | tf_op jit(solution)/shard_map/rev | solution.py:46
  512.0 8.1 %fusion.13 = f32[5,4,2,2,16,1281]{5,4,3,2,1,0:T(8,128)S(1)} fusion(bf16[16,40,5,1281,1,1,1]{3,1,0,6,5,4,2:T(8,128)(2,1)} %bitcast.58, bf16[4,16,5,2,2,16,40]{6,5,4,3,2,1,0:T(8,128)(2,1)} %get-tuple-element.7), kind=kOutput, calls=%fused_computation.20 | convolution fusion | flops 2098790400 | bytes 16395520 | tf_op jit(solution)/shard_map/vtkmrli,tikc->kvmrlc/dot_general | solution.py:48
  520.1 0.0 slice-done
  520.1 0.0 slice-done.1
  520.1 0.0 slice-done.2
  520.1 0.0 copy-start.1
  520.1 9.2 %fusion.10 = f32[5,4,2,2,16,1281]{5,4,3,1,0,2:T(8,128)} fusion(bf16[16,40,5,1281,1,1,1]{3,1,0,6,4,2,5:T(8,128)(2,1)S(1)} %bitcast.61, bf16[4,16,5,2,2,16,40]{6,5,4,3,2,1,0:T(8,128)(2,1)} %rev.3), kind=kOutput, calls=%fused_computation.19 | convolution fusion | flops 2098790400 | bytes 16395520 | tf_op jit(solution)/shard_map/vtkmrli,tikc->kvmrlc/dot_general | solution.py:51
  529.3 3.9 fusion.20
  533.3 0.1 copy.55
  533.4 25.4 %all_to_all.20 = bf16[5,4,2,16,1281]{4,3,2,0,1:T(8,128)(2,1)S(1)} all-to-all(bf16[5,4,2,16,1281]{4,3,2,0,1:T(8,128)(2,1)S(1)} %copy.55), channel_id=1, replica_groups=mesh['lev'=4,'lat'=32] {'lev'}, dimensions={1} | all-to-all | bytes 3279360 | tf_op jit(solution)/shard_map/all_to_all | solution.py:71
  558.8 1.4 copy.56
  (15 shorter events, 0.1 us)
Async XLA Ops:
  0.0 173.4 %all-to-all-start = ((bf16[64,40,640]{2,1,0:T(8,128)(2,1)}), bf16[64,40,640]{2,1,0:T(8,128)(2,1)S(1)}, u32[]{:S(2)}, u32[]{:S(2)}) async-start(bf16[64,40,640]{2,1,0:T(8,128)(2,1)} %param.4), calls=%async_computation | async-start | bytes 6553600 | tf_op jit(solution)/shard_map/all_to_all | solution.py:32
  4.4 55.2 %copy-start.2 = (s32[640]{0:T(1024)S(1)}, s32[640]{0:T(1024)}, u32[]{:S(2)}) copy-start(s32[640]{0:T(1024)} %param.7) | copy-start | bytes 7684
  173.4 4.7 copy-start
  332.4 14.3 %copy-start.3 = (f32[64]{0:T(128)S(1)}, f32[64]{0:T(128)}, u32[]{:S(2)}) copy-start(f32[64]{0:T(128)} %param.6) | copy-start | bytes 772
  334.9 55.0 %all-to-all-start.1 = ((bf16[128,2,6400]{2,1,0:T(2,128)(2,1)}), bf16[128,2,6400]{2,1,0:T(2,128)(2,1)S(1)}, u32[]{:S(2)}, u32[]{:S(2)}) async-start(bf16[128,2,6400]{2,1,0:T(2,128)(2,1)} %reshape.335), calls=%async_computation.1 | async-start | bytes 6553600 | tf_op jit(solution)/shard_map/all_to_all | solution.py:42
  498.3 21.7 %slice-start = ((s8[9011200]{0:T(1024)(128)(4,1)}), s8[622592]{0:T(1024)(128)(4,1)S(1)}, s32[]{:S(2)}) async-start(s8[9011200]{0:T(1024)(128)(4,1)} %bitcast.59), calls=%async_computation.3 | async-start | bytes 1245184
  512.0 8.1 %slice-start.1 = ((s8[9011200]{0:T(1024)(128)(4,1)}), s8[4194304]{0:T(1024)(128)(4,1)S(1)}, s32[]{:S(2)}) async-start(s8[9011200]{0:T(1024)(128)(4,1)} %bitcast.59), calls=%async_computation.4 | async-start | bytes 8388608
  512.0 8.1 %slice-start.2 = ((s8[9011200]{0:T(1024)(128)(4,1)}), s8[4194304]{0:T(1024)(128)(4,1)S(1)}, s32[]{:S(2)}) async-start(s8[9011200]{0:T(1024)(128)(4,1)} %bitcast.59), calls=%async_computation.5 | async-start | bytes 8388608
  520.1 9.2 %copy-start.1 = (f32[5,4,16,1281]{3,2,1,0:T(8,128)S(1)}, f32[5,4,16,1281]{3,2,1,0:T(8,128)}, u32[]{:S(2)}) copy-start(f32[5,4,16,1281]{3,2,1,0:T(8,128)} %add_divide_fusion) | copy-start | bytes 4919044
where the time goes:
time: 572 us; the launch traced here: 561 us
  local copies, waits for them, and re-layouts  238 us (42%)
  other arithmetic  224 us (39%)
  waiting for transfers between devices  28.3 us (5%)
  matrix products  28.1 us (5%)
  blocking collectives  25.4 us (4%)
  starting transfers between devices  16.2 us (3%)
    convert_element_type x2, other arithmetic, per_device(): fourier = (spectra * (1.0 / lon_count)).astype(jnp.bfloat16)  83.2 us
    another operation x1, local copies, waits for them, and re-layouts, circle_rows(): jnp.stack([jnp.cos(angle), -jnp.sin(angle)], axis=-2).astype(jnp.bfloat16)  72.1 us
    all_to_all x1, other arithmetic, per_device(): lax.all_to_all(payload, ('lev', 'lat'), split_axis=0, concat_axis=0, tile...  69.6 us
    another operation x1, other arithmetic  55.2 us
    all_to_all x1, waiting for transfers between devices, per_device(): lax.all_to_all(payload, ('lev', 'lat'), split_axis=0, concat_axis=0, tile...  28.3 us
    convert_element_type x1, local copies, waits for them, and re-layouts, circle_rows(): jnp.stack([jnp.cos(angle), -jnp.sin(angle)], axis=-2).astype(jnp.bfloat16)  27.1 us
    unnamed x17, local copies, waits for them, and re-layouts  26.6 us
    convert_element_type x2, local copies, waits for them, and re-layouts, per_device(): fourier = (spectra * (1.0 / lon_count)).astype(jnp.bfloat16)  26.2 us
  transfers between devices with their start and end apart: 2, of which 1 were waited for; matrix products, arithmetic and copies ran while one was open for 33% of the time, Pallas kernels for 0%

commit v1 on v0

v1 whole, which is shorter than its diff:
```python
import functools
import math

import jax
import jax.numpy as jnp
import numpy as np
from jax import lax
from jax.experimental import pallas as pl
from jax.experimental.pallas import tpu as pltpu
from jax.sharding import PartitionSpec as P

F32 = jnp.float32
BF16 = jnp.bfloat16
NT = (((1,), (1,)), ((), ()))
NN = (((1,), (0,)), ((), ()))
LANES = 128
VMEM_BYTES = 60 * 1024 * 1024


COS_TERMS = [((-1) ** n) * (2 * math.pi) ** (2 * n) / math.factorial(2 * n) for n in range(10)]


def cos_turns(turns):
    part = turns - jnp.floor(turns + 0.5)
    square = part * part
    total = jnp.full_like(square, COS_TERMS[-1])
    for term in COS_TERMS[-2::-1]:
        total = total * square + term
    return total


def circle_kernel(lon_count, wave_ref, quarter_ref, out_ref):
    rows, cols = out_ref.shape
    wave = wave_ref[...].astype(F32)
    quarter = quarter_ref[...].astype(F32) * 0.25
    lane = lax.broadcasted_iota(jnp.int32, (rows, LANES), 1).astype(F32)

    def at(offset):
        product = wave * (lane + offset)
        product = product - jnp.floor(product * (1.0 / lon_count)) * lon_count
        return cos_turns(product * (1.0 / lon_count) + quarter)

    step = wave * float(LANES)
    step = step - jnp.floor(step * (1.0 / lon_count)) * lon_count
    twice = 2.0 * cos_turns(step * (1.0 / lon_count))
    before, now = at(0.0), at(float(LANES))
    out_ref[:, :LANES] = before.astype(BF16)
    out_ref[:, LANES : 2 * LANES] = now.astype(BF16)
    for tile in range(2, cols // LANES):
        before, now = now, twice * now - before
        out_ref[:, tile * LANES : (tile + 1) * LANES] = now.astype(BF16)


def circle_table(waves, quarters, lon_count, cols):
    rows = waves.shape[0]
    block = 64
    spread = lambda v: jnp.broadcast_to(v[:, None], (rows, LANES))
    return pl.pallas_call(
        functools.partial(circle_kernel, lon_count),
        grid=(rows // block,),
        in_specs=[pl.BlockSpec((block, LANES), lambda i: (i, 0))] * 2,
        out_specs=pl.BlockSpec((block, cols), lambda i: (i, 0)),
        out_shape=jax.ShapeDtypeStruct((rows, cols), BF16),
        cost_estimate=pl.CostEstimate(
            flops=rows * cols * 10, bytes_accessed=rows * cols * 2, transcendentals=0
        ),
        name="circle",
    )(spread(waves), spread(quarters))


def fourier_kernel(south_ref, g_ref, circle_ref, spread_ref, lane_ref, out_ref, fold_ref):
    dests = out_ref.shape[0]
    quarter = g_ref.shape[2]
    lats = g_ref.shape[1]
    bands = g_ref.shape[0] // 4
    tiles = bands * lats // LANES
    main = dests * 8

    @pl.when(pl.program_id(0) == 0)
    def _():
        def step(b, carry):
            def squared(q):
                value = g_ref[pl.ds(q * bands + 2 * b, 2)].astype(F32)
                return (value * jnp.abs(value)).reshape(2 * lats, quarter)

            rows = pl.ds(pl.multiple_of(b * 2 * lats, 16), 2 * lats)
            for half in range(2):
                near, far = squared(half), squared(half + 2)
                cols = slice(half * quarter, (half + 1) * quarter)
                fold_ref[0, rows, cols] = (near + far).astype(BF16)
                fold_ref[1, rows, cols] = (near - far).astype(BF16)
            return carry

        lax.fori_loop(0, bands // 2, step, 0)

    south = south_ref[0]
    pieces = []
    for tile in range(tiles):
        rows = slice(tile * LANES, (tile + 1) * LANES)
        both = []
        for kind in range(2):
            value = lax.dot_general(
                circle_ref[0, kind], fold_ref[kind, rows, :], NT, preferred_element_type=F32
            )
            index = jnp.broadcast_to(lane_ref[0:1, :], value.shape)
            value = jnp.take_along_axis(value, index, axis=1, mode="promise_in_bounds")
            both.append(value[:main].reshape(dests, 8, LANES))
            pieces.append(value[main:].astype(BF16))
        place = jnp.where(south == 1, tiles - 1 - tile, tile)
        out_ref[:, pl.ds(pl.multiple_of(place * 16, 16), 16), :] = jnp.concatenate(
            both, axis=1
        ).astype(BF16)
    last = jnp.concatenate(pieces, axis=0)
    moved = lax.dot_general(spread_ref[...], last, NN, preferred_element_type=F32)
    out_ref[:, tiles * 16 :, :] = moved.reshape(dests, 24, LANES).astype(BF16)


def fourier(south, received, circle, spread, lane_index, dev_count):
    steps = circle.shape[0]
    dests = dev_count // steps
    bands4, lats, quarter = received.shape
    lat_half = bands4 // 4 * lats
    tiles = lat_half // LANES
    rows = tiles * 16 + 24
    return pl.pallas_call(
        fourier_kernel,
        grid_spec=pltpu.PrefetchScalarGridSpec(
            num_scalar_prefetch=1,
            grid=(steps,),
            in_specs=[
                pl.BlockSpec(received.shape, lambda i, s: (0, 0, 0)),
                pl.BlockSpec((1,) + circle.shape[1:], lambda i, s: (i, 0, 0, 0)),
                pl.BlockSpec(spread.shape, lambda i, s: (0, 0)),
                pl.BlockSpec(lane_index.shape, lambda i, s: (0, 0)),
            ],
            out_specs=pl.BlockSpec((dests, rows, LANES), lambda i, s: (i, 0, 0)),
            scratch_shapes=[pltpu.VMEM((2, lat_half, 2 * quarter), BF16)],
        ),
        out_shape=jax.ShapeDtypeStruct((dev_count, rows, LANES), BF16),
        compiler_params=pltpu.CompilerParams(vmem_limit_bytes=VMEM_BYTES),
        name="fourier",
    )(south, received, circle, spread, lane_index)


def legendre_kernel(
    scale, norm, pairs_ref, recv_ref, basis_ref, rate_ref, mix_ref, tail_ref, last_ref, out_ref, x_ref
):
    slot = pl.program_id(0)
    levs = out_ref.shape[0]
    cols = basis_ref.shape[1]
    waves = cols - 1
    lat_half = basis_ref.shape[2]
    tiles = lat_half // LANES
    group = recv_ref.shape[0] // (2 * levs)

    @pl.when(slot == 0)
    def _():
        def step(x, carry):
            north = pl.ds(x * 2 * group, group)
            south = pl.ds(x * 2 * group + group, group)
            dest = pl.ds(pl.multiple_of(x * 32, 32), 32)

            def moved(rows, height, matrix):
                n = recv_ref[north, rows, :].reshape(group * height, LANES).astype(F32)
                s = recv_ref[south, rows, :].reshape(group * height, LANES).astype(F32)
                sides = jnp.concatenate([n + s, n - s], axis=1).astype(BF16)
                return lax.dot_general(
                    matrix, sides, NN, preferred_element_type=F32
                ).astype(BF16)

            for tile in range(tiles):
                value = moved(slice(tile * 16, tile * 16 + 16), 16, mix_ref[...])
                lanes = slice(tile * LANES, (tile + 1) * LANES)
                for k in range(4):
                    for kind in range(2):
                        part = value[(k * 2 + kind) * 32 : (k * 2 + kind + 1) * 32]
                        for par in range(2):
                            x_ref[k, par, kind, dest, lanes] = part[:, par * LANES : (par + 1) * LANES]
            base = tiles * 16
            value = moved(slice(base, base + 16), 16, tail_ref[...])
            end = moved(slice(base + 16, base + 24), 8, last_ref[...])
            for tile in range(tiles):
                lanes = slice(tile * LANES, (tile + 1) * LANES)
                for kind in range(2):
                    part = (
                        value[(tile * 2 + kind) * 32 : (tile * 2 + kind + 1) * 32]
                        if tile < 4
                        else end[kind * 32 : (kind + 1) * 32]
                    )
                    for par in range(2):
                        x_ref[4, par, kind, dest, lanes] = part[:, par * LANES : (par + 1) * LANES]
            return carry

        lax.fori_loop(0, levs, step, 0)

    pair = pairs_ref[slot]
    bound = waves - pair
    first_kind = lax.rem(pair, 2)
    rate = rate_ref[...]
    rows = levs * 32

    def damping(column, second):
        degree = jnp.where(second, column - 1, pair + column)
        scaled = (degree * (degree + 1)).astype(F32) / norm
        return scale / (1.0 + rate[:, : column.shape[1]] * (scaled * scaled))

    width = 256

    def block(start):
        column = start + lax.broadcasted_iota(jnp.int32, (1, width), 1)
        second = column >= bound
        even = lax.rem(jnp.where(second, column + pair, column), 2) == 0
        factor = damping(column, second)
        basis = basis_ref[0, start : start + width, :]

        def product(kind):
            left = x_ref[slot, :, kind].reshape(2 * rows, lat_half)
            both = lax.dot_general(left, basis, NT, preferred_element_type=F32)
            return jnp.where(even, both[:rows], both[rows:])

        whole = start >= bound
        value = product(jnp.where(whole, 1 - first_kind, first_kind)) * factor
        out_ref[:, 0, :, start : start + width] = value.astype(BF16).reshape(levs, 32, width)

        @pl.when((start < bound) & (bound < start + width))
        def _():
            other = product(1 - first_kind) * factor
            kept = jnp.where(second, other, value)
            out_ref[:, 0, :, start : start + width] = kept.astype(BF16).reshape(levs, 32, width)

    for start in range(0, waves, width):
        block(start)
    column = jnp.full((1, 1), waves, jnp.int32)
    left = x_ref[slot, first_kind, 1 - first_kind].astype(F32)
    final = jnp.sum(left * basis_ref[0, waves:cols, :].astype(F32), axis=1, keepdims=True)
    final = final * damping(column, column >= bound)
    out_ref[:, 0, :, waves:cols] = final.astype(BF16).reshape(levs, 32, 1)


def legendre(pairs, received, basis, rates, mix, tail, last, levs, lon_count, norm):
    slots, cols, lat_half = basis.shape
    whole = lambda a: pl.BlockSpec(a.shape, lambda k, p: (0,) * a.ndim)
    return pl.pallas_call(
        functools.partial(legendre_kernel, 1.0 / lon_count, norm),
        grid_spec=pltpu.PrefetchScalarGridSpec(
            num_scalar_prefetch=1,
            grid=(slots,),
            in_specs=[
                whole(received),
                pl.BlockSpec((1, cols, lat_half), lambda k, p: (k, 0, 0)),
                whole(rates),
                whole(mix),
                whole(tail),
                whole(last),
            ],
            out_specs=pl.BlockSpec((levs, 1, 32, cols), lambda k, p: (0, k, 0, 0)),
            scratch_shapes=[pltpu.VMEM((slots, 2, 2, levs * 32, lat_half), BF16)],
        ),
        out_shape=jax.ShapeDtypeStruct((levs, slots, 32, cols), BF16),
        compiler_params=pltpu.CompilerParams(vmem_limit_bytes=VMEM_BYTES),
        name="legendre",
    )(pairs, received, basis, rates, mix, tail, last)


def placing(out_rows, in_rows, target):
    goal = target(lax.broadcasted_iota(jnp.int32, (out_rows, in_rows), 1))
    return (goal == lax.broadcasted_iota(jnp.int32, (out_rows, in_rows), 0)).astype(BF16)


def per_device(grid_values, basis_table, damping_rates, pair_table):
    levs, lat_count = lax.axis_size("lev"), lax.axis_size("lat")
    dev_count = levs * lat_count
    half_bands = lat_count // 2
    lon_count = grid_values.shape[2] * levs
    slots, cols = basis_table.shape[1], basis_table.shape[2]
    top = cols - 2
    lat_half = basis_table.shape[0]
    tiles = lat_half // LANES
    group = half_bands
    me_lat = lax.axis_index("lat")
    flat = lax.axis_index("lev") * lat_count + me_lat
    south = (me_lat >= half_bands).astype(jnp.int32)

    groups = [
        [x * lat_count + h * half_bands + b for x in range(levs) for b in range(half_bands)]
        for h in range(2)
    ]
    circles = lax.all_to_all(
        grid_values, ("lev", "lat"), 0, 0, axis_index_groups=groups, tiled=True
    )

    steps = 4
    other = top - pair_table
    odd = pair_table % 2 == 1
    kinds = []
    for wave in (jnp.where(odd, other, pair_table), jnp.where(odd, pair_table, other)):
        wave = jnp.repeat(wave.reshape(steps, dev_count // steps, slots), 2, axis=2)
        head = wave[:, :, : 2 * slots - 2].reshape(steps, -1)
        kinds.append(jnp.concatenate([head, wave[:, :, 2 * slots - 2 :].reshape(steps, -1)], axis=1))
    waves = jnp.stack(kinds, axis=1)
    quarters = jnp.broadcast_to(jnp.arange(waves.shape[2], dtype=jnp.int32) % 2, waves.shape)
    circle = circle_table(
        waves.reshape(-1), quarters.reshape(-1), lon_count, lon_count // 2
    ).reshape(waves.shape + (lon_count // 2,))

    dests = dev_count // steps
    count = dests * 2

    def spread_target(i):
        tile, rest = i // (2 * count), i % (2 * count)
        kind, rest = rest // count, rest % count
        tile = jnp.where(south == 1, tiles - 1 - tile, tile)
        return (rest // 2) * 24 + tile * 4 + kind * 2 + rest % 2

    spread = placing(dests * 24, tiles * 2 * count, spread_target)
    lane = jnp.arange(LANES, dtype=jnp.int32)
    lane_index = jnp.broadcast_to(jnp.where(south == 1, LANES - 1 - lane, lane), (8, LANES))
    packed = fourier(south[None], circles, circle, spread, lane_index, dev_count)
    received = lax.all_to_all(packed, ("lev", "lat"), 0, 0, tiled=True)

    def mix_target(i):
        level, row = i // 16, i % 16
        kind, k, r = row // 8, row // 2 % 4, row % 2
        return ((k * 2 + kind) * 2 + r) * group + level

    def tail_target(i):
        level, row = i // 16, i % 16
        return row * group + level

    def last_target(i):
        level, row = i // 8, i % 8
        return row * group + level

    mix = placing(256, 256, mix_target)
    tail = placing(256, 256, tail_target)
    last = placing(64, 128, last_target)
    pairs = lax.dynamic_slice_in_dim(pair_table, flat * slots, slots)
    rates = jnp.broadcast_to(damping_rates.reshape(levs, 1, group), (levs, 2, group)).reshape(-1)
    rates = jnp.broadcast_to(rates[:, None], (rates.shape[0], 256))
    outgoing = legendre(
        pairs,
        received,
        jnp.transpose(basis_table, (1, 2, 0)),
        rates,
        mix,
        tail,
        last,
        levs,
        lon_count,
        float(top * (top + 1)),
    )
    result = lax.all_to_all(outgoing, "lev", 0, 0, tiled=True)
    return jnp.transpose(result, (1, 0, 2, 3)).reshape(slots, levs, 2, group, cols)


def solution(mesh):
    placed = (P(None, "lat", "lev"), P(None, ("lev", "lat"), None), P(), P())
    return jax.shard_map(
        per_device,
        mesh=mesh,
        in_specs=placed,
        out_specs=P("lat", None, None, "lev", None),
        check_vma=False,
    )
```

time: 572 us -> 170 us (0.30); the launches traced: 561 us -> 167 us
  local copies, waits for them, and re-layouts: 238 us -> 11.2 us
  other arithmetic: 224 us -> 2.6 us
  Pallas kernels: 0 us -> 52.3 us
  matrix products: 28.1 us -> 0 us
  waiting for transfers between devices: 28.3 us -> 54.6 us
    convert_element_type x3, other arithmetic: 87.1 us -> 2.52 us  [placing(): (goal == lax.broadcasted_iota(jnp.int32, (out_rows, in_rows), 0)).astype(...]
    another operation x3 -> x1, local copies, waits for them, and re-layouts: 72.1 us -> 0.01 us  [per_device(): waves = jnp.stack(kinds, axis=1)]
    all_to_all x1 -> x0, other arithmetic: 69.6 us -> none  [per_device(): lax.all_to_all(payload, ('lev', 'lat'), split_axis=0, concat_axis=0, tile...]
    another operation x2, other arithmetic: 61.5 us -> 0.01 us  [per_device(): waves = jnp.stack(kinds, axis=1)]
    convert_element_type x5 -> x0, local copies, waits for them, and re-layouts: 53.8 us -> none  [the longest x1 27.1 us: circle_rows(): jnp.stack([jnp.cos(angle), -jnp.sin(angle)], axis=-2).astype(jnp.bfloat16)]
    pallas_call x0 -> x3, Pallas kernels: none -> 52.3 us  [the longest x1 21.9 us: circle_table(): pl.pallas_call(functools.partial(circle_kernel, lon_count), grid=(rows //...]
    dot_general x3 -> x0, matrix products: 28.1 us -> none  [the longest x1 10.8 us: per_device(): lax.dot_general(circle, squared, (((1,), (2,)), ((), ())), preferred_elem...]
    all_to_all x2, waiting for transfers between devices: 28.3 us -> 54.6 us  [the longest x1 42.3 us: per_device(): received = lax.all_to_all(packed, ('lev', 'lat'), 0, 0, tiled=True)]
  transfers between devices with their start and end apart: 2 -> 2, of which waited for: 1 -> 2; matrix products, arithmetic and copies ran while one was open for 33% -> 5% of each run, Pallas kernels for 0% -> 13%
where the time goes in v1:
time: 170 us; the launch traced here: 167 us
  waiting for transfers between devices  54.6 us (32%)
  Pallas kernels  52.3 us (31%)
  blocking collectives  26.6 us (16%)
  starting transfers between devices  19.2 us (11%)
  local copies, waits for them, and re-layouts  11.2 us (7%)
  other arithmetic  2.6 us (2%)
    all_to_all x1, waiting for transfers between devices, per_device(): received = lax.all_to_all(packed, ('lev', 'lat'), 0, 0, tiled=True)  42.3 us
    all_to_all x1, blocking collectives, per_device(): result = lax.all_to_all(outgoing, 'lev', 0, 0, tiled=True)  26.6 us
    pallas_call x1, Pallas kernels, circle_table(): pl.pallas_call(functools.partial(circle_kernel, lon_count), grid=(rows //...  21.9 us
    pallas_call x1, Pallas kernels, legendre(): pl.pallas_call(functools.partial(legendre_kernel, 1.0 / lon_count, norm),...  15.4 us
    pallas_call x1, Pallas kernels, fourier(): pl.pallas_call(fourier_kernel, grid_spec=pltpu.PrefetchScalarGridSpec(num...  15 us
    all_to_all x1, waiting for transfers between devices, per_device(): lax.all_to_all(grid_values, ('lev', 'lat'), 0, 0, axis_index_groups=group...  12.3 us
    all_to_all x1, starting transfers between devices, per_device(): lax.all_to_all(grid_values, ('lev', 'lat'), 0, 0, axis_index_groups=group...  10 us
    all_to_all x1, starting transfers between devices, per_device(): received = lax.all_to_all(packed, ('lev', 'lat'), 0, 0, tiled=True)  9.2 us
  transfers between devices with their start and end apart: 2, of which 2 were waited for; matrix products, arithmetic and copies ran while one was open for 5% of the time, Pallas kernels for 13%

profile of v1, /device:TPU:0, one launch (start us, length us, event | category | flops | bytes accessed | tf_op | source)
XLA Modules:
  0.0 166.7 jit_solution(18017132242461524803)
XLA Ops:
  0.0 0.0 copy-start.2
  0.0 10.0 %all-to-all-start = ((bf16[64,40,640]{2,1,0:T(8,128)(2,1)}), bf16[64,40,640]{2,1,0:T(8,128)(2,1)S(1)}, u32[]{:S(2)}, u32[]{:S(2)}) async-start(bf16[64,40,640]{2,1,0:T(8,128)(2,1)} %param.4), calls=%async_computation | async-start | bytes 6553600 | tf_op jit(solution)/shard_map/all_to_all | solution.py:288
  10.1 0.0 copy-done.2
  10.1 0.2 reshape.35
  10.3 0.1 copy.6
  10.4 0.2 reshape.39
  10.6 0.1 copy.10
  10.7 0.1 copy.8
  10.8 0.1 copy.9
  10.9 0.1 copy.7
  11.0 0.1 reshape.37
  11.1 0.1 copy.12
  11.2 0.1 copy.13
  11.3 0.1 copy.11
  11.4 0.1 reshape.41
  11.5 0.1 broadcast_in_dim.46
  11.6 0.1 broadcast_in_dim.49
  11.7 2.0 %broadcast_in_dim.47.wave_ref = s32[2560,128]{1,0:T(8,128)} broadcast(s32[2560]{0:T(1024)S(1)} %broadcast_in_dim.46), dimensions={0} | broadcast | bytes 1320960 | tf_op jit(solution)/shard_map/broadcast_in_dim | solution.py:57
  13.7 2.0 %broadcast_in_dim.50.quarter_ref = s32[2560,128]{1,0:T(8,128)} broadcast(s32[2560]{0:T(1024)S(1)} %broadcast_in_dim.49), dimensions={0} | broadcast | bytes 1320960 | tf_op jit(solution)/shard_map/broadcast_in_dim | solution.py:57
  15.6 21.9 %circle.1 = bf16[2560,1280]{1,0:T(8,128)(2,1)} custom-call(s32[2560,128]{1,0:T(8,128)} %broadcast_in_dim.47.wave_ref, s32[2560,128]{1,0:T(8,128)} %broadcast_in_dim.50.quarter_ref), custom_call_target="tpu_custom_call" | custom-call | flops 32768000 | bytes 6553600 | tf_op jit(solution)/shard_map/circle/pallas_call | solution.py:58
  37.6 1.1 fusion.15.spread_ref
  38.7 12.3 %all-to-all-done.g_ref = bf16[64,40,640]{2,1,0:T(8,128)(2,1)S(1)} async-done(((bf16[64,40,640]{2,1,0:T(8,128)(2,1)}), bf16[64,40,640]{2,1,0:T(8,128)(2,1)S(1)}, u32[]{:S(2)}, u32[]{:S(2)}) %all-to-all-start) | async-done | bytes 3276832 | tf_op jit(solution)/shard_map/all_to_all | solution.py:288
  51.0 0.0 copy-start.1
  51.0 0.6 broadcast_in_dim.51.lane_ref
  51.6 1.1 copy-done.1
  52.8 15.0 %fourier.1 = bf16[128,104,128]{2,1,0:T(8,128)(2,1)} custom-call(s32[1]{0:T(128)} %bitcast.south_ref, bf16[64,40,640]{2,1,0:T(8,128)(2,1)} %copy-done.1, bf16[4,2,320,1280]{3,2,1,0:T(8,128)(2,1)} %bitcast.14, bf16[768,640]{1,0:T(8,128)(2,1)} %fusion.15.spread_ref, s32[8,128]{1,0:T(8,128)} %broadcast_in_dim.51.lane_ref), custom_call_target="tpu_custom_call" | custom-call | tf_op jit(solution)/shard_map/fourier/pallas_call | solution.py:125
  67.8 0.0 copy-start.3
  67.8 9.2 %all-to-all-start.1 = ((bf16[128,104,128]{2,1,0:T(8,128)(2,1)}), bf16[128,104,128]{2,1,0:T(8,128)(2,1)S(1)}, u32[]{:S(2)}, u32[]{:S(2)}) async-start(bf16[128,104,128]{2,1,0:T(8,128)(2,1)} %fourier.1), calls=%async_computation.1 | async-start | bytes 6815744 | tf_op jit(solution)/shard_map/all_to_all | solution.py:319
  77.0 0.7 dynamic_slice.3.pairs_ref
  77.7 0.0 copy-done.3
  77.7 0.1 broadcast_in_dim.52
  77.8 0.1 broadcast_in_dim.54
  77.9 0.6 fusion.33.last_ref
  78.5 0.8 fusion.31
  79.3 42.3 %all-to-all-done.1.recv_ref = bf16[128,104,128]{2,1,0:T(8,128)(2,1)S(1)} async-done(((bf16[128,104,128]{2,1,0:T(8,128)(2,1)}), bf16[128,104,128]{2,1,0:T(8,128)(2,1)S(1)}, u32[]{:S(2)}, u32[]{:S(2)}) %all-to-all-start.1) | async-done | bytes 3407904 | tf_op jit(solution)/shard_map/all_to_all | solution.py:319
  121.6 0.0 copy-start
  121.6 0.8 broadcast_in_dim.55.rate_ref
  122.5 0.9 copy-done
  123.4 15.4 %legendre.1 = bf16[4,5,32,1281]{3,2,1,0:T(8,128)(2,1)} custom-call(s32[5]{0:T(128)} %dynamic_slice.3.pairs_ref, bf16[128,104,128]{2,1,0:T(8,128)(2,1)} %copy-done, bf16[5,1281,640]{2,1,0:T(8,128)(2,1)} %bitcast.15, f32[128,256]{1,0:T(8,128)} %broadcast_in_dim.55.rate_ref, bf16[256,256]{1,0:T(8,128)(2,1)} %get-tuple-element.6.mix_ref, ...), custom_call_target="tpu_custom_call" | custom-call | tf_op jit(solution)/shard_map/legendre/pallas_call | solution.py:243
  138.8 26.6 %all_to_all.15 = bf16[4,5,32,1281]{3,2,1,0:T(8,128)(2,1)S(1)} all-to-all(bf16[4,5,32,1281]{3,2,1,0:T(8,128)(2,1)} %legendre.1), channel_id=1, replica_groups=mesh['lev'=4,'lat'=32] {'lev'}, dimensions={0} | all-to-all | bytes 3279360 | tf_op jit(solution)/shard_map/all_to_all | solution.py:352
  165.3 1.4 copy.15
  (23 shorter events, 0.1 us)
Async XLA Ops:
  0.0 10.1 %copy-start.2 = (s32[640]{0:T(1024)S(1)}, s32[640]{0:T(1024)}, u32[]{:S(2)}) copy-start(s32[640]{0:T(1024)} %param.7) | copy-start | bytes 7684
  0.0 51.0 %all-to-all-start = ((bf16[64,40,640]{2,1,0:T(8,128)(2,1)}), bf16[64,40,640]{2,1,0:T(8,128)(2,1)S(1)}, u32[]{:S(2)}, u32[]{:S(2)}) async-start(bf16[64,40,640]{2,1,0:T(8,128)(2,1)} %param.4), calls=%async_computation | async-start | bytes 6553600 | tf_op jit(solution)/shard_map/all_to_all | solution.py:288
  51.0 1.8 %copy-start.1 = (bf16[64,40,640]{2,1,0:T(8,128)(2,1)}, bf16[64,40,640]{2,1,0:T(8,128)(2,1)S(1)}, u32[]{:S(2)}) copy-start(bf16[64,40,640]{2,1,0:T(8,128)(2,1)S(1)} %all-to-all-done.g_ref) | copy-start | bytes 9830404
  67.8 9.9 %copy-start.3 = (f32[64]{0:T(128)S(1)}, f32[64]{0:T(128)}, u32[]{:S(2)}) copy-start(f32[64]{0:T(128)} %param.6) | copy-start | bytes 772
  67.8 53.8 %all-to-all-start.1 = ((bf16[128,104,128]{2,1,0:T(8,128)(2,1)}), bf16[128,104,128]{2,1,0:T(8,128)(2,1)S(1)}, u32[]{:S(2)}, u32[]{:S(2)}) async-start(bf16[128,104,128]{2,1,0:T(8,128)(2,1)} %fourier.1), calls=%async_computation.1 | async-start | bytes 6815744 | tf_op jit(solution)/shard_map/all_to_all | solution.py:319
  121.6 1.7 %copy-start = (bf16[128,104,128]{2,1,0:T(8,128)(2,1)}, bf16[128,104,128]{2,1,0:T(8,128)(2,1)S(1)}, u32[]{:S(2)}) copy-start(bf16[128,104,128]{2,1,0:T(8,128)(2,1)S(1)} %all-to-all-done.1.recv_ref) | copy-start | bytes 10223620

commit v2 on v0

v2 whole, which is shorter than its diff:
```python
import functools
import math

import jax
import jax.numpy as jnp
from jax import lax
from jax.experimental import pallas as pl
from jax.experimental.pallas import tpu as pltpu
from jax.sharding import PartitionSpec as P


F32 = jnp.float32
BF16 = jnp.bfloat16
NT = (((1,), (1,)), ((), ()))
LANES = 128


COS_TERMS = [((-1) ** n) * (2 * math.pi) ** (2 * n) / math.factorial(2 * n) for n in range(10)]


def cos_turns(turns):
    part = turns - jnp.floor(turns + 0.5)
    square = part * part
    total = jnp.full_like(square, COS_TERMS[-1])
    for term in COS_TERMS[-2::-1]:
        total = total * square + term
    return total


def circle_kernel(lon_count, wave_ref, quarter_ref, out_ref):
    rows, cols = out_ref.shape
    wave = wave_ref[...].astype(F32)
    quarter = quarter_ref[...].astype(F32) * 0.25
    lane = lax.broadcasted_iota(jnp.int32, (rows, LANES), 1).astype(F32)

    def at(offset):
        product = wave * (lane + offset)
        product = product - jnp.floor(product * (1.0 / lon_count)) * lon_count
        return cos_turns(product * (1.0 / lon_count) + quarter)

    step = wave * float(LANES)
    step = step - jnp.floor(step * (1.0 / lon_count)) * lon_count
    twice = 2.0 * cos_turns(step * (1.0 / lon_count))
    before, now = at(0.0), at(float(LANES))
    out_ref[:, :LANES] = before.astype(BF16)
    out_ref[:, LANES : 2 * LANES] = now.astype(BF16)
    for tile in range(2, cols // LANES):
        before, now = now, twice * now - before
        out_ref[:, tile * LANES : (tile + 1) * LANES] = now.astype(BF16)


def circle_table(waves, quarters, lon_count, cols):
    rows = waves.shape[0]
    block = 64
    spread = lambda v: jnp.broadcast_to(v[:, None], (rows, LANES))
    return pl.pallas_call(
        functools.partial(circle_kernel, lon_count),
        grid=(rows // block,),
        in_specs=[pl.BlockSpec((block, LANES), lambda i: (i, 0))] * 2,
        out_specs=pl.BlockSpec((block, cols), lambda i: (i, 0)),
        out_shape=jax.ShapeDtypeStruct((rows, cols), BF16),
        cost_estimate=pl.CostEstimate(
            flops=rows * cols * 10, bytes_accessed=rows * cols * 2, transcendentals=0
        ),
        name="circle",
    )(spread(waves), spread(quarters))


def fourier_kernel(
    south_ref, g_ref, circle_ref, lane_ref, out_ref, g_buf, circle_buf, fold_ref, tail_ref, out_buf,
    g_sem, circle_sem, out_sem,
):
    steps, dests = out_buf.shape[:2]
    _, bands, lats, quarter = g_buf.shape
    tiles = bands * lats // LANES
    main = dests * 8
    end = out_ref.shape[1] - tiles * 16
    groups = [(low, min(2, tiles - low)) for low in range(0, tiles, 2)]
    south = south_ref[0]

    def g_copy(j):
        part = pl.ds(2 * j, 2)
        return pltpu.make_async_copy(g_ref.at[:, part], g_buf.at[:, part], g_sem.at[j])

    def circle_copy(i):
        return pltpu.make_async_copy(circle_ref.at[i], circle_buf.at[i], circle_sem.at[i])

    for j in range(bands // 2):
        g_copy(j).start()
    for i in range(steps):
        circle_copy(i).start()
    tail_ref[...] = jnp.zeros_like(tail_ref)

    def fold(j, carry):
        g_copy(j).wait()

        def squared(q):
            value = g_buf[q, pl.ds(2 * j, 2)].astype(F32)
            return (value * jnp.abs(value)).reshape(2 * lats, quarter)

        rows = pl.ds(pl.multiple_of(j * 2 * lats, 16), 2 * lats)
        for half in range(2):
            near, far = squared(half), squared(half + 2)
            cols = slice(half * quarter, (half + 1) * quarter)
            fold_ref[0, rows, cols] = (near + far).astype(BF16)
            fold_ref[1, rows, cols] = (near - far).astype(BF16)
        return carry

    lax.fori_loop(0, bands // 2, fold, 0)
    index = jnp.broadcast_to(lane_ref[0:1, :], (circle_buf.shape[2], LANES))

    def out_copy(i, start, size, sem):
        rows = pl.ds(start, size)
        return pltpu.make_async_copy(
            out_buf.at[i, :, rows], out_ref.at[pl.ds(i * dests, dests), rows], out_sem.at[i, sem]
        )

    def start_of(low, many):
        start = jnp.where(south == 1, tiles - low - many, low) * 16
        return pl.multiple_of(start, 16)

    def step(i, carry):
        circle_copy(i).wait()
        for n, (low, many) in enumerate(groups):
            rows = slice(low * LANES, (low + many) * LANES)
            values = [
                lax.dot_general(
                    circle_buf[i, kind], fold_ref[kind, rows, :], NT, preferred_element_type=F32
                )
                for kind in range(2)
            ]
            for at in range(many):
                place = jnp.where(south == 1, tiles - 1 - (low + at), low + at)
                both = []
                for kind in range(2):
                    value = jnp.take_along_axis(
                        values[kind][:, at * LANES : (at + 1) * LANES],
                        index,
                        axis=1,
                        mode="promise_in_bounds",
                    )
                    both.append(value[:main].reshape(dests, 8, LANES))
                    for r in range(2):
                        spot = pl.ds(place * 4 + kind * 2 + r, dests, stride=end)
                        tail_ref[spot, :] = value[main + r * dests : main + (r + 1) * dests]
                rows16 = pl.ds(pl.multiple_of(place * 16, 16), 16)
                out_buf[i, :, rows16, :] = jnp.concatenate(both, axis=1).astype(BF16)
            out_copy(i, start_of(low, many), many * 16, n).start()
        last = tail_ref[...].reshape(dests, end, LANES)
        out_buf[i, :, tiles * 16 :, :] = last.astype(BF16)
        out_copy(i, tiles * 16, end, len(groups)).start()
        return carry

    lax.fori_loop(0, steps, step, 0)
    for i in range(steps):
        for n, (low, many) in enumerate(groups):
            out_copy(i, start_of(low, many), many * 16, n).wait()
        out_copy(i, tiles * 16, end, len(groups)).wait()


def fourier(south, received, circle, lane_index, dev_count):
    steps = circle.shape[0]
    dests = dev_count // steps
    _, bands, lats, quarter = received.shape
    lat_half = bands * lats
    tiles = lat_half // LANES
    end = -(-tiles * 4 // 8) * 8
    rows = tiles * 16 + end
    anywhere = pl.BlockSpec(memory_space=pl.ANY)
    return pl.pallas_call(
        fourier_kernel,
        in_specs=[
            pl.BlockSpec(memory_space=pltpu.SMEM),
            anywhere,
            pl.BlockSpec(memory_space=pltpu.HBM),
            pl.BlockSpec(memory_space=pltpu.VMEM),
        ],
        out_specs=pl.BlockSpec(memory_space=pltpu.HBM),
        scratch_shapes=[
            pltpu.VMEM(received.shape, BF16),
            pltpu.VMEM(circle.shape, BF16),
            pltpu.VMEM((2, lat_half, 2 * quarter), BF16),
            pltpu.VMEM((dests * end, LANES), F32),
            pltpu.VMEM((steps, dests, rows, LANES), BF16),
            pltpu.SemaphoreType.DMA((bands // 2,)),
            pltpu.SemaphoreType.DMA((steps,)),
            pltpu.SemaphoreType.DMA((steps, -(-tiles // 2) + 1)),
        ],
        out_shape=jax.ShapeDtypeStruct((dev_count, rows, LANES), BF16),
        compiler_params=pltpu.CompilerParams(vmem_limit_bytes=FOURIER_VMEM),
        cost_estimate=pl.CostEstimate(
            flops=2 * circle.size * lat_half,
            bytes_accessed=2 * (received.size + circle.size + dev_count * rows * LANES),
            transcendentals=0,
        ),
        name="fourier",
    )(south, received, circle, lane_index)


FOURIER_VMEM = 59 * 1024 * 1024
LEGENDRE_VMEM = 113 * 512 * 1024


def legendre_kernel(
    scale, norm, first, count, me_ref, pairs_ref, recv_ref, basis_ref, rate_ref, *refs
):
    levs = recv_ref.shape[1]
    out_refs = refs[:levs]
    recv_buf, basis_buf, x_ref, main_ref, tail_ref, out_buf, recv_sem, basis_sem, out_sem = refs[levs:]
    group = recv_ref.shape[0] // 2
    cols, lats = basis_ref.shape[1:]
    waves = cols - 1
    tiles = lats // LANES
    end = recv_ref.shape[2] - tiles * 16
    rows = x_ref.shape[3]
    part = rows // levs
    me = me_ref[0]

    def recv_copy(x):
        return pltpu.make_async_copy(recv_ref.at[:, x], recv_buf.at[x], recv_sem.at[x])

    def basis_copy(k):
        return pltpu.make_async_copy(basis_ref.at[first + k], basis_buf.at[k], basis_sem.at[k])

    for x in range(levs):
        recv_copy(x).start()
    for k in range(count):
        basis_copy(k).start()

    mains = [k for k in range(first, first + count) if k < 4]

    def gather(x, carry):
        recv_copy(x).wait()
        base = lax.rem(x - me + levs, levs) * part

        def sides(span, height, into):
            n = recv_buf[x, :group, span, :].astype(F32).reshape(group * height, LANES)
            s = recv_buf[x, group:, span, :].astype(F32).reshape(group * height, LANES)
            into[0] = n + s
            into[1] = n - s

        def put(slot, kind, tile, r, from_ref, start, stride):
            lanes = slice(tile * LANES, (tile + 1) * LANES)
            dest = pl.ds(pl.multiple_of(base + r * group, 16), group)
            for par in range(2):
                value = from_ref[par, pl.ds(start, group, stride=stride), :]
                x_ref[slot - first, par, kind, dest, lanes] = value.astype(BF16)

        for tile in range(tiles):
            sides(slice(tile * 16, tile * 16 + 16), 16, main_ref.at[tile])
            for kind in range(2):
                for k in mains:
                    for r in range(2):
                        put(k, kind, tile, r, main_ref.at[tile], kind * 8 + k * 2 + r, 16)
        if first + count > 4:
            sides(slice(tiles * 16, tiles * 16 + end), end, tail_ref)
            for tile in range(tiles):
                for kind in range(2):
                    for r in range(2):
                        put(4, kind, tile, r, tail_ref, tile * 4 + kind * 2 + r, end)
        return carry

    lax.fori_loop(0, levs, gather, 0)

    width = 256
    rate = jnp.broadcast_to(rate_ref[...], (rows, LANES))
    rates = jnp.concatenate([rate] * (width // LANES), axis=1)

    def out_copy(k, s):
        return pltpu.make_async_copy(out_buf.at[s, k], out_refs[s].at[k], out_sem.at[k, s])

    def slot_step(k, carry):
        basis_copy(k).wait()
        pair = pairs_ref[k + first]
        bound = waves - pair
        first_kind = lax.rem(pair, 2)

        def damping(column, second):
            degree = jnp.where(second, column - 1, pair + column)
            scaled = (degree * (degree + 1)).astype(F32) / norm
            return scale / (1.0 + rates[:, : column.shape[1]] * (scaled * scaled))

        def emit(start, value):
            value = value.astype(BF16)
            for s in range(levs):
                out_buf[s, k, :, start : start + value.shape[1]] = value[s * part : (s + 1) * part]

        def block(start):
            column = start + lax.broadcasted_iota(jnp.int32, (1, width), 1)
            second = column >= bound
            even = lax.rem(jnp.where(second, column + pair, column), 2) == 0
            factor = damping(column, second)
            basis = basis_buf[k, start : start + width, :]

            def product(kind):
                left = x_ref[k, :, kind].reshape(2 * rows, lats)
                both = lax.dot_general(left, basis, NT, preferred_element_type=F32)
                return jnp.where(even, both[:rows], both[rows:]) * factor

            value = product(jnp.where(start >= bound, 1 - first_kind, first_kind))
            emit(start, value)

            @pl.when((start < bound) & (bound < start + width))
            def _():
                emit(start, jnp.where(second, product(1 - first_kind), value))

        for start in range(0, waves, width):
            block(start)
        column = jnp.full((1, 1), waves, jnp.int32)
        left = x_ref[k, first_kind, 1 - first_kind].astype(F32)
        final = jnp.sum(left * basis_buf[k, waves:, :].astype(F32), axis=1, keepdims=True)
        emit(waves, final * damping(column, column >= bound))
        for s in range(levs):
            out_copy(k, s).start()
        return carry

    lax.fori_loop(0, count, slot_step, 0)
    for k in range(count):
        for s in range(levs):
            out_copy(k, s).wait()


def legendre(first, count, me, pairs, received, basis, rates, lon_count, norm):
    _, cols, lats = basis.shape
    lat_count, levs, rows, _ = received.shape
    group = lat_count // 2
    part = 2 * group
    tiles = lats // LANES
    end = rows - tiles * 16
    anywhere = pl.BlockSpec(memory_space=pl.ANY)
    scalars = pl.BlockSpec(memory_space=pltpu.SMEM)
    return pl.pallas_call(
        functools.partial(legendre_kernel, 1.0 / lon_count, norm, first, count),
        in_specs=[
            scalars,
            scalars,
            anywhere,
            pl.BlockSpec(memory_space=pltpu.HBM),
            pl.BlockSpec(memory_space=pltpu.VMEM),
        ],
        out_specs=[anywhere] * levs,
        scratch_shapes=[
            pltpu.VMEM((levs, lat_count, rows, LANES), BF16),
            pltpu.VMEM((count, cols, lats), BF16),
            pltpu.VMEM((count, 2, 2, levs * part, lats), BF16),
            pltpu.VMEM((tiles, 2, group * 16, LANES), F32),
            pltpu.VMEM((2, group * end, LANES), F32),
            pltpu.VMEM((levs, count, part, cols), BF16),
            pltpu.SemaphoreType.DMA((levs,)),
            pltpu.SemaphoreType.DMA((count,)),
            pltpu.SemaphoreType.DMA((count, levs)),
        ],
        out_shape=[jax.ShapeDtypeStruct((count, part, cols), BF16)] * levs,
        compiler_params=pltpu.CompilerParams(vmem_limit_bytes=LEGENDRE_VMEM),
        cost_estimate=pl.CostEstimate(
            flops=2 * count * cols * lats * 256,
            bytes_accessed=2 * count * cols * (lats + 128),
            transcendentals=0,
        ),
        name="legendre",
    )(me, pairs, received, basis, rates)


def assemble_kernel(counts, me_ref, *refs):
    levs = refs[-2].shape[1]
    out_ref, sem = refs[-2:]
    copies, low = [], 0
    for c, count in enumerate(counts):
        for s in range(levs):
            lev = lax.rem(me_ref[0] - s + levs, levs)
            n = c * levs + s
            dest = out_ref.at[low : low + count, lev]
            copies.append(pltpu.make_async_copy(refs[n], dest, sem.at[n]))
        low += count
    for copy in copies:
        copy.start()
    for copy in copies:
        copy.wait()


def assemble(me, parts):
    levs = len(parts[0])
    _, part, cols = parts[0][0].shape
    counts = [p[0].shape[0] for p in parts]
    flat = [a for p in parts for a in p]
    anywhere = pl.BlockSpec(memory_space=pl.ANY)
    return pl.pallas_call(
        functools.partial(assemble_kernel, counts),
        in_specs=[pl.BlockSpec(memory_space=pltpu.SMEM)] + [anywhere] * len(flat),
        out_specs=anywhere,
        scratch_shapes=[pltpu.SemaphoreType.DMA((len(flat),))],
        out_shape=jax.ShapeDtypeStruct((sum(counts), levs, part, cols), BF16),
        compiler_params=pltpu.CompilerParams(vmem_limit_bytes=1024 * 1024),
        name="assemble",
    )(me, *flat)


def transform(grid_values, basis_table, damping_rates, pair_table):
    levs, lat_count = lax.axis_size("lev"), lax.axis_size("lat")
    dev_count = levs * lat_count
    half_bands = lat_count // 2
    lon_count = grid_values.shape[2] * levs
    slots, cols = basis_table.shape[1], basis_table.shape[2]
    top = cols - 2
    group = half_bands
    me_lev, me_lat = lax.axis_index("lev"), lax.axis_index("lat")
    south = (me_lat >= half_bands).astype(jnp.int32)

    halves = [
        [x * lat_count + h * half_bands + b for x in range(levs) for b in range(half_bands)]
        for h in range(2)
    ]
    everyone = [[x * lat_count + b for b in range(lat_count) for x in range(levs)]]
    circles = lax.all_to_all(
        grid_values, ("lev", "lat"), 0, 0, axis_index_groups=halves, tiled=True
    ).reshape((levs, half_bands) + grid_values.shape[1:])

    steps = 2
    table = jnp.transpose(pair_table.reshape(levs, lat_count, slots), (1, 0, 2))
    table = table.reshape(steps, dev_count // steps, slots)
    other = top - table
    odd = table % 2 == 1
    kinds = []
    for wave in (jnp.where(odd, other, table), jnp.where(odd, table, other)):
        head = jnp.repeat(wave[:, :, : slots - 1], 2, axis=2).reshape(steps, -1)
        kinds.append(jnp.concatenate([head, wave[:, :, slots - 1], wave[:, :, slots - 1]], axis=1))
    waves = jnp.stack(kinds, axis=1)
    row = jnp.arange(waves.shape[2], dtype=jnp.int32)
    main = dev_count // steps * 2 * (slots - 1)
    quarters = jnp.where(row < main, row % 2, (row >= main + dev_count // steps).astype(jnp.int32))
    quarters = jnp.broadcast_to(quarters, waves.shape)
    circle = circle_table(
        waves.reshape(-1), quarters.reshape(-1), lon_count, lon_count // 2
    ).reshape(waves.shape + (lon_count // 2,))

    lane = jnp.arange(LANES, dtype=jnp.int32)
    lane_index = jnp.broadcast_to(jnp.where(south == 1, LANES - 1 - lane, lane), (8, LANES))
    packed = fourier(south[None], circles, circle, lane_index, dev_count)
    me = me_lev[None].astype(jnp.int32)
    pairs = lax.dynamic_slice_in_dim(pair_table, (me_lev * lat_count + me_lat) * slots, slots)
    rates = jnp.roll(damping_rates.reshape(levs, 1, group), -me_lev, axis=0)
    rates = jnp.broadcast_to(rates, (levs, 2, group)).reshape(-1, 1)
    packed, pairs, rates, me = lax.optimization_barrier((packed, pairs, rates, me))
    received = lax.all_to_all(
        packed, ("lev", "lat"), 0, 0, axis_index_groups=everyone, tiled=True
    ).reshape((lat_count, levs) + packed.shape[1:])

    basis = jnp.transpose(basis_table, (1, 2, 0))
    parts = []
    for first, count in CHUNKS:
        outs = legendre(
            first, count, me, pairs, received, basis, rates, lon_count, float(top * (top + 1))
        )
        moved = [outs[0]]
        for s in range(1, levs):
            to = [(i, (i + s) % levs) for i in range(levs)]
            moved.append(lax.ppermute(outs[s], "lev", to))
        parts.append(moved)
    return assemble(me, parts).reshape(slots, levs, 2, group, cols)


CHUNKS = ((0, 2), (2, 3))


def solution(mesh):
    placed = (P(None, "lat", "lev"), P(None, ("lev", "lat"), None), P(), P())
    return jax.shard_map(
        transform,
        mesh=mesh,
        in_specs=placed,
        out_specs=P("lat", None, None, "lev", None),
        check_vma=False,
    )
```

time: 572 us -> 168 us (0.29); the launches traced: 561 us -> 165 us
  other arithmetic: 224 us -> 2.06 us
  local copies, waits for them, and re-layouts: 238 us -> 17.8 us
  Pallas kernels: 0 us -> 53.1 us
  waiting for transfers between devices: 28.3 us -> 62.8 us
  matrix products: 28.1 us -> 0 us
  blocking collectives: 25.4 us -> 0 us
  starting transfers between devices: 16.2 us -> 28.8 us
    convert_element_type x3 -> x0, other arithmetic: 87.1 us -> none  [the longest x2 83.2 us: per_device(): fourier = (spectra * (1.0 / lon_count)).astype(jnp.bfloat16)]
    another operation x3, local copies, waits for them, and re-layouts: 72.1 us -> 1.11 us  [the longest x2 1.1 us: transform(): head = jnp.repeat(wave[:, :, :slots - 1], 2, axis=2).reshape(steps, -1)]
    all_to_all x1 -> x0, other arithmetic: 69.6 us -> none  [per_device(): lax.all_to_all(payload, ('lev', 'lat'), split_axis=0, concat_axis=0, tile...]
    another operation x2, other arithmetic: 61.5 us -> 0.76 us  [transform(): waves = jnp.stack(kinds, axis=1)]
    convert_element_type x5 -> x0, local copies, waits for them, and re-layouts: 53.8 us -> none  [the longest x1 27.1 us: circle_rows(): jnp.stack([jnp.cos(angle), -jnp.sin(angle)], axis=-2).astype(jnp.bfloat16)]
    pallas_call x0 -> x5, Pallas kernels: none -> 53.1 us  [the longest x1 21.9 us: circle_table(): pl.pallas_call(functools.partial(circle_kernel, lon_count), grid=(rows //...]
    dot_general x3 -> x0, matrix products: 28.1 us -> none  [the longest x1 10.8 us: per_device(): lax.dot_general(circle, squared, (((1,), (2,)), ((), ())), preferred_elem...]
    all_to_all x1 -> x0, blocking collectives: 25.4 us -> none  [per_device(): lax.all_to_all(outgoing, 'lev', split_axis=1, concat_axis=1, tiled=True)]
  transfers between devices with their start and end apart: 2 -> 8, of which waited for: 1 -> 4; matrix products, arithmetic and copies ran while one was open for 33% -> 9% of each run, Pallas kernels for 0% -> 20%
where the time goes in v2:
time: 168 us; the launch traced here: 165 us
  waiting for transfers between devices  62.8 us (37%)
  Pallas kernels  53.1 us (32%)
  starting transfers between devices  28.8 us (17%)
  local copies, waits for them, and re-layouts  17.8 us (11%)
  other arithmetic  2.06 us (1%)
    all_to_all x1, waiting for transfers between devices, transform(): lax.all_to_all(packed, ('lev', 'lat'), 0, 0, axis_index_groups=everyone,...  43.3 us
    pallas_call x1, Pallas kernels, circle_table(): pl.pallas_call(functools.partial(circle_kernel, lon_count), grid=(rows //...  21.9 us
    pallas_call x2, Pallas kernels, legendre(): pl.pallas_call(functools.partial(legendre_kernel, 1.0 / lon_count, norm,...  19.4 us
    ppermute x6, waiting for transfers between devices, transform(): moved.append(lax.ppermute(outs[s], 'lev', to))  15.3 us
    pallas_call x1, Pallas kernels, fourier(): pl.pallas_call(fourier_kernel, in_specs=[pl.BlockSpec(memory_space=pltpu....  10.6 us
    all_to_all x1, starting transfers between devices, transform(): lax.all_to_all(grid_values, ('lev', 'lat'), 0, 0, axis_index_groups=halve...  10 us
    ppermute x6, starting transfers between devices, transform(): moved.append(lax.ppermute(outs[s], 'lev', to))  9.54 us
    all_to_all x1, starting transfers between devices, transform(): lax.all_to_all(packed, ('lev', 'lat'), 0, 0, axis_index_groups=everyone,...  9.19 us
  transfers between devices with their start and end apart: 8, of which 4 were waited for; matrix products, arithmetic and copies ran while one was open for 9% of the time, Pallas kernels for 20%

profile of v2, /device:TPU:0, one launch (start us, length us, event | category | flops | bytes accessed | tf_op | source)
XLA Modules:
  0.0 164.8 jit_solution(7478733232648751686)
XLA Ops:
  0.0 10.0 %all-to-all-start = ((bf16[64,40,640]{2,1,0:T(8,128)(2,1)}), bf16[64,40,640]{2,1,0:T(8,128)(2,1)S(1)}, u32[]{:S(2)}, u32[]{:S(2)}) async-start(bf16[64,40,640]{2,1,0:T(8,128)(2,1)} %param.4), calls=%async_computation | async-start | bytes 6553600 | tf_op jit(solution)/shard_map/all_to_all | solution.py:414
  10.1 0.0 copy-done.5
  10.1 0.2 reshape.27
  10.3 0.3 copy.9
  10.6 0.1 reshape.28
  10.7 0.6 subtract_select_fusion.1
  11.3 0.7 copy.10
  12.1 1.0 broadcast_in_dim.40
  13.1 0.8 reshape_reshape.6
  14.0 0.7 subtract_select_fusion
  14.7 0.6 copy-done.4
  15.2 0.7 copy.11
  16.0 1.0 broadcast_in_dim.41
  17.0 0.3 reshape_reshape.7
  17.3 0.7 slice_bitcast_fusion
  18.0 0.8 add_bitcast_fusion
  18.8 1.3 dynamic_slice.7.pairs_ref
  20.1 0.7 reshape.30
  20.8 0.1 reshape.31
  20.9 2.0 %broadcast_in_dim.43.wave_ref = s32[2560,128]{1,0:T(8,128)} broadcast(s32[2560]{0:T(1024)S(1)} %broadcast_in_dim.42), dimensions={0} | broadcast | bytes 1320960 | tf_op jit(solution)/shard_map/broadcast_in_dim | solution.py:55
  22.9 2.0 %broadcast_in_dim.46.quarter_ref = s32[2560,128]{1,0:T(8,128)} broadcast(s32[2560]{0:T(1024)S(1)} %broadcast_in_dim.45), dimensions={0} | broadcast | bytes 1320960 | tf_op jit(solution)/shard_map/broadcast_in_dim | solution.py:55
  24.9 21.9 %circle.1 = bf16[2560,1280]{1,0:T(8,128)(2,1)} custom-call(s32[2560,128]{1,0:T(8,128)} %broadcast_in_dim.43.wave_ref, s32[2560,128]{1,0:T(8,128)} %broadcast_in_dim.46.quarter_ref), custom_call_target="tpu_custom_call" | custom-call | flops 32768000 | bytes 6553600 | tf_op jit(solution)/shard_map/circle/pallas_call | solution.py:56
  46.8 4.2 %all-to-all-done = bf16[64,40,640]{2,1,0:T(8,128)(2,1)S(1)} async-done(((bf16[64,40,640]{2,1,0:T(8,128)(2,1)}), bf16[64,40,640]{2,1,0:T(8,128)(2,1)S(1)}, u32[]{:S(2)}, u32[]{:S(2)}) %all-to-all-start) | async-done | bytes 3276832 | tf_op jit(solution)/shard_map/all_to_all | solution.py:414
  51.0 0.6 broadcast_in_dim.47.lane_ref
  51.6 1.2 copy-done.3
  52.8 10.6 %fourier.1 = bf16[128,104,128]{2,1,0:T(8,128)(2,1)} custom-call(s32[1]{0:T(128)} %bitcast.south_ref, bf16[4,16,40,640]{3,2,1,0:T(8,128)(2,1)} %bitcast.25, bf16[2,2,640,1280]{3,2,1,0:T(8,128)(2,1)} %bitcast.24, s32[8,128]{1,0:T(8,128)} %broadcast_in_dim.47.lane_ref), custom_call_target="tpu_custom_call" | custom-call | flops 4194304000 | bytes 13238272 | tf_op jit(solution)/shard_map/fourier/pallas_call | solution.py:170
  63.4 9.2 %all-to-all-start.1 = ((bf16[128,104,128]{2,1,0:T(8,128)(2,1)}), bf16[128,104,128]{2,1,0:T(8,128)(2,1)S(1)}, u32[]{:S(2)}, u32[]{:S(2)}) async-start(bf16[128,104,128]{2,1,0:T(8,128)(2,1)} %fourier.1), calls=%async_computation.1 | async-start | bytes 6815744 | tf_op jit(solution)/shard_map/all_to_all | solution.py:444
  72.6 0.7 copy.13.rate_ref
  73.3 43.3 %all-to-all-done.1 = bf16[128,104,128]{2,1,0:T(8,128)(2,1)S(1)} async-done(((bf16[128,104,128]{2,1,0:T(8,128)(2,1)}), bf16[128,104,128]{2,1,0:T(8,128)(2,1)S(1)}, u32[]{:S(2)}, u32[]{:S(2)}) %all-to-all-start.1) | async-done | bytes 3407904 | tf_op jit(solution)/shard_map/all_to_all | solution.py:444
  116.7 1.7 %copy-done.2 = bf16[128,104,128]{2,1,0:T(8,128)(2,1)} copy-done((bf16[128,104,128]{2,1,0:T(8,128)(2,1)}, bf16[128,104,128]{2,1,0:T(8,128)(2,1)S(1)}, u32[]{:S(2)}) %copy-start.2) | copy-done | bytes 3407896
  118.4 8.4 %legendre.2 = (bf16[2,32,1281]{2,1,0:T(8,128)(2,1)}, bf16[2,32,1281]{2,1,0:T(8,128)(2,1)}, bf16[2,32,1281]{2,1,0:T(8,128)(2,1)}, bf16[2,32,1281]{2,1,0:T(8,128)(2,1)}) custom-call(s32[1]{0:T(128)} %bitcast.9.me_ref, s32[5]{0:T(128)} %dynamic_slice.7.pairs_ref, bf16[32,4,104,128]{3,2,1,0:T(8,128)(2,1)} %bitcast.22, bf16[5,1281,640]{2,1,0:T(8,128)(2,1)} %bitcast.20, ...), custom_call_target="tpu_custom_call" | custom-call | flops 839516160 | bytes 3935232 | tf_op jit(solution)/shard_map/legendre/pallas_call | solution.py:332
  126.8 0.6 collective-permute-start
  127.5 10.9 %legendre.3 = (bf16[3,32,1281]{2,1,0:T(8,128)(2,1)}, bf16[3,32,1281]{2,1,0:T(8,128)(2,1)}, bf16[3,32,1281]{2,1,0:T(8,128)(2,1)}, bf16[3,32,1281]{2,1,0:T(8,128)(2,1)}) custom-call(s32[1]{0:T(128)} %bitcast.9.me_ref, s32[5]{0:T(128)} %dynamic_slice.7.pairs_ref, bf16[32,4,104,128]{3,2,1,0:T(8,128)(2,1)} %bitcast.23, bf16[5,1281,640]{2,1,0:T(8,128)(2,1)} %bitcast.21, ...), custom_call_target="tpu_custom_call" | custom-call | flops 1259274240 | bytes 5902848 | tf_op jit(solution)/shard_map/legendre/pallas_call | solution.py:332
  138.4 0.9 collective-permute-start.3
  139.3 3.3 %collective-permute-start.4 = (bf16[3,32,1281]{2,1,0:T(8,128)(2,1)}, bf16[3,32,1281]{2,1,0:T(8,128)(2,1)S(1)}, u32[]{:S(2)}, u32[]{:S(2)}) collective-permute-start(bf16[3,32,1281]{2,1,0:T(8,128)(2,1)} %get-tuple-element.27), channel_id=1, source_target_pairs={{0,64},{32,96},{64,0},{96,32},{1,65},{33,97},{65,1},{97,33},{2,66}... | collective-permute-start | bytes 737864 | tf_op jit(solution)/shard_map/ppermute | solution.py:457
  142.6 1.1 collective-permute-start.5
  143.7 0.0 copy-done.7
  143.7 0.9 collective-permute-start.1
  144.7 0.0 collective-permute-done.refs_1_
  144.7 2.7 %collective-permute-start.2 = (bf16[2,32,1281]{2,1,0:T(8,128)(2,1)S(1)}, bf16[2,32,1281]{2,1,0:T(8,128)(2,1)S(1)}, u32[]{:S(2)}, u32[]{:S(2)}) collective-permute-start(bf16[2,32,1281]{2,1,0:T(8,128)(2,1)S(1)} %copy-done.6), channel_id=1, source_target_pairs={{0,96},{32,0},{64,32},{96,64},{1,97},{33,1},{65,33},{97,65},{2,98}... | collective-permute-start | bytes 491912 | tf_op jit(solution)/shard_map/ppermute | solution.py:457
  147.3 11.6 %collective-permute-done.1.refs_2_ = bf16[2,32,1281]{2,1,0:T(8,128)(2,1)S(1)} collective-permute-done((bf16[2,32,1281]{2,1,0:T(8,128)(2,1)S(1)}, bf16[2,32,1281]{2,1,0:T(8,128)(2,1)S(1)}, u32[]{:S(2)}, u32[]{:S(2)}) %collective-permute-start.1) | collective-permute-done | bytes 164000 | tf_op jit(solution)/shard_map/ppermute | solution.py:457
  158.9 3.6 %collective-permute-done.2.refs_3_ = bf16[2,32,1281]{2,1,0:T(8,128)(2,1)S(1)} collective-permute-done((bf16[2,32,1281]{2,1,0:T(8,128)(2,1)S(1)}, bf16[2,32,1281]{2,1,0:T(8,128)(2,1)S(1)}, u32[]{:S(2)}, u32[]{:S(2)}) %collective-permute-start.2) | collective-permute-done | bytes 164000 | tf_op jit(solution)/shard_map/ppermute | solution.py:457
  162.6 0.0 collective-permute-done.3.refs_5_
  162.6 0.0 collective-permute-done.4.refs_6_
  162.6 0.0 collective-permute-done.5.refs_7_
  162.6 0.0 copy-start
  162.6 0.9 copy-done
  163.6 1.3 assemble.1
  (22 shorter events, 0.1 us)
Async XLA Ops:
  0.0 10.1 %copy-start.5 = (s32[640]{0:T(1024)S(1)}, s32[640]{0:T(1024)}, u32[]{:S(2)}) copy-start(s32[640]{0:T(1024)} %param.7) | copy-start | bytes 7684
  0.0 51.0 %all-to-all-start = ((bf16[64,40,640]{2,1,0:T(8,128)(2,1)}), bf16[64,40,640]{2,1,0:T(8,128)(2,1)S(1)}, u32[]{:S(2)}, u32[]{:S(2)}) async-start(bf16[64,40,640]{2,1,0:T(8,128)(2,1)} %param.4), calls=%async_computation | async-start | bytes 6553600 | tf_op jit(solution)/shard_map/all_to_all | solution.py:414
  14.7 0.6 copy-start.4
  51.0 1.8 %copy-start.3 = (bf16[64,40,640]{2,1,0:T(8,128)(2,1)}, bf16[64,40,640]{2,1,0:T(8,128)(2,1)S(1)}, u32[]{:S(2)}) copy-start(bf16[64,40,640]{2,1,0:T(8,128)(2,1)S(1)} %all-to-all-done) | copy-start | bytes 9830404
  63.4 53.3 %all-to-all-start.1 = ((bf16[128,104,128]{2,1,0:T(8,128)(2,1)}), bf16[128,104,128]{2,1,0:T(8,128)(2,1)S(1)}, u32[]{:S(2)}, u32[]{:S(2)}) async-start(bf16[128,104,128]{2,1,0:T(8,128)(2,1)} %fourier.1), calls=%async_computation.1 | async-start | bytes 6815744 | tf_op jit(solution)/shard_map/all_to_all | solution.py:444
  116.7 1.7 %copy-start.2 = (bf16[128,104,128]{2,1,0:T(8,128)(2,1)}, bf16[128,104,128]{2,1,0:T(8,128)(2,1)S(1)}, u32[]{:S(2)}) copy-start(bf16[128,104,128]{2,1,0:T(8,128)(2,1)S(1)} %all-to-all-done.1) | copy-start | bytes 10223620
  126.8 16.9 %copy-start.7 = (bf16[2,32,1281]{2,1,0:T(8,128)(2,1)S(1)}, bf16[2,32,1281]{2,1,0:T(8,128)(2,1)}, u32[]{:S(2)}) copy-start(bf16[2,32,1281]{2,1,0:T(8,128)(2,1)} %get-tuple-element.23) | copy-start | bytes 491908
  126.8 17.9 %copy-start.6 = (bf16[2,32,1281]{2,1,0:T(8,128)(2,1)S(1)}, bf16[2,32,1281]{2,1,0:T(8,128)(2,1)}, u32[]{:S(2)}) copy-start(bf16[2,32,1281]{2,1,0:T(8,128)(2,1)} %get-tuple-element.24) | copy-start | bytes 491908
  126.8 35.8 %copy-start.1 = (bf16[2,32,1281]{2,1,0:T(8,128)(2,1)S(1)}, bf16[2,32,1281]{2,1,0:T(8,128)(2,1)}, u32[]{:S(2)}) copy-start(bf16[2,32,1281]{2,1,0:T(8,128)(2,1)} %get-tuple-element.21.refs_0_) | copy-start | bytes 491908
  126.8 17.8 %collective-permute-start = (bf16[2,32,1281]{2,1,0:T(8,128)(2,1)}, bf16[2,32,1281]{2,1,0:T(8,128)(2,1)S(1)}, u32[]{:S(2)}, u32[]{:S(2)}) collective-permute-start(bf16[2,32,1281]{2,1,0:T(8,128)(2,1)} %get-tuple-element.22), channel_id=1, source_target_pairs={{0,32},{32,64},{64,96},{96,0},{1,33},{33,65},{65,97},{97,1},{2,34}... | collective-permute-start | bytes 491912 | tf_op jit(solution)/shard_map/ppermute | solution.py:457
  138.4 24.2 %collective-permute-start.3 = (bf16[3,32,1281]{2,1,0:T(8,128)(2,1)}, bf16[3,32,1281]{2,1,0:T(8,128)(2,1)S(1)}, u32[]{:S(2)}, u32[]{:S(2)}) collective-permute-start(bf16[3,32,1281]{2,1,0:T(8,128)(2,1)} %get-tuple-element.26), channel_id=1, source_target_pairs={{0,32},{32,64},{64,96},{96,0},{1,33},{33,65},{65,97},{97,1},{2,34}... | collective-permute-start | bytes 737864 | tf_op jit(solution)/shard_map/ppermute | solution.py:457
  139.3 23.3 %collective-permute-start.4 = (bf16[3,32,1281]{2,1,0:T(8,128)(2,1)}, bf16[3,32,1281]{2,1,0:T(8,128)(2,1)S(1)}, u32[]{:S(2)}, u32[]{:S(2)}) collective-permute-start(bf16[3,32,1281]{2,1,0:T(8,128)(2,1)} %get-tuple-element.27), channel_id=1, source_target_pairs={{0,64},{32,96},{64,0},{96,32},{1,65},{33,97},{65,1},{97,33},{2,66}... | collective-permute-start | bytes 737864 | tf_op jit(solution)/shard_map/ppermute | solution.py:457
  142.6 20.0 %collective-permute-start.5 = (bf16[3,32,1281]{2,1,0:T(8,128)(2,1)}, bf16[3,32,1281]{2,1,0:T(8,128)(2,1)S(1)}, u32[]{:S(2)}, u32[]{:S(2)}) collective-permute-start(bf16[3,32,1281]{2,1,0:T(8,128)(2,1)} %get-tuple-element.28), channel_id=1, source_target_pairs={{0,96},{32,0},{64,32},{96,64},{1,97},{33,1},{65,33},{97,65},{2,98}... | collective-permute-start | bytes 737864 | tf_op jit(solution)/shard_map/ppermute | solution.py:457
  143.7 15.2 %collective-permute-start.1 = (bf16[2,32,1281]{2,1,0:T(8,128)(2,1)S(1)}, bf16[2,32,1281]{2,1,0:T(8,128)(2,1)S(1)}, u32[]{:S(2)}, u32[]{:S(2)}) collective-permute-start(bf16[2,32,1281]{2,1,0:T(8,128)(2,1)S(1)} %copy-done.7), channel_id=1, source_target_pairs={{0,64},{32,96},{64,0},{96,32},{1,65},{33,97},{65,1},{97,33},{2,66}... | collective-permute-start | bytes 491912 | tf_op jit(solution)/shard_map/ppermute | solution.py:457
  144.7 17.9 %collective-permute-start.2 = (bf16[2,32,1281]{2,1,0:T(8,128)(2,1)S(1)}, bf16[2,32,1281]{2,1,0:T(8,128)(2,1)S(1)}, u32[]{:S(2)}, u32[]{:S(2)}) collective-permute-start(bf16[2,32,1281]{2,1,0:T(8,128)(2,1)S(1)} %copy-done.6), channel_id=1, source_target_pairs={{0,96},{32,0},{64,32},{96,64},{1,97},{33,1},{65,33},{97,65},{2,98}... | collective-permute-start | bytes 491912 | tf_op jit(solution)/shard_map/ppermute | solution.py:457
  162.6 1.0 copy-start

commit v3 on v2

v3 whole, which is shorter than its diff:
```python
import functools
import math

import jax
import jax.numpy as jnp
from jax import lax
from jax.experimental import pallas as pl
from jax.experimental.pallas import tpu as pltpu
from jax.sharding import PartitionSpec as P


F32 = jnp.float32
BF16 = jnp.bfloat16
NT = (((1,), (1,)), ((), ()))
LANES = 128


COS_TERMS = [((-1) ** n) * (2 * math.pi) ** (2 * n) / math.factorial(2 * n) for n in range(10)]


def cos_turns(turns):
    part = turns - jnp.floor(turns + 0.5)
    square = part * part
    total = jnp.full_like(square, COS_TERMS[-1])
    for term in COS_TERMS[-2::-1]:
        total = total * square + term
    return total


def circle_kernel(lon_count, wave_ref, quarter_ref, out_ref):
    rows, cols = out_ref.shape
    size = 64
    lane = lax.broadcasted_iota(jnp.int32, (size, LANES), 1).astype(F32)

    def block(i, carry):
        span = pl.ds(pl.multiple_of(i * size, size), size)
        wave = wave_ref[span, :].astype(F32)
        quarter = quarter_ref[span, :].astype(F32) * 0.25

        def turns(product):
            product = product - jnp.floor(product * (1.0 / lon_count)) * lon_count
            return product * (1.0 / lon_count)

        twice = 2.0 * cos_turns(turns(wave * float(LANES)))
        before = cos_turns(turns(wave * lane) + quarter)
        now = cos_turns(turns(wave * (lane + float(LANES))) + quarter)
        out_ref[span, :LANES] = before.astype(BF16)
        out_ref[span, LANES : 2 * LANES] = now.astype(BF16)
        for tile in range(2, cols // LANES):
            before, now = now, twice * now - before
            out_ref[span, tile * LANES : (tile + 1) * LANES] = now.astype(BF16)
        return carry

    lax.fori_loop(0, rows // size, block, 0)


def circle_table(waves, quarters, lon_count, cols):
    rows = waves.shape[0]
    return pl.pallas_call(
        functools.partial(circle_kernel, lon_count),
        in_specs=[VMEM_SPEC] * 2,
        out_specs=VMEM_SPEC,
        out_shape=jax.ShapeDtypeStruct((rows, cols), BF16),
        compiler_params=pltpu.CompilerParams(vmem_limit_bytes=CIRCLE_VMEM),
        cost_estimate=pl.CostEstimate(
            flops=rows * cols * 10, bytes_accessed=rows * cols * 2, transcendentals=0
        ),
        name="circle",
    )(waves, quarters)


VMEM_SPEC = pl.BlockSpec(memory_space=pltpu.VMEM)
HBM_SPEC = pl.BlockSpec(memory_space=pltpu.HBM)


def in_hbm(x):
    return pltpu.with_memory_space_constraint(x, pltpu.HBM)


CIRCLE_VMEM = 12 * 1024 * 1024


def fourier_kernel(
    south_ref, g_ref, table_ref, lane_ref, out_ref, circle_ref, fold_ref, tail_ref, sem
):
    _, bands, lats, quarter = g_ref.shape
    steps = circle_ref.shape[0]
    tiles = bands * lats // LANES
    end = out_ref.shape[1] - tiles * 16
    dests = out_ref.shape[0] // steps
    main = dests * 8
    south = south_ref[0]

    def table_copy(i):
        return pltpu.make_async_copy(table_ref.at[i], circle_ref.at[i], sem.at[i])

    for i in range(steps):
        table_copy(i).start()
    tail_ref[...] = jnp.zeros_like(tail_ref)

    def fold(j, carry):
        def squared(q):
            value = g_ref[q, pl.ds(2 * j, 2)].astype(F32)
            return (value * jnp.abs(value)).reshape(2 * lats, quarter)

        rows = pl.ds(pl.multiple_of(j * 2 * lats, 16), 2 * lats)
        for half in range(2):
            near, far = squared(half), squared(half + 2)
            cols = slice(half * quarter, (half + 1) * quarter)
            fold_ref[0, rows, cols] = (near + far).astype(BF16)
            fold_ref[1, rows, cols] = (near - far).astype(BF16)
        return carry

    lax.fori_loop(0, bands // 2, fold, 0)
    index = jnp.broadcast_to(lane_ref[0:1, :], (circle_ref.shape[2], LANES))

    def step(i, carry):
        table_copy(i).wait()
        span = pl.ds(i * dests, dests)
        for low in range(0, tiles, 2):
            many = min(2, tiles - low)
            rows = slice(low * LANES, (low + many) * LANES)
            values = [
                lax.dot_general(
                    circle_ref[i, kind], fold_ref[kind, rows, :], NT, preferred_element_type=F32
                )
                for kind in range(2)
            ]
            for at in range(many):
                place = jnp.where(south == 1, tiles - 1 - (low + at), low + at)
                both = []
                for kind in range(2):
                    value = jnp.take_along_axis(
                        values[kind][:, at * LANES : (at + 1) * LANES],
                        index,
                        axis=1,
                        mode="promise_in_bounds",
                    )
                    both.append(value[:main].reshape(dests, 8, LANES))
                    for r in range(2):
                        spot = pl.ds(place * 4 + kind * 2 + r, dests, stride=end)
                        tail_ref[spot, :] = value[main + r * dests : main + (r + 1) * dests]
                rows16 = pl.ds(pl.multiple_of(place * 16, 16), 16)
                out_ref[span, rows16, :] = jnp.concatenate(both, axis=1).astype(BF16)
        last = tail_ref[...].reshape(dests, end, LANES)
        out_ref[span, tiles * 16 :, :] = last.astype(BF16)
        return carry

    lax.fori_loop(0, steps, step, 0)


def fourier(south, received, circle, lane_index, dev_count):
    steps = circle.shape[0]
    dests = dev_count // steps
    _, bands, lats, quarter = received.shape
    lat_half = bands * lats
    tiles = lat_half // LANES
    end = -(-tiles * 4 // 8) * 8
    rows = tiles * 16 + end
    return pl.pallas_call(
        fourier_kernel,
        in_specs=[pl.BlockSpec(memory_space=pltpu.SMEM), VMEM_SPEC, HBM_SPEC, VMEM_SPEC],
        out_specs=VMEM_SPEC,
        scratch_shapes=[
            pltpu.VMEM(circle.shape, BF16),
            pltpu.VMEM((2, lat_half, 2 * quarter), BF16),
            pltpu.VMEM((dests * end, LANES), F32),
            pltpu.SemaphoreType.DMA((steps,)),
        ],
        out_shape=jax.ShapeDtypeStruct((dev_count, rows, LANES), BF16),
        compiler_params=pltpu.CompilerParams(vmem_limit_bytes=FOURIER_VMEM),
        cost_estimate=pl.CostEstimate(
            flops=2 * circle.size * lat_half,
            bytes_accessed=2 * (received.size + circle.size + dev_count * rows * LANES),
            transcendentals=0,
        ),
        name="fourier",
    )(south, received, in_hbm(circle), lane_index)


FOURIER_VMEM = 24 * 1024 * 1024
LEGENDRE_VMEM = 24 * 1024 * 1024


def gather_kernel(first, me_ref, recv_ref, basis_ref, x_ref, part_ref, main_ref, tail_ref, sem):
    levs = recv_ref.shape[1]
    group = recv_ref.shape[0] // 2
    slots, _, _, tiles, rows, _ = x_ref.shape
    end = recv_ref.shape[2] - tiles * 16
    part = rows // levs
    copies = slot_copies(basis_ref, part_ref, sem, first)
    for copy in copies:
        copy.start()

    def step(x, carry):
        base = lax.rem(x - me_ref[0] + levs, levs) * part

        def sides(span, height, into):
            n = recv_ref[:group, x, span, :].astype(F32).reshape(group * height, LANES)
            s = recv_ref[group:, x, span, :].astype(F32).reshape(group * height, LANES)
            into[0] = n + s
            into[1] = n - s

        def put(slot, kind, tile, r, from_ref, start, stride):
            dest = pl.ds(pl.multiple_of(base + r * group, 16), group)
            for par in range(2):
                value = from_ref[par, pl.ds(start, group, stride=stride), :]
                x_ref[slot, par, kind, tile, dest, :] = value.astype(BF16)

        for tile in range(tiles):
            sides(slice(tile * 16, tile * 16 + 16), 16, main_ref.at[tile])
            for kind in range(2):
                for k in range(slots - 1):
                    for r in range(2):
                        put(k, kind, tile, r, main_ref.at[tile], kind * 8 + k * 2 + r, 16)
        sides(slice(tiles * 16, tiles * 16 + end), end, tail_ref)
        for tile in range(tiles):
            for kind in range(2):
                for r in range(2):
                    put(slots - 1, kind, tile, r, tail_ref, tile * 4 + kind * 2 + r, end)
        return carry

    lax.fori_loop(0, levs, step, 0)
    for copy in copies:
        copy.wait()


def slot_copies(basis_ref, part_ref, sem, first):
    return [
        pltpu.make_async_copy(basis_ref.at[first + k], part_ref.at[k], sem.at[k])
        for k in range(part_ref.shape[0])
    ]


def gather(me, received, basis, chunk):
    slots, cols, lats = basis.shape
    lat_count, levs, rows, _ = received.shape
    group = lat_count // 2
    tiles = lats // LANES
    end = rows - tiles * 16
    first, count = chunk
    return pl.pallas_call(
        functools.partial(gather_kernel, first),
        in_specs=[pl.BlockSpec(memory_space=pltpu.SMEM), VMEM_SPEC, HBM_SPEC],
        out_specs=[VMEM_SPEC] * 2,
        scratch_shapes=[
            pltpu.VMEM((tiles, 2, group * 16, LANES), F32),
            pltpu.VMEM((2, group * end, LANES), F32),
            pltpu.SemaphoreType.DMA((count,)),
        ],
        out_shape=[
            jax.ShapeDtypeStruct((slots, 2, 2, tiles, levs * 2 * group, LANES), BF16),
            jax.ShapeDtypeStruct((count, cols, lats), BF16),
        ],
        compiler_params=pltpu.CompilerParams(vmem_limit_bytes=LEGENDRE_VMEM),
        cost_estimate=pl.CostEstimate(
            flops=20 * received.size, bytes_accessed=4 * received.size, transcendentals=0
        ),
        name="gather",
    )(me, received, in_hbm(basis))


def legendre_kernel(scale, norm, levs, first, ahead, pairs_ref, x_ref, basis_ref, rate_ref, *refs):
    copies = []
    if ahead is not None:
        all_ref, part_ref, sem = refs[0], refs[1 + levs], refs[2 + levs]
        copies = slot_copies(all_ref, part_ref, sem, ahead)
        refs = refs[1:]
    for copy in copies:
        copy.start()
    out_refs = refs[:levs]
    count = basis_ref.shape[0]
    waves = basis_ref.shape[1] - 1
    tiles, rows = x_ref.shape[3:5]
    part = rows // levs
    width = 256
    rates = jnp.concatenate([rate_ref[...]] * (width // LANES), axis=1)

    def slot_step(k, carry):
        pair = pairs_ref[k + first]
        bound = waves - pair
        first_kind = lax.rem(pair, 2)

        def damping(column, second):
            degree = jnp.where(second, column - 1, pair + column)
            scaled = (degree * (degree + 1)).astype(F32) / norm
            return scale / (1.0 + rates[:, : column.shape[1]] * (scaled * scaled))

        def emit(start, value):
            value = value.astype(BF16)
            for s in range(levs):
                out_refs[s][k, :, start : start + value.shape[1]] = value[s * part : (s + 1) * part]

        def side(par, kind):
            return jnp.concatenate([x_ref[k + first, par, kind, t] for t in range(tiles)], axis=1)

        def block(start):
            column = start + lax.broadcasted_iota(jnp.int32, (1, width), 1)
            second = column >= bound
            even = lax.rem(jnp.where(second, column + pair, column), 2) == 0
            factor = damping(column, second)
            basis = basis_ref[k, start : start + width, :]

            def product(kind):
                left = jnp.concatenate([side(0, kind), side(1, kind)], axis=0)
                both = lax.dot_general(left, basis, NT, preferred_element_type=F32)
                return jnp.where(even, both[:rows], both[rows:]) * factor

            value = product(jnp.where(start >= bound, 1 - first_kind, first_kind))
            emit(start, value)

            @pl.when((start < bound) & (bound < start + width))
            def _():
                emit(start, jnp.where(second, product(1 - first_kind), value))

        for start in range(0, waves, width):
            block(start)
        column = jnp.full((1, 1), waves, jnp.int32)
        left = side(first_kind, 1 - first_kind).astype(F32)
        final = jnp.sum(left * basis_ref[k, waves:, :].astype(F32), axis=1, keepdims=True)
        emit(waves, final * damping(column, column >= bound))
        return carry

    lax.fori_loop(0, count, slot_step, 0)
    for copy in copies:
        copy.wait()


def legendre(first, ahead, pairs, x, basis, basis_all, rates, levs, lon_count, norm):
    count, cols, lats = basis.shape
    part = x.shape[4] // levs
    specs = [pl.BlockSpec(memory_space=pltpu.SMEM), VMEM_SPEC, VMEM_SPEC, VMEM_SPEC]
    shapes = [jax.ShapeDtypeStruct((count, part, cols), BF16)] * levs
    operands, scratch = [pairs, x, basis, rates], []
    if ahead is not None:
        specs.append(HBM_SPEC)
        operands.append(in_hbm(basis_all))
        shapes.append(jax.ShapeDtypeStruct((ahead[1], cols, lats), BF16))
        scratch.append(pltpu.SemaphoreType.DMA((ahead[1],)))
    return pl.pallas_call(
        functools.partial(
            legendre_kernel, 1.0 / lon_count, norm, levs, first, ahead and ahead[0]
        ),
        in_specs=specs,
        out_specs=[VMEM_SPEC] * len(shapes),
        out_shape=shapes,
        scratch_shapes=scratch,
        compiler_params=pltpu.CompilerParams(vmem_limit_bytes=LEGENDRE_VMEM),
        cost_estimate=pl.CostEstimate(
            flops=2 * count * cols * lats * 256,
            bytes_accessed=2 * count * cols * (lats + 128),
            transcendentals=0,
        ),
        name="legendre",
    )(*operands)


def assemble_kernel(counts, me_ref, *refs):
    levs = refs[-2].shape[1]
    out_ref, sem = refs[-2:]
    copies, low = [], 0
    for c, count in enumerate(counts):
        for s in range(levs):
            lev = lax.rem(me_ref[0] - s + levs, levs)
            n = c * levs + s
            dest = out_ref.at[low : low + count, lev]
            copies.append(pltpu.make_async_copy(refs[n], dest, sem.at[n]))
        low += count
    for copy in copies:
        copy.start()
    for copy in copies:
        copy.wait()


def assemble(me, parts):
    levs = len(parts[0])
    _, part, cols = parts[0][0].shape
    counts = [p[0].shape[0] for p in parts]
    flat = [a for p in parts for a in p]
    anywhere = pl.BlockSpec(memory_space=pl.ANY)
    return pl.pallas_call(
        functools.partial(assemble_kernel, counts),
        in_specs=[pl.BlockSpec(memory_space=pltpu.SMEM)] + [anywhere] * len(flat),
        out_specs=anywhere,
        scratch_shapes=[pltpu.SemaphoreType.DMA((len(flat),))],
        out_shape=jax.ShapeDtypeStruct((sum(counts), levs, part, cols), BF16),
        compiler_params=pltpu.CompilerParams(vmem_limit_bytes=1024 * 1024),
        name="assemble",
    )(me, *flat)


def transform(grid_values, basis_table, damping_rates, pair_table):
    levs, lat_count = lax.axis_size("lev"), lax.axis_size("lat")
    dev_count = levs * lat_count
    half_bands = lat_count // 2
    lon_count = grid_values.shape[2] * levs
    slots, cols = basis_table.shape[1], basis_table.shape[2]
    top = cols - 2
    group = half_bands
    me_lev, me_lat = lax.axis_index("lev"), lax.axis_index("lat")
    south = (me_lat >= half_bands).astype(jnp.int32)

    halves = [
        [x * lat_count + h * half_bands + b for x in range(levs) for b in range(half_bands)]
        for h in range(2)
    ]
    everyone = [[x * lat_count + b for b in range(lat_count) for x in range(levs)]]
    circles = lax.all_to_all(
        grid_values, ("lev", "lat"), 0, 0, axis_index_groups=halves, tiled=True
    )
    circles = circles.reshape((levs, half_bands) + grid_values.shape[1:])

    steps = 2
    table = jnp.transpose(pair_table.reshape(levs, lat_count, slots), (1, 0, 2))
    table = table.reshape(steps, dev_count // steps, slots)
    other = top - table
    odd = table % 2 == 1
    kinds = []
    for wave in (jnp.where(odd, other, table), jnp.where(odd, table, other)):
        head = jnp.repeat(wave[:, :, : slots - 1], 2, axis=2).reshape(steps, -1)
        kinds.append(jnp.concatenate([head, wave[:, :, slots - 1], wave[:, :, slots - 1]], axis=1))
    waves = jnp.stack(kinds, axis=1)
    row = jnp.arange(waves.shape[2], dtype=jnp.int32)
    main = dev_count // steps * 2 * (slots - 1)
    quarters = jnp.where(row < main, row % 2, (row >= main + dev_count // steps).astype(jnp.int32))
    quarters = jnp.broadcast_to(quarters, waves.shape)
    lane = jnp.arange(LANES, dtype=jnp.int32)
    lane_index = jnp.broadcast_to(jnp.where(south == 1, LANES - 1 - lane, lane), (8, LANES))
    me = me_lev[None].astype(jnp.int32)
    pairs = lax.dynamic_slice_in_dim(pair_table, (me_lev * lat_count + me_lat) * slots, slots)
    rates = jnp.roll(damping_rates.reshape(levs, 1, group), -me_lev, axis=0)
    rates = jnp.broadcast_to(rates, (levs, 2, group)).reshape(-1, 1)
    rates = jnp.broadcast_to(rates, (rates.shape[0], LANES))
    spread = lambda v: jnp.broadcast_to(v.reshape(-1)[:, None], (v.size, LANES))
    wave_rows, quarter_rows, lane_index, south, me, pairs, rates = lax.optimization_barrier(
        (spread(waves), spread(quarters), lane_index, south[None], me, pairs, rates)
    )
    circle = circle_table(wave_rows, quarter_rows, lon_count, lon_count // 2)
    circle = circle.reshape(waves.shape + (lon_count // 2,))
    packed = fourier(south, circles, circle, lane_index, dev_count)
    received = lax.all_to_all(
        packed, ("lev", "lat"), 0, 0, axis_index_groups=everyone, tiled=True
    ).reshape((lat_count, levs) + packed.shape[1:])
    basis = jnp.transpose(basis_table, (1, 2, 0))
    x, ready = gather(me, received, basis, CHUNKS[0])
    parts = []
    for c, (first, count) in enumerate(CHUNKS):
        ahead = CHUNKS[c + 1] if c + 1 < len(CHUNKS) else None
        norm = float(top * (top + 1))
        outs = legendre(
            first, ahead, pairs, x, ready, basis, rates, levs, lon_count, norm
        )
        ready = outs[-1]
        moved = [outs[0]]
        for s in range(1, levs):
            to = [(i, (i + s) % levs) for i in range(levs)]
            moved.append(lax.ppermute(outs[s], "lev", to))
        parts.append(moved)
    return assemble(me, parts).reshape(slots, levs, 2, group, cols)


CHUNKS = ((0, 2), (2, 3))


def solution(mesh):
    placed = (P(None, "lat", "lev"), P(None, ("lev", "lat"), None), P(), P())
    return jax.shard_map(
        transform,
        mesh=mesh,
        in_specs=placed,
        out_specs=P("lat", None, None, "lev", None),
        check_vma=False,
    )
```

time: 168 us -> 151 us (0.90); the launches traced: 165 us -> 151 us
  blocking collectives: 0 us -> 53.1 us
  waiting for transfers between devices: 62.8 us -> 36.9 us
  Pallas kernels: 53.1 us -> 27.4 us
  starting transfers between devices: 28.8 us -> 19.6 us
  local copies, waits for them, and re-layouts: 17.8 us -> 13 us
    all_to_all x0 -> x1, blocking collectives: none -> 53.1 us  [transform(): lax.all_to_all(packed, ('lev', 'lat'), 0, 0, axis_index_groups=everyone,...]
    all_to_all x1 -> x0, waiting for transfers between devices: 43.3 us -> none  [transform(): lax.all_to_all(packed, ('lev', 'lat'), 0, 0, axis_index_groups=everyone,...]
    all_to_all x1, waiting for transfers between devices: 4.22 us -> 21.9 us  [transform(): lax.all_to_all(grid_values, ('lev', 'lat'), 0, 0, axis_index_groups=halve...]
    pallas_call x1 -> x2, Pallas kernels: 21.9 us -> 7.53 us  [the longest x1 5.16 us: circle_table(): pl.pallas_call(functools.partial(circle_kernel, lon_count), in_specs=[VME...]
    all_to_all x1 -> x0, starting transfers between devices: 9.19 us -> none  [transform(): lax.all_to_all(packed, ('lev', 'lat'), 0, 0, axis_index_groups=everyone,...]
    pallas_call x2, Pallas kernels: 19.4 us -> 10.8 us  [legendre(): pl.pallas_call(functools.partial(legendre_kernel, 1.0 / lon_count, norm,...]
    pallas_call x1, Pallas kernels: 10.6 us -> 7.87 us  [fourier(): pl.pallas_call(fourier_kernel, in_specs=[pl.BlockSpec(memory_space=pltpu....]
    broadcast_in_dim x4 -> x6, local copies, waits for them, and re-layouts: 3.97 us -> 2.23 us  [the longest x2 1.4 us: transform(): rates = jnp.broadcast_to(rates, (rates.shape[0], LANES))]
  transfers between devices with their start and end apart: 8 -> 7, of which waited for: 4 -> 3; matrix products, arithmetic and copies ran while one was open for 9% -> 7% of each run, Pallas kernels for 20% -> 8%
where the time goes in v3:
time: 151 us
  blocking collectives  53.1 us (35%)
  waiting for transfers between devices  36.9 us (24%)
  Pallas kernels  27.4 us (18%)
  starting transfers between devices  19.6 us (13%)
  local copies, waits for them, and re-layouts  13 us (9%)
    all_to_all x1, blocking collectives, transform(): lax.all_to_all(packed, ('lev', 'lat'), 0, 0, axis_index_groups=everyone,...  53.1 us
    all_to_all x1, waiting for transfers between devices, transform(): lax.all_to_all(grid_values, ('lev', 'lat'), 0, 0, axis_index_groups=halve...  21.9 us
    ppermute x6, waiting for transfers between devices, transform(): moved.append(lax.ppermute(outs[s], 'lev', to))  15.1 us
    pallas_call x2, Pallas kernels, legendre(): pl.pallas_call(functools.partial(legendre_kernel, 1.0 / lon_count, norm,...  10.8 us
    all_to_all x1, starting transfers between devices, transform(): lax.all_to_all(grid_values, ('lev', 'lat'), 0, 0, axis_index_groups=halve...  10 us
    ppermute x6, starting transfers between devices, transform(): moved.append(lax.ppermute(outs[s], 'lev', to))  9.52 us
    pallas_call x1, Pallas kernels, fourier(): pl.pallas_call(fourier_kernel, in_specs=[pl.BlockSpec(memory_space=pltpu....  7.87 us
    pallas_call x1, Pallas kernels, circle_table(): pl.pallas_call(functools.partial(circle_kernel, lon_count), in_specs=[VME...  5.16 us
  transfers between devices with their start and end apart: 7, of which 3 were waited for; matrix products, arithmetic and copies ran while one was open for 7% of the time, Pallas kernels for 8%

profile of v3, /device:TPU:0, one launch (start us, length us, event | category | flops | bytes accessed | tf_op | source)
XLA Modules:
  0.0 151.0 jit_solution(7208662152377868813)
XLA Ops:
  0.0 0.0 copy-start.3
  0.0 10.0 %all-to-all-start = ((bf16[64,40,640]{2,1,0:T(8,128)(2,1)}), bf16[64,40,640]{2,1,0:T(8,128)(2,1)S(1)}, u32[]{:S(2)}, u32[]{:S(2)}) async-start(bf16[64,40,640]{2,1,0:T(8,128)(2,1)} %param.4), calls=%async_computation | async-start | bytes 6553600 | tf_op jit(solution)/shard_map/all_to_all | solution.py:408
  10.1 0.0 copy-done.3
  10.1 0.2 reshape.25
  10.3 0.1 dynamic_slice.7.pairs_ref
  10.4 0.0 copy-done.4
  10.4 0.1 reshape.27
  10.5 0.7 broadcast_in_dim.58
  11.2 0.3 copy.7
  11.5 0.1 reshape.26
  11.7 0.0 copy-start.1
  11.7 0.0 copy-start.2
  11.7 0.6 copy-done.2
  12.3 0.0 copy-done.1
  12.3 0.7 copy.8
  13.0 0.7 copy.9
  13.8 1.0 broadcast_in_dim.47
  14.8 0.8 reshape_reshape.7
  15.7 1.0 broadcast_in_dim.46
  16.7 0.8 reshape_reshape.6
  17.5 0.7 slice_bitcast_fusion
  18.2 0.7 slice_bitcast_fusion.1
  18.9 0.8 add_bitcast_fusion
  19.7 0.7 broadcast_in_dim.59.rate_ref
  20.5 0.4 broadcast_in_dim.49.wave_ref
  20.9 0.4 broadcast_in_dim.52.quarter_ref
  21.3 5.2 %circle.1 = bf16[2560,1280]{1,0:T(8,128)(2,1)S(1)} custom-call(s32[2560,128]{1,0:T(8,128)S(1)} %broadcast_in_dim.49.wave_ref, s32[2560,128]{1,0:T(8,128)S(1)} %broadcast_in_dim.52.quarter_ref), custom_call_target="tpu_custom_call" | custom-call | flops 32768000 | bytes 6553600 | tf_op jit(solution)/shard_map/circle/pallas_call | solution.py:59
  26.4 0.0 copy-start
  26.4 2.7 %copy-done = bf16[2560,1280]{1,0:T(8,128)(2,1)} copy-done((bf16[2560,1280]{1,0:T(8,128)(2,1)}, bf16[2560,1280]{1,0:T(8,128)(2,1)S(1)}, u32[]{:S(2)}) %copy-start) | copy-done | bytes 6553624
  29.1 21.9 %all-to-all-done = bf16[64,40,640]{2,1,0:T(8,128)(2,1)S(1)} async-done(((bf16[64,40,640]{2,1,0:T(8,128)(2,1)}), bf16[64,40,640]{2,1,0:T(8,128)(2,1)S(1)}, u32[]{:S(2)}, u32[]{:S(2)}) %all-to-all-start) | async-done | bytes 3276832 | tf_op jit(solution)/shard_map/all_to_all | solution.py:408
  51.0 7.9 %fourier.1 = bf16[128,104,128]{2,1,0:T(8,128)(2,1)S(1)} custom-call(s32[1]{0:T(128)} %bitcast.5.south_ref, bf16[4,16,40,640]{3,2,1,0:T(8,128)(2,1)S(1)} %bitcast.22, bf16[2,2,640,1280]{3,2,1,0:T(8,128)(2,1)} %bitcast.21, s32[8,128]{1,0:T(8,128)S(1)} %broadcast_in_dim.53.lane_ref), custom_call_target="tpu_custom_call" | custom-call | flops 4194304000 | bytes 13238272 | tf_op jit(solution)/shard_map/fourier/pallas_call | solution.py:160
  58.9 53.1 %all_to_all.10 = bf16[128,104,128]{2,1,0:T(8,128)(2,1)S(1)} all-to-all(bf16[128,104,128]{2,1,0:T(8,128)(2,1)S(1)} %fourier.1), channel_id=1, replica_groups={{0,32,64,96,1,33,65,97,2,34,66,98,3,35,67,99,4,36,68,100,5,37,69,101,6,..., dimensions={0} | all-to-all | bytes 6815744 | tf_op jit(solution)/shard_map/all_to_all | solution.py:441
  112.0 2.4 %gather.1 = (bf16[5,2,2,5,128,128]{5,4,3,2,1,0:T(8,128)(2,1)S(1)}, bf16[2,1281,640]{2,1,0:T(8,128)(2,1)S(1)}) custom-call(s32[1]{0:T(128)} %bitcast.6.me_ref, bf16[32,4,104,128]{3,2,1,0:T(8,128)(2,1)S(1)} %bitcast.20, bf16[5,1281,640]{2,1,0:T(8,128)(2,1)} %bitcast.23), custom_call_target="tpu_custom_call" | custom-call | flops 34078720 | bytes 6815744 | tf_op jit(solution)/shard_map/gather/pallas_call | solution.py:242
  114.3 4.4 %legendre.2 = (bf16[2,32,1281]{2,1,0:T(8,128)(2,1)S(1)}, bf16[2,32,1281]{2,1,0:T(8,128)(2,1)S(1)}, bf16[2,32,1281]{2,1,0:T(8,128)(2,1)S(1)}, bf16[2,32,1281]{2,1,0:T(8,128)(2,1)S(1)}, bf16[3,1281,640]{2,1,0:T(8,128)(2,1)S(1)}) custom-call(s32[5]{0:T(128)S(1)} %dynamic_slice.7.pairs_ref, bf16[5,2,2,5,128,128]{5,4,3,2,1,0:T(8,128)(2,1)S(1)} %get-tuple-element.29.x_ref, ...), custom_call_target="tpu_custom_call" | custom-call | flops 839516160 | bytes 3935232 | tf_op jit(solution)/shard_map/legendre/pallas_call | solution.py:340
  118.8 0.7 collective-permute-start
  119.4 6.3 %legendre.3 = (bf16[3,32,1281]{2,1,0:T(8,128)(2,1)S(1)}, bf16[3,32,1281]{2,1,0:T(8,128)(2,1)S(1)}, bf16[3,32,1281]{2,1,0:T(8,128)(2,1)S(1)}, bf16[3,32,1281]{2,1,0:T(8,128)(2,1)S(1)}) custom-call(s32[5]{0:T(128)S(1)} %dynamic_slice.7.pairs_ref, bf16[5,2,2,5,128,128]{5,4,3,2,1,0:T(8,128)(2,1)S(1)} %get-tuple-element.29.x_ref, ...), custom_call_target="tpu_custom_call" | custom-call | flops 1259274240 | bytes 5902848 | tf_op jit(solution)/shard_map/legendre/pallas_call | solution.py:340
  125.8 1.0 collective-permute-start.3
  126.7 3.2 %collective-permute-start.4 = (bf16[3,32,1281]{2,1,0:T(8,128)(2,1)S(1)}, bf16[3,32,1281]{2,1,0:T(8,128)(2,1)S(1)}, u32[]{:S(2)}, u32[]{:S(2)}) collective-permute-start(bf16[3,32,1281]{2,1,0:T(8,128)(2,1)S(1)} %get-tuple-element.39), channel_id=1, source_target_pairs={{0,64},{32,96},{64,0},{96,32},{1,65},{33,97},{65,1},{97,33},{2,66}... | collective-permute-start | bytes 737864 | tf_op jit(solution)/shard_map/ppermute | solution.py:457
  129.9 1.1 collective-permute-start.5
  131.0 0.9 collective-permute-start.1
  132.0 0.0 collective-permute-done.refs_1_
  132.0 2.6 %collective-permute-start.2 = (bf16[2,32,1281]{2,1,0:T(8,128)(2,1)S(1)}, bf16[2,32,1281]{2,1,0:T(8,128)(2,1)S(1)}, u32[]{:S(2)}, u32[]{:S(2)}) collective-permute-start(bf16[2,32,1281]{2,1,0:T(8,128)(2,1)S(1)} %get-tuple-element.35), channel_id=1, source_target_pairs={{0,96},{32,0},{64,32},{96,64},{1,97},{33,1},{65,33},{97,65},{2,98}... | collective-permute-start | bytes 491912 | tf_op jit(solution)/shard_map/ppermute | solution.py:457
  134.6 11.4 %collective-permute-done.1.refs_2_ = bf16[2,32,1281]{2,1,0:T(8,128)(2,1)S(1)} collective-permute-done((bf16[2,32,1281]{2,1,0:T(8,128)(2,1)S(1)}, bf16[2,32,1281]{2,1,0:T(8,128)(2,1)S(1)}, u32[]{:S(2)}, u32[]{:S(2)}) %collective-permute-start.1) | collective-permute-done | bytes 164000 | tf_op jit(solution)/shard_map/ppermute | solution.py:457
  146.0 3.7 %collective-permute-done.2.refs_3_ = bf16[2,32,1281]{2,1,0:T(8,128)(2,1)S(1)} collective-permute-done((bf16[2,32,1281]{2,1,0:T(8,128)(2,1)S(1)}, bf16[2,32,1281]{2,1,0:T(8,128)(2,1)S(1)}, u32[]{:S(2)}, u32[]{:S(2)}) %collective-permute-start.2) | collective-permute-done | bytes 164000 | tf_op jit(solution)/shard_map/ppermute | solution.py:457
  149.7 0.0 collective-permute-done.3.refs_5_
  149.7 0.0 collective-permute-done.4.refs_6_
  149.7 0.0 collective-permute-done.5.refs_7_
  149.7 1.3 assemble.1
  (16 shorter events, 0.1 us)
Async XLA Ops:
  0.0 10.1 %copy-start.3 = (s32[640]{0:T(1024)S(1)}, s32[640]{0:T(1024)}, u32[]{:S(2)}) copy-start(s32[640]{0:T(1024)} %param.7) | copy-start | bytes 7684
  0.0 10.4 %copy-start.4 = (f32[64]{0:T(128)S(1)}, f32[64]{0:T(128)}, u32[]{:S(2)}) copy-start(f32[64]{0:T(128)} %param.6) | copy-start | bytes 772
  0.0 51.0 %all-to-all-start = ((bf16[64,40,640]{2,1,0:T(8,128)(2,1)}), bf16[64,40,640]{2,1,0:T(8,128)(2,1)S(1)}, u32[]{:S(2)}, u32[]{:S(2)}) async-start(bf16[64,40,640]{2,1,0:T(8,128)(2,1)} %param.4), calls=%async_computation | async-start | bytes 6553600 | tf_op jit(solution)/shard_map/all_to_all | solution.py:408
  11.7 0.6 copy-start.1
  11.7 0.6 copy-start.2
  26.4 2.7 %copy-start = (bf16[2560,1280]{1,0:T(8,128)(2,1)}, bf16[2560,1280]{1,0:T(8,128)(2,1)S(1)}, u32[]{:S(2)}) copy-start(bf16[2560,1280]{1,0:T(8,128)(2,1)S(1)} %circle.1) | copy-start | bytes 19660804
  118.8 13.2 %collective-permute-start = (bf16[2,32,1281]{2,1,0:T(8,128)(2,1)S(1)}, bf16[2,32,1281]{2,1,0:T(8,128)(2,1)S(1)}, u32[]{:S(2)}, u32[]{:S(2)}) collective-permute-start(bf16[2,32,1281]{2,1,0:T(8,128)(2,1)S(1)} %get-tuple-element.33), channel_id=1, source_target_pairs={{0,32},{32,64},{64,96},{96,0},{1,33},{33,65},{65,97},{97,1},{2,34}... | collective-permute-start | bytes 491912 | tf_op jit(solution)/shard_map/ppermute | solution.py:457
  125.8 23.9 %collective-permute-start.3 = (bf16[3,32,1281]{2,1,0:T(8,128)(2,1)S(1)}, bf16[3,32,1281]{2,1,0:T(8,128)(2,1)S(1)}, u32[]{:S(2)}, u32[]{:S(2)}) collective-permute-start(bf16[3,32,1281]{2,1,0:T(8,128)(2,1)S(1)} %get-tuple-element.38), channel_id=1, source_target_pairs={{0,32},{32,64},{64,96},{96,0},{1,33},{33,65},{65,97},{97,1},{2,34}... | collective-permute-start | bytes 737864 | tf_op jit(solution)/shard_map/ppermute | solution.py:457
  126.7 23.0 %collective-permute-start.4 = (bf16[3,32,1281]{2,1,0:T(8,128)(2,1)S(1)}, bf16[3,32,1281]{2,1,0:T(8,128)(2,1)S(1)}, u32[]{:S(2)}, u32[]{:S(2)}) collective-permute-start(bf16[3,32,1281]{2,1,0:T(8,128)(2,1)S(1)} %get-tuple-element.39), channel_id=1, source_target_pairs={{0,64},{32,96},{64,0},{96,32},{1,65},{33,97},{65,1},{97,33},{2,66}... | collective-permute-start | bytes 737864 | tf_op jit(solution)/shard_map/ppermute | solution.py:457
  129.9 19.8 %collective-permute-start.5 = (bf16[3,32,1281]{2,1,0:T(8,128)(2,1)S(1)}, bf16[3,32,1281]{2,1,0:T(8,128)(2,1)S(1)}, u32[]{:S(2)}, u32[]{:S(2)}) collective-permute-start(bf16[3,32,1281]{2,1,0:T(8,128)(2,1)S(1)} %get-tuple-element.40), channel_id=1, source_target_pairs={{0,96},{32,0},{64,32},{96,64},{1,97},{33,1},{65,33},{97,65},{2,98}... | collective-permute-start | bytes 737864 | tf_op jit(solution)/shard_map/ppermute | solution.py:457
  131.0 15.0 %collective-permute-start.1 = (bf16[2,32,1281]{2,1,0:T(8,128)(2,1)S(1)}, bf16[2,32,1281]{2,1,0:T(8,128)(2,1)S(1)}, u32[]{:S(2)}, u32[]{:S(2)}) collective-permute-start(bf16[2,32,1281]{2,1,0:T(8,128)(2,1)S(1)} %get-tuple-element.34), channel_id=1, source_target_pairs={{0,64},{32,96},{64,0},{96,32},{1,65},{33,97},{65,1},{97,33},{2,66}... | collective-permute-start | bytes 491912 | tf_op jit(solution)/shard_map/ppermute | solution.py:457
  132.0 17.7 %collective-permute-start.2 = (bf16[2,32,1281]{2,1,0:T(8,128)(2,1)S(1)}, bf16[2,32,1281]{2,1,0:T(8,128)(2,1)S(1)}, u32[]{:S(2)}, u32[]{:S(2)}) collective-permute-start(bf16[2,32,1281]{2,1,0:T(8,128)(2,1)S(1)} %get-tuple-element.35), channel_id=1, source_target_pairs={{0,96},{32,0},{64,32},{96,64},{1,97},{33,1},{65,33},{97,65},{2,98}... | collective-permute-start | bytes 491912 | tf_op jit(solution)/shard_map/ppermute | solution.py:457

commit v4 on v3

--- a/solution.py
+++ b/solution.py
@@ -12,6 +12,7 @@
 F32 = jnp.float32
 BF16 = jnp.bfloat16
 NT = (((1,), (1,)), ((), ()))
+NN = (((1,), (0,)), ((), ()))
 LANES = 128
 
 
@@ -83,7 +84,8 @@
 def fourier_kernel(
     south_ref, g_ref, table_ref, lane_ref, out_ref, circle_ref, fold_ref, tail_ref, sem
 ):
-    _, bands, lats, quarter = g_ref.shape
+    _, cores, bands, lats, quarter = g_ref.shape
+    bands = bands * cores
     steps = circle_ref.shape[0]
     tiles = bands * lats // LANES
     end = out_ref.shape[1] - tiles * 16
@@ -100,10 +102,10 @@
 
     def fold(j, carry):
         def squared(q):
-            value = g_ref[q, pl.ds(2 * j, 2)].astype(F32)
-            return (value * jnp.abs(value)).reshape(2 * lats, quarter)
-
-        rows = pl.ds(pl.multiple_of(j * 2 * lats, 16), 2 * lats)
+            value = g_ref[q, :, j].astype(F32)
+            return (value * jnp.abs(value)).reshape(cores * lats, quarter)
+
+        rows = pl.ds(pl.multiple_of(j * cores * lats, 16), cores * lats)
         for half in range(2):
             near, far = squared(half), squared(half + 2)
             cols = slice(half * quarter, (half + 1) * quarter)
@@ -111,7 +113,7 @@
             fold_ref[1, rows, cols] = (near - far).astype(BF16)
         return carry
 
-    lax.fori_loop(0, bands // 2, fold, 0)
+    lax.fori_loop(0, bands // cores, fold, 0)
     index = jnp.broadcast_to(lane_ref[0:1, :], (circle_ref.shape[2], LANES))
 
     def step(i, carry):
@@ -152,8 +154,8 @@
 def fourier(south, received, circle, lane_index, dev_count):
     steps = circle.shape[0]
     dests = dev_count // steps
-    _, bands, lats, quarter = received.shape
-    lat_half = bands * lats
+    _, cores, bands, lats, quarter = received.shape
+    lat_half = cores * bands * lats
     tiles = lat_half // LANES
     end = -(-tiles * 4 // 8) * 8
     rows = tiles * 16 + end
@@ -182,22 +184,20 @@
 LEGENDRE_VMEM = 24 * 1024 * 1024
 
 
-def gather_kernel(first, me_ref, recv_ref, basis_ref, x_ref, part_ref, main_ref, tail_ref, sem):
-    levs = recv_ref.shape[1]
-    group = recv_ref.shape[0] // 2
-    slots, _, _, tiles, rows, _ = x_ref.shape
-    end = recv_ref.shape[2] - tiles * 16
+def gather_kernel(first, total, me_ref, recv_ref, x_ref, main_ref, tail_ref):
+    levs, nc, ny, nz = recv_ref.shape[:4]
+    group = nc * ny * nz // 2
+    count, _, _, tiles, rows, _ = x_ref.shape
+    mains = range(first, min(first + count, total - 1))
+    end = recv_ref.shape[4] - tiles * 16
     part = rows // levs
-    copies = slot_copies(basis_ref, part_ref, sem, first)
-    for copy in copies:
-        copy.start()
 
     def step(x, carry):
         base = lax.rem(x - me_ref[0] + levs, levs) * part
 
         def sides(span, height, into):
-            n = recv_ref[:group, x, span, :].astype(F32).reshape(group * height, LANES)
-            s = recv_ref[group:, x, span, :].astype(F32).reshape(group * height, LANES)
+            n = recv_ref[x, :, : ny // 2, :, span, :].astype(F32).reshape(group * height, LANES)
+            s = recv_ref[x, :, ny // 2 :, :, span, :].astype(F32).reshape(group * height, LANES)
             into[0] = n + s
             into[1] = n - s
 
@@ -205,78 +205,97 @@
             dest = pl.ds(pl.multiple_of(base + r * group, 16), group)
             for par in range(2):
                 value = from_ref[par, pl.ds(start, group, stride=stride), :]
-                x_ref[slot, par, kind, tile, dest, :] = value.astype(BF16)
+                x_ref[slot - first, par, kind, tile, dest, :] = value.astype(BF16)
 
         for tile in range(tiles):
             sides(slice(tile * 16, tile * 16 + 16), 16, main_ref.at[tile])
             for kind in range(2):
-                for k in range(slots - 1):
+                for k in mains:
                     for r in range(2):
                         put(k, kind, tile, r, main_ref.at[tile], kind * 8 + k * 2 + r, 16)
-        sides(slice(tiles * 16, tiles * 16 + end), end, tail_ref)
-        for tile in range(tiles):
-            for kind in range(2):
-                for r in range(2):
-                    put(slots - 1, kind, tile, r, tail_ref, tile * 4 + kind * 2 + r, end)
+        if first + count == total:
+            sides(slice(tiles * 16, tiles * 16 + end), end, tail_ref)
+            for tile in range(tiles):
+                for kind in range(2):
+                    for r in range(2):
+                        put(total - 1, kind, tile, r, tail_ref, tile * 4 + kind * 2 + r, end)
         return carry
 
     lax.fori_loop(0, levs, step, 0)
-    for copy in copies:
-        copy.wait()
-
-
-def slot_copies(basis_ref, part_ref, sem, first):
-    return [
-        pltpu.make_async_copy(basis_ref.at[first + k], part_ref.at[k], sem.at[k])
-        for k in range(part_ref.shape[0])
-    ]
-
-
-def gather(me, received, basis, chunk):
+
+
+def turn_kernel(basis_ref, out_ref, last_ref):
+    lats, waves = out_ref.shape[1:]
+    size = 256
+    row = lax.broadcasted_iota(jnp.int32, (size, size), 0)
+    eye = (row == lax.broadcasted_iota(jnp.int32, (size, size), 1)).astype(BF16)
+    for start in range(0, waves, size):
+        for low in range(0, lats, size):
+            high = min(low + size, lats)
+            out_ref[0, low:high, start : start + size] = lax.dot_general(
+                eye[: high - low, : high - low],
+                basis_ref[0, start : start + size, low:high],
+                NT,
+                preferred_element_type=F32,
+            ).astype(BF16)
+    last_ref[0] = basis_ref[0, waves:, :]
+
+
+def turn(basis):
     slots, cols, lats = basis.shape
-    lat_count, levs, rows, _ = received.shape
-    group = lat_count // 2
+    return pl.pallas_call(
+        turn_kernel,
+        grid=(slots,),
+        in_specs=[pl.BlockSpec((1, cols, lats), lambda k: (k, 0, 0))],
+        out_specs=[
+            pl.BlockSpec((1, lats, cols - 1), lambda k: (k, 0, 0)),
+            pl.BlockSpec((1, 1, lats), lambda k: (k, 0, 0)),
+        ],
+        out_shape=[
+            jax.ShapeDtypeStruct((slots, lats, cols - 1), BF16),
+            jax.ShapeDtypeStruct((slots, 1, lats), BF16),
+        ],
+        compiler_params=pltpu.CompilerParams(vmem_limit_bytes=LEGENDRE_VMEM),
+        cost_estimate=pl.CostEstimate(
+            flops=2 * 256 * basis.size, bytes_accessed=4 * basis.size, transcendentals=0
+        ),
+        name="turn",
+    )(basis)
+
+
+def gather(first, count, me, received, slots, lats):
+    levs, nc, ny, nz, rows, _ = received.shape
+    group = nc * ny * nz // 2
     tiles = lats // LANES
     end = rows - tiles * 16
-    first, count = chunk
-    return pl.pallas_call(
-        functools.partial(gather_kernel, first),
-        in_specs=[pl.BlockSpec(memory_space=pltpu.SMEM), VMEM_SPEC, HBM_SPEC],
-        out_specs=[VMEM_SPEC] * 2,
+    return pl.pallas_call(
+        functools.partial(gather_kernel, first, slots),
+        in_specs=[pl.BlockSpec(memory_space=pltpu.SMEM), VMEM_SPEC],
+        out_specs=VMEM_SPEC,
         scratch_shapes=[
             pltpu.VMEM((tiles, 2, group * 16, LANES), F32),
             pltpu.VMEM((2, group * end, LANES), F32),
-            pltpu.SemaphoreType.DMA((count,)),
         ],
-        out_shape=[
-            jax.ShapeDtypeStruct((slots, 2, 2, tiles, levs * 2 * group, LANES), BF16),
-            jax.ShapeDtypeStruct((count, cols, lats), BF16),
-        ],
+        out_shape=jax.ShapeDtypeStruct((count, 2, 2, tiles, levs * 2 * group, LANES), BF16),
         compiler_params=pltpu.CompilerParams(vmem_limit_bytes=LEGENDRE_VMEM),
         cost_estimate=pl.CostEstimate(
             flops=20 * received.size, bytes_accessed=4 * received.size, transcendentals=0
         ),
         name="gather",
-    )(me, received, in_hbm(basis))
-
-
-def legendre_kernel(scale, norm, levs, first, ahead, pairs_ref, x_ref, basis_ref, rate_ref, *refs):
-    copies = []
-    if ahead is not None:
-        all_ref, part_ref, sem = refs[0], refs[1 + levs], refs[2 + levs]
-        copies = slot_copies(all_ref, part_ref, sem, ahead)
-        refs = refs[1:]
-    for copy in copies:
-        copy.start()
-    out_refs = refs[:levs]
-    count = basis_ref.shape[0]
-    waves = basis_ref.shape[1] - 1
+    )(me, received)
+
+
+def legendre_kernel(
+    scale, norm, first, count, pairs_ref, x_ref, basis_ref, last_ref, rate_ref, *out_refs
+):
+    levs = len(out_refs)
+    waves = basis_ref.shape[2]
     tiles, rows = x_ref.shape[3:5]
     part = rows // levs
     width = 256
     rates = jnp.concatenate([rate_ref[...]] * (width // LANES), axis=1)
 
-    def slot_step(k, carry):
+    def slot_step(k):
         pair = pairs_ref[k + first]
         bound = waves - pair
         first_kind = lax.rem(pair, 2)
@@ -286,65 +305,49 @@
             scaled = (degree * (degree + 1)).astype(F32) / norm
             return scale / (1.0 + rates[:, : column.shape[1]] * (scaled * scaled))
 
-        def emit(start, value):
-            value = value.astype(BF16)
-            for s in range(levs):
-                out_refs[s][k, :, start : start + value.shape[1]] = value[s * part : (s + 1) * part]
-
         def side(par, kind):
-            return jnp.concatenate([x_ref[k + first, par, kind, t] for t in range(tiles)], axis=1)
-
-        def block(start):
+            return jnp.concatenate([x_ref[k, par, kind, t] for t in range(tiles)], axis=1)
+
+        def product(start, kind):
             column = start + lax.broadcasted_iota(jnp.int32, (1, width), 1)
             second = column >= bound
             even = lax.rem(jnp.where(second, column + pair, column), 2) == 0
-            factor = damping(column, second)
-            basis = basis_ref[k, start : start + width, :]
-
-            def product(kind):
-                left = jnp.concatenate([side(0, kind), side(1, kind)], axis=0)
-                both = lax.dot_general(left, basis, NT, preferred_element_type=F32)
-                return jnp.where(even, both[:rows], both[rows:]) * factor
-
-            value = product(jnp.where(start >= bound, 1 - first_kind, first_kind))
-            emit(start, value)
-
-            @pl.when((start < bound) & (bound < start + width))
-            def _():
-                emit(start, jnp.where(second, product(1 - first_kind), value))
+            left = jnp.concatenate([side(0, kind), side(1, kind)], axis=0)
+            basis = basis_ref[k + first, :, pl.ds(start, width)]
+            both = lax.dot_general(left, basis, NN, preferred_element_type=F32)
+            value = jnp.where(even, both[:rows], both[rows:]) * damping(column, second)
+            return value.astype(BF16), second
 
         for start in range(0, waves, width):
-            block(start)
+            value, _ = product(start, jnp.where(start >= bound, 1 - first_kind, first_kind))
+            for s in range(levs):
+                out_refs[s][k, :, start : start + width] = value[s * part : (s + 1) * part]
+        start = pl.multiple_of(jnp.minimum(bound // width, waves // width - 1) * width, width)
+        value, second = product(start, 1 - first_kind)
+        for s in range(levs):
+            spot = (k, slice(None), pl.ds(start, width))
+            kept = jnp.where(second, value[s * part : (s + 1) * part].astype(F32), out_refs[s][spot].astype(F32))
+            out_refs[s][spot] = kept.astype(BF16)
         column = jnp.full((1, 1), waves, jnp.int32)
         left = side(first_kind, 1 - first_kind).astype(F32)
-        final = jnp.sum(left * basis_ref[k, waves:, :].astype(F32), axis=1, keepdims=True)
-        emit(waves, final * damping(column, column >= bound))
-        return carry
-
-    lax.fori_loop(0, count, slot_step, 0)
-    for copy in copies:
-        copy.wait()
-
-
-def legendre(first, ahead, pairs, x, basis, basis_all, rates, levs, lon_count, norm):
-    count, cols, lats = basis.shape
+        final = jnp.sum(left * last_ref[k + first].astype(F32), axis=1, keepdims=True)
+        final = (final * damping(column, column >= bound)).astype(BF16)
+        for s in range(levs):
+            out_refs[s][k, :, waves:] = final[s * part : (s + 1) * part]
+
+    for k in range(count):
+        slot_step(k)
+
+
+def legendre(first, count, pairs, x, basis, last, rates, levs, lon_count, norm):
+    _, lats, waves = basis.shape
+    cols = waves + 1
     part = x.shape[4] // levs
-    specs = [pl.BlockSpec(memory_space=pltpu.SMEM), VMEM_SPEC, VMEM_SPEC, VMEM_SPEC]
-    shapes = [jax.ShapeDtypeStruct((count, part, cols), BF16)] * levs
-    operands, scratch = [pairs, x, basis, rates], []
-    if ahead is not None:
-        specs.append(HBM_SPEC)
-        operands.append(in_hbm(basis_all))
-        shapes.append(jax.ShapeDtypeStruct((ahead[1], cols, lats), BF16))
-        scratch.append(pltpu.SemaphoreType.DMA((ahead[1],)))
-    return pl.pallas_call(
-        functools.partial(
-            legendre_kernel, 1.0 / lon_count, norm, levs, first, ahead and ahead[0]
-        ),
-        in_specs=specs,
-        out_specs=[VMEM_SPEC] * len(shapes),
-        out_shape=shapes,
-        scratch_shapes=scratch,
+    return pl.pallas_call(
+        functools.partial(legendre_kernel, 1.0 / lon_count, norm, first, count),
+        in_specs=[pl.BlockSpec(memory_space=pltpu.SMEM)] + [VMEM_SPEC] * 4,
+        out_specs=[VMEM_SPEC] * levs,
+        out_shape=[jax.ShapeDtypeStruct((count, part, cols), BF16)] * levs,
         compiler_params=pltpu.CompilerParams(vmem_limit_bytes=LEGENDRE_VMEM),
         cost_estimate=pl.CostEstimate(
             flops=2 * count * cols * lats * 256,
@@ -352,7 +355,7 @@
             transcendentals=0,
         ),
         name="legendre",
-    )(*operands)
+    )(pairs, x, basis, last, rates)
 
 
 def assemble_kernel(counts, me_ref, *refs):
@@ -396,22 +399,33 @@
     lon_count = grid_values.shape[2] * levs
     slots, cols = basis_table.shape[1], basis_table.shape[2]
     top = cols - 2
+    lat_half = basis_table.shape[0]
     group = half_bands
     me_lev, me_lat = lax.axis_index("lev"), lax.axis_index("lat")
     south = (me_lat >= half_bands).astype(jnp.int32)
 
+    ny, nz, nc = LAT_AXES
+    at = lambda x, y, z, c: x * lat_count + (y * nz + z) * nc + c
     halves = [
-        [x * lat_count + h * half_bands + b for x in range(levs) for b in range(half_bands)]
+        [
+            at(x, y + h * ny // 2, z, c)
+            for x in range(levs)
+            for c in range(nc)
+            for y in range(ny // 2)
+            for z in range(nz)
+        ]
         for h in range(2)
     ]
-    everyone = [[x * lat_count + b for b in range(lat_count) for x in range(levs)]]
+    everyone = [
+        [at(x, y, z, c) for x in range(levs) for c in range(nc) for y in range(ny) for z in range(nz)]
+    ]
     circles = lax.all_to_all(
         grid_values, ("lev", "lat"), 0, 0, axis_index_groups=halves, tiled=True
     )
-    circles = circles.reshape((levs, half_bands) + grid_values.shape[1:])
+    circles = circles.reshape((levs, nc, half_bands // nc) + grid_values.shape[1:])
 
     steps = 2
-    table = jnp.transpose(pair_table.reshape(levs, lat_count, slots), (1, 0, 2))
+    table = jnp.transpose(pair_table.reshape(levs, ny, nz, nc, slots), (0, 3, 1, 2, 4))
     table = table.reshape(steps, dev_count // steps, slots)
     other = top - table
     odd = table % 2 == 1
@@ -435,22 +449,18 @@
     wave_rows, quarter_rows, lane_index, south, me, pairs, rates = lax.optimization_barrier(
         (spread(waves), spread(quarters), lane_index, south[None], me, pairs, rates)
     )
+    basis, last = turn(jnp.transpose(basis_table, (1, 2, 0)))
     circle = circle_table(wave_rows, quarter_rows, lon_count, lon_count // 2)
     circle = circle.reshape(waves.shape + (lon_count // 2,))
     packed = fourier(south, circles, circle, lane_index, dev_count)
     received = lax.all_to_all(
         packed, ("lev", "lat"), 0, 0, axis_index_groups=everyone, tiled=True
-    ).reshape((lat_count, levs) + packed.shape[1:])
-    basis = jnp.transpose(basis_table, (1, 2, 0))
-    x, ready = gather(me, received, basis, CHUNKS[0])
+    ).reshape((levs, nc, ny, nz) + packed.shape[1:])
     parts = []
-    for c, (first, count) in enumerate(CHUNKS):
-        ahead = CHUNKS[c + 1] if c + 1 < len(CHUNKS) else None
+    for first, count in CHUNKS:
         norm = float(top * (top + 1))
-        outs = legendre(
-            first, ahead, pairs, x, ready, basis, rates, levs, lon_count, norm
-        )
-        ready = outs[-1]
+        x = gather(first, count, me, received, slots, lat_half)
+        outs = legendre(first, count, pairs, x, basis, last, rates, levs, lon_count, norm)
         moved = [outs[0]]
         for s in range(1, levs):
             to = [(i, (i + s) % levs) for i in range(levs)]
@@ -460,6 +470,7 @@
 
 
 CHUNKS = ((0, 2), (2, 3))
+LAT_AXES = (4, 4, 2)
 
 
 def solution(mesh):

time: 151 us -> 147 us (0.974)
  blocking collectives: 53.1 us -> 0 us
  waiting for transfers between devices: 36.9 us -> 74.1 us
  starting transfers between devices: 19.6 us -> 28.5 us
  local copies, waits for them, and re-layouts: 13 us -> 17.8 us
  Pallas kernels: 27.4 us -> 25.3 us
    all_to_all x1 -> x0, blocking collectives: 53.1 us -> none  [transform(): lax.all_to_all(packed, ('lev', 'lat'), 0, 0, axis_index_groups=everyone,...]
    all_to_all x0 -> x1, waiting for transfers between devices: none -> 33.8 us  [transform(): lax.all_to_all(packed, ('lev', 'lat'), 0, 0, axis_index_groups=everyone,...]
    all_to_all x0 -> x1, starting transfers between devices: none -> 8.97 us  [transform(): lax.all_to_all(packed, ('lev', 'lat'), 0, 0, axis_index_groups=everyone,...]
    unnamed x10 -> x14, local copies, waits for them, and re-layouts: 3.3 us -> 11.5 us
    pallas_call x2, Pallas kernels: 10.8 us -> 4.6 us  [legendre(): pl.pallas_call(functools.partial(legendre_kernel, 1.0 / lon_count, norm,...]
    all_to_all x1, waiting for transfers between devices: 21.9 us -> 26.8 us  [transform(): lax.all_to_all(grid_values, ('lev', 'lat'), 0, 0, axis_index_groups=halve...]
    pallas_call x1 -> x3, Pallas kernels: 2.36 us -> 6.34 us  [the longest x1 3.59 us: turn(): pl.pallas_call(turn_kernel, grid=(slots,), in_specs=[pl.BlockSpec((1, col...]
    ppermute x6, waiting for transfers between devices: 15.1 us -> 13.6 us  [transform(): moved.append(lax.ppermute(outs[s], 'lev', to))]
  transfers between devices with their start and end apart: 7 -> 8, of which waited for: 3 -> 4; matrix products, arithmetic and copies ran while one was open for 7% -> 4% of each run, Pallas kernels for 8% -> 8%
where the time goes in v4:
time: 147 us; the launch traced here: 146 us
  waiting for transfers between devices  74.1 us (50%)
  starting transfers between devices  28.5 us (19%)
  Pallas kernels  25.3 us (17%)
  local copies, waits for them, and re-layouts  17.8 us (12%)
    all_to_all x1, waiting for transfers between devices, transform(): lax.all_to_all(packed, ('lev', 'lat'), 0, 0, axis_index_groups=everyone,...  33.8 us
    all_to_all x1, waiting for transfers between devices, transform(): lax.all_to_all(grid_values, ('lev', 'lat'), 0, 0, axis_index_groups=halve...  26.8 us
    ppermute x6, waiting for transfers between devices, transform(): moved.append(lax.ppermute(outs[s], 'lev', to))  13.6 us
    unnamed x14, local copies, waits for them, and re-layouts  11.5 us
    all_to_all x1, starting transfers between devices, transform(): lax.all_to_all(grid_values, ('lev', 'lat'), 0, 0, axis_index_groups=halve...  10 us
    ppermute x6, starting transfers between devices, transform(): moved.append(lax.ppermute(outs[s], 'lev', to))  9.54 us
    all_to_all x1, starting transfers between devices, transform(): lax.all_to_all(packed, ('lev', 'lat'), 0, 0, axis_index_groups=everyone,...  8.97 us
    pallas_call x1, Pallas kernels, fourier(): pl.pallas_call(fourier_kernel, in_specs=[pl.BlockSpec(memory_space=pltpu....  7.88 us
  transfers between devices with their start and end apart: 8, of which 4 were waited for; matrix products, arithmetic and copies ran while one was open for 4% of the time, Pallas kernels for 8%

profile of v4, /device:TPU:0, one launch (start us, length us, event | category | flops | bytes accessed | tf_op | source)
XLA Modules:
  0.0 146.2 jit_solution(16204291088518241571)
XLA Ops:
  0.0 10.0 %all-to-all-start = ((bf16[64,40,640]{2,1,0:T(8,128)(2,1)}), bf16[64,40,640]{2,1,0:T(8,128)(2,1)S(1)}, u32[]{:S(2)}, u32[]{:S(2)}) async-start(bf16[64,40,640]{2,1,0:T(8,128)(2,1)} %param.4), calls=%async_computation | async-start | bytes 6553600 | tf_op jit(solution)/shard_map/all_to_all | solution.py:422
  10.1 0.0 copy-done.5
  10.1 0.2 reshape.25
  10.3 0.1 dynamic_slice.7.pairs_ref
  10.4 0.0 copy-done.6
  10.4 0.1 reshape.27
  10.5 0.1 broadcast_in_dim.58
  10.7 0.3 copy.7
  11.0 0.1 reshape.26
  11.2 0.1 copy.8
  11.3 0.1 copy.9
  11.4 0.9 broadcast_in_dim.47
  12.3 1.2 reshape_reshape.7
  13.5 0.9 broadcast_in_dim.46
  14.4 1.2 reshape_reshape.6
  15.6 0.1 add_bitcast_fusion
  15.8 0.1 broadcast_in_dim.59.rate_ref
  15.8 0.4 broadcast_in_dim.49.wave_ref
  16.3 0.4 broadcast_in_dim.52.quarter_ref
  16.7 5.2 %circle.1 = bf16[2560,1280]{1,0:T(8,128)(2,1)S(1)} custom-call(s32[2560,128]{1,0:T(8,128)S(1)} %broadcast_in_dim.49.wave_ref, s32[2560,128]{1,0:T(8,128)S(1)} %broadcast_in_dim.52.quarter_ref), custom_call_target="tpu_custom_call" | custom-call | flops 32768000 | bytes 6553600 | tf_op jit(solution)/shard_map/circle/pallas_call | solution.py:60
  21.8 2.7 %copy-done.3 = bf16[2560,1280]{1,0:T(8,128)(2,1)} copy-done((bf16[2560,1280]{1,0:T(8,128)(2,1)}, bf16[2560,1280]{1,0:T(8,128)(2,1)S(1)}, u32[]{:S(2)}) %copy-start.3) | copy-done | bytes 6553624
  24.5 26.8 %all-to-all-done = bf16[64,40,640]{2,1,0:T(8,128)(2,1)S(1)} async-done(((bf16[64,40,640]{2,1,0:T(8,128)(2,1)}), bf16[64,40,640]{2,1,0:T(8,128)(2,1)S(1)}, u32[]{:S(2)}, u32[]{:S(2)}) %all-to-all-start) | async-done | bytes 3276832 | tf_op jit(solution)/shard_map/all_to_all | solution.py:422
  51.3 7.9 %fourier.1 = bf16[128,104,128]{2,1,0:T(8,128)(2,1)S(1)} custom-call(s32[1]{0:T(128)} %bitcast.5.south_ref, bf16[4,2,8,40,640]{4,3,2,1,0:T(8,128)(2,1)S(1)} %bitcast.24, bf16[2,2,640,1280]{3,2,1,0:T(8,128)(2,1)} %bitcast.23, s32[8,128]{1,0:T(8,128)S(1)} %broadcast_in_dim.53.lane_ref), custom_call_target="tpu_custom_call" | custom-call | flops 4194304000 | bytes 13238272 | tf_op jit(solution)/shard_map/fourier/pallas_call | solution.py:162
  59.2 1.8 %copy-done.4 = bf16[128,104,128]{2,1,0:T(8,128)(2,1)} copy-done((bf16[128,104,128]{2,1,0:T(8,128)(2,1)}, bf16[128,104,128]{2,1,0:T(8,128)(2,1)S(1)}, u32[]{:S(2)}) %copy-start.4) | copy-done | bytes 3407896
  61.0 9.0 %all-to-all-start.1 = ((bf16[128,104,128]{2,1,0:T(8,128)(2,1)}), bf16[128,104,128]{2,1,0:T(8,128)(2,1)S(1)}, u32[]{:S(2)}, u32[]{:S(2)}) async-start(bf16[128,104,128]{2,1,0:T(8,128)(2,1)} %copy-done.4), calls=%async_computation.1 | async-start | bytes 6815744 | tf_op jit(solution)/shard_map/all_to_all | solution.py:456
  70.0 0.0 copy-start.2
  70.0 3.3 %copy-done.2 = bf16[640,5,1281]{0,2,1:T(8,128)(2,1)S(1)} copy-done((bf16[640,5,1281]{0,2,1:T(8,128)(2,1)S(1)}, bf16[640,5,1281]{0,2,1:T(8,128)(2,1)}, u32[]{:S(2)}) %copy-start.2) | copy-done | bytes 8198424
  73.3 3.6 %turn.1 = (bf16[5,640,1280]{2,1,0:T(8,128)(2,1)S(1)}, bf16[5,1,640]{2,1,0:T(2,128)(2,1)S(1)}) custom-call(bf16[5,1281,640]{2,1,0:T(8,128)(2,1)S(1)} %bitcast.22), custom_call_target="tpu_custom_call" | custom-call | flops 2098790400 | bytes 16396800 | tf_op jit(solution)/shard_map/turn/pallas_call | solution.py:246
  76.9 3.2 %copy-done = bf16[5,640,1280]{2,1,0:T(8,128)(2,1)} copy-done((bf16[5,640,1280]{2,1,0:T(8,128)(2,1)}, bf16[5,640,1280]{2,1,0:T(8,128)(2,1)S(1)}, u32[]{:S(2)}) %copy-start) | copy-done | bytes 8192024
  80.1 33.8 %all-to-all-done.1 = bf16[128,104,128]{2,1,0:T(8,128)(2,1)S(1)} async-done(((bf16[128,104,128]{2,1,0:T(8,128)(2,1)}), bf16[128,104,128]{2,1,0:T(8,128)(2,1)S(1)}, u32[]{:S(2)}, u32[]{:S(2)}) %all-to-all-start.1) | async-done | bytes 3407904 | tf_op jit(solution)/shard_map/all_to_all | solution.py:456
  113.9 1.2 gather.2.x_ref
  115.1 1.5 %gather.3.x_ref = bf16[3,2,2,5,128,128]{5,4,3,2,1,0:T(8,128)(2,1)S(1)} custom-call(s32[1]{0:T(128)} %bitcast.6.me_ref, bf16[4,2,4,4,104,128]{5,4,3,2,1,0:T(8,128)(2,1)S(1)} %bitcast.21), custom_call_target="tpu_custom_call" | custom-call | flops 34078720 | bytes 6815744 | tf_op jit(solution)/shard_map/gather/pallas_call | solution.py:271
  116.6 0.6 copy-done.1
  117.2 2.0 %legendre.2 = (bf16[2,32,1281]{2,1,0:T(8,128)(2,1)S(1)}, bf16[2,32,1281]{2,1,0:T(8,128)(2,1)S(1)}, bf16[2,32,1281]{2,1,0:T(8,128)(2,1)S(1)}, bf16[2,32,1281]{2,1,0:T(8,128)(2,1)S(1)}) custom-call(s32[5]{0:T(128)S(1)} %dynamic_slice.7.pairs_ref, bf16[2,2,2,5,128,128]{5,4,3,2,1,0:T(8,128)(2,1)S(1)} %gather.2.x_ref, bf16[5,640,1280]{2,1,0:T(8,128)(2,1)S(1)} %copy-done.1, ...), custom_call_target="tpu_custom_call" | custom-call | flops 839516160 | bytes 3935232 | tf_op jit(solution)/shard_map/legendre/pallas_call | solution.py:346
  119.2 0.3 collective-permute-start
  119.4 2.6 %legendre.3 = (bf16[3,32,1281]{2,1,0:T(8,128)(2,1)S(1)}, bf16[3,32,1281]{2,1,0:T(8,128)(2,1)S(1)}, bf16[3,32,1281]{2,1,0:T(8,128)(2,1)S(1)}, bf16[3,32,1281]{2,1,0:T(8,128)(2,1)S(1)}) custom-call(s32[5]{0:T(128)S(1)} %dynamic_slice.7.pairs_ref, bf16[3,2,2,5,128,128]{5,4,3,2,1,0:T(8,128)(2,1)S(1)} %gather.3.x_ref, bf16[5,640,1280]{2,1,0:T(8,128)(2,1)S(1)} %copy-done.1, ...), custom_call_target="tpu_custom_call" | custom-call | flops 1259274240 | bytes 5902848 | tf_op jit(solution)/shard_map/legendre/pallas_call | solution.py:346
  122.1 2.0 %collective-permute-start.3 = (bf16[3,32,1281]{2,1,0:T(8,128)(2,1)S(1)}, bf16[3,32,1281]{2,1,0:T(8,128)(2,1)S(1)}, u32[]{:S(2)}, u32[]{:S(2)}) collective-permute-start(bf16[3,32,1281]{2,1,0:T(8,128)(2,1)S(1)} %get-tuple-element.36), channel_id=1, source_target_pairs={{0,32},{32,64},{64,96},{96,0},{1,33},{33,65},{65,97},{97,1},{2,34}... | collective-permute-start | bytes 737864 | tf_op jit(solution)/shard_map/ppermute | solution.py:467
  124.1 2.6 %collective-permute-start.4 = (bf16[3,32,1281]{2,1,0:T(8,128)(2,1)S(1)}, bf16[3,32,1281]{2,1,0:T(8,128)(2,1)S(1)}, u32[]{:S(2)}, u32[]{:S(2)}) collective-permute-start(bf16[3,32,1281]{2,1,0:T(8,128)(2,1)S(1)} %get-tuple-element.37), channel_id=1, source_target_pairs={{0,64},{32,96},{64,0},{96,32},{1,65},{33,97},{65,1},{97,33},{2,66}... | collective-permute-start | bytes 737864 | tf_op jit(solution)/shard_map/ppermute | solution.py:467
  126.7 2.3 %collective-permute-start.5 = (bf16[3,32,1281]{2,1,0:T(8,128)(2,1)S(1)}, bf16[3,32,1281]{2,1,0:T(8,128)(2,1)S(1)}, u32[]{:S(2)}, u32[]{:S(2)}) collective-permute-start(bf16[3,32,1281]{2,1,0:T(8,128)(2,1)S(1)} %get-tuple-element.38), channel_id=1, source_target_pairs={{0,96},{32,0},{64,32},{96,64},{1,97},{33,1},{65,33},{97,65},{2,98}... | collective-permute-start | bytes 737864 | tf_op jit(solution)/shard_map/ppermute | solution.py:467
  129.0 0.0 collective-permute-start.1
  129.0 0.0 collective-permute-done.refs_1_
  129.0 2.4 %collective-permute-start.2 = (bf16[2,32,1281]{2,1,0:T(8,128)(2,1)S(1)}, bf16[2,32,1281]{2,1,0:T(8,128)(2,1)S(1)}, u32[]{:S(2)}, u32[]{:S(2)}) collective-permute-start(bf16[2,32,1281]{2,1,0:T(8,128)(2,1)S(1)} %get-tuple-element.34), channel_id=1, source_target_pairs={{0,96},{32,0},{64,32},{96,64},{1,97},{33,1},{65,33},{97,65},{2,98}... | collective-permute-start | bytes 491912 | tf_op jit(solution)/shard_map/ppermute | solution.py:467
  131.4 11.2 %collective-permute-done.1.refs_2_ = bf16[2,32,1281]{2,1,0:T(8,128)(2,1)S(1)} collective-permute-done((bf16[2,32,1281]{2,1,0:T(8,128)(2,1)S(1)}, bf16[2,32,1281]{2,1,0:T(8,128)(2,1)S(1)}, u32[]{:S(2)}, u32[]{:S(2)}) %collective-permute-start.1) | collective-permute-done | bytes 164000 | tf_op jit(solution)/shard_map/ppermute | solution.py:467
  142.6 2.3 %collective-permute-done.2.refs_3_ = bf16[2,32,1281]{2,1,0:T(8,128)(2,1)S(1)} collective-permute-done((bf16[2,32,1281]{2,1,0:T(8,128)(2,1)S(1)}, bf16[2,32,1281]{2,1,0:T(8,128)(2,1)S(1)}, u32[]{:S(2)}, u32[]{:S(2)}) %collective-permute-start.2) | collective-permute-done | bytes 164000 | tf_op jit(solution)/shard_map/ppermute | solution.py:467
  144.9 0.0 collective-permute-done.3.refs_5_
  144.9 0.0 collective-permute-done.4.refs_6_
  144.9 0.0 collective-permute-done.5.refs_7_
  144.9 1.3 assemble.1
  (23 shorter events, 0.1 us)
Async XLA Ops:
  0.0 10.1 %copy-start.5 = (s32[640]{0:T(1024)S(1)}, s32[640]{0:T(1024)}, u32[]{:S(2)}) copy-start(s32[640]{0:T(1024)} %param.7) | copy-start | bytes 7684
  0.0 10.4 %copy-start.6 = (f32[64]{0:T(128)S(1)}, f32[64]{0:T(128)}, u32[]{:S(2)}) copy-start(f32[64]{0:T(128)} %param.6) | copy-start | bytes 772
  0.0 51.3 %all-to-all-start = ((bf16[64,40,640]{2,1,0:T(8,128)(2,1)}), bf16[64,40,640]{2,1,0:T(8,128)(2,1)S(1)}, u32[]{:S(2)}, u32[]{:S(2)}) async-start(bf16[64,40,640]{2,1,0:T(8,128)(2,1)} %param.4), calls=%async_computation | async-start | bytes 6553600 | tf_op jit(solution)/shard_map/all_to_all | solution.py:422
  21.8 2.7 %copy-start.3 = (bf16[2560,1280]{1,0:T(8,128)(2,1)}, bf16[2560,1280]{1,0:T(8,128)(2,1)S(1)}, u32[]{:S(2)}) copy-start(bf16[2560,1280]{1,0:T(8,128)(2,1)S(1)} %circle.1) | copy-start | bytes 19660804
  59.2 1.8 %copy-start.4 = (bf16[128,104,128]{2,1,0:T(8,128)(2,1)}, bf16[128,104,128]{2,1,0:T(8,128)(2,1)S(1)}, u32[]{:S(2)}) copy-start(bf16[128,104,128]{2,1,0:T(8,128)(2,1)S(1)} %fourier.1) | copy-start | bytes 10223620
  61.0 52.9 %all-to-all-start.1 = ((bf16[128,104,128]{2,1,0:T(8,128)(2,1)}), bf16[128,104,128]{2,1,0:T(8,128)(2,1)S(1)}, u32[]{:S(2)}, u32[]{:S(2)}) async-start(bf16[128,104,128]{2,1,0:T(8,128)(2,1)} %copy-done.4), calls=%async_computation.1 | async-start | bytes 6815744 | tf_op jit(solution)/shard_map/all_to_all | solution.py:456
  70.0 3.3 %copy-start.2 = (bf16[640,5,1281]{0,2,1:T(8,128)(2,1)S(1)}, bf16[640,5,1281]{0,2,1:T(8,128)(2,1)}, u32[]{:S(2)}) copy-start(bf16[640,5,1281]{0,2,1:T(8,128)(2,1)} %param.5) | copy-start | bytes 24595204
  76.9 3.2 %copy-start = (bf16[5,640,1280]{2,1,0:T(8,128)(2,1)}, bf16[5,640,1280]{2,1,0:T(8,128)(2,1)S(1)}, u32[]{:S(2)}) copy-start(bf16[5,640,1280]{2,1,0:T(8,128)(2,1)S(1)} %get-tuple-element.28.basis_ref) | copy-start | bytes 24576004
  113.9 3.3 %copy-start.1 = (bf16[5,640,1280]{2,1,0:T(8,128)(2,1)S(1)}, bf16[5,640,1280]{2,1,0:T(8,128)(2,1)}, u32[]{:S(2)}) copy-start(bf16[5,640,1280]{2,1,0:T(8,128)(2,1)} %copy-done) | copy-start | bytes 24576004
  119.2 9.8 %collective-permute-start = (bf16[2,32,1281]{2,1,0:T(8,128)(2,1)S(1)}, bf16[2,32,1281]{2,1,0:T(8,128)(2,1)S(1)}, u32[]{:S(2)}, u32[]{:S(2)}) collective-permute-start(bf16[2,32,1281]{2,1,0:T(8,128)(2,1)S(1)} %get-tuple-element.32), channel_id=1, source_target_pairs={{0,32},{32,64},{64,96},{96,0},{1,33},{33,65},{65,97},{97,1},{2,34}... | collective-permute-start | bytes 491912 | tf_op jit(solution)/shard_map/ppermute | solution.py:467
  122.1 22.8 %collective-permute-start.3 = (bf16[3,32,1281]{2,1,0:T(8,128)(2,1)S(1)}, bf16[3,32,1281]{2,1,0:T(8,128)(2,1)S(1)}, u32[]{:S(2)}, u32[]{:S(2)}) collective-permute-start(bf16[3,32,1281]{2,1,0:T(8,128)(2,1)S(1)} %get-tuple-element.36), channel_id=1, source_target_pairs={{0,32},{32,64},{64,96},{96,0},{1,33},{33,65},{65,97},{97,1},{2,34}... | collective-permute-start | bytes 737864 | tf_op jit(solution)/shard_map/ppermute | solution.py:467
  124.1 20.8 %collective-permute-start.4 = (bf16[3,32,1281]{2,1,0:T(8,128)(2,1)S(1)}, bf16[3,32,1281]{2,1,0:T(8,128)(2,1)S(1)}, u32[]{:S(2)}, u32[]{:S(2)}) collective-permute-start(bf16[3,32,1281]{2,1,0:T(8,128)(2,1)S(1)} %get-tuple-element.37), channel_id=1, source_target_pairs={{0,64},{32,96},{64,0},{96,32},{1,65},{33,97},{65,1},{97,33},{2,66}... | collective-permute-start | bytes 737864 | tf_op jit(solution)/shard_map/ppermute | solution.py:467
  126.7 18.3 %collective-permute-start.5 = (bf16[3,32,1281]{2,1,0:T(8,128)(2,1)S(1)}, bf16[3,32,1281]{2,1,0:T(8,128)(2,1)S(1)}, u32[]{:S(2)}, u32[]{:S(2)}) collective-permute-start(bf16[3,32,1281]{2,1,0:T(8,128)(2,1)S(1)} %get-tuple-element.38), channel_id=1, source_target_pairs={{0,96},{32,0},{64,32},{96,64},{1,97},{33,1},{65,33},{97,65},{2,98}... | collective-permute-start | bytes 737864 | tf_op jit(solution)/shard_map/ppermute | solution.py:467
  129.0 13.6 %collective-permute-start.1 = (bf16[2,32,1281]{2,1,0:T(8,128)(2,1)S(1)}, bf16[2,32,1281]{2,1,0:T(8,128)(2,1)S(1)}, u32[]{:S(2)}, u32[]{:S(2)}) collective-permute-start(bf16[2,32,1281]{2,1,0:T(8,128)(2,1)S(1)} %get-tuple-element.33), channel_id=1, source_target_pairs={{0,64},{32,96},{64,0},{96,32},{1,65},{33,97},{65,1},{97,33},{2,66}... | collective-permute-start | bytes 491912 | tf_op jit(solution)/shard_map/ppermute | solution.py:467
  129.0 15.9 %collective-permute-start.2 = (bf16[2,32,1281]{2,1,0:T(8,128)(2,1)S(1)}, bf16[2,32,1281]{2,1,0:T(8,128)(2,1)S(1)}, u32[]{:S(2)}, u32[]{:S(2)}) collective-permute-start(bf16[2,32,1281]{2,1,0:T(8,128)(2,1)S(1)} %get-tuple-element.34), channel_id=1, source_target_pairs={{0,96},{32,0},{64,32},{96,64},{1,97},{33,1},{65,33},{97,65},{2,98}... | collective-permute-start | bytes 491912 | tf_op jit(solution)/shard_map/ppermute | solution.py:467

commit v5 on v4

--- a/solution.py
+++ b/solution.py
@@ -286,9 +286,10 @@
 
 
 def legendre_kernel(
-    scale, norm, first, count, pairs_ref, x_ref, basis_ref, last_ref, rate_ref, *out_refs
+    scale, norm, levs, first, count, pairs_ref, x_ref, basis_ref, last_ref, rate_ref, *refs
 ):
-    levs = len(out_refs)
+    out_refs, edge_refs = refs[-2 * levs : -levs], refs[-levs:]
+    before = refs[: -2 * levs]
     waves = basis_ref.shape[2]
     tiles, rows = x_ref.shape[3:5]
     part = rows // levs
@@ -331,23 +332,28 @@
         column = jnp.full((1, 1), waves, jnp.int32)
         left = side(first_kind, 1 - first_kind).astype(F32)
         final = jnp.sum(left * last_ref[k + first].astype(F32), axis=1, keepdims=True)
-        final = (final * damping(column, column >= bound)).astype(BF16)
-        for s in range(levs):
-            out_refs[s][k, :, waves:] = final[s * part : (s + 1) * part]
-
+        return final * damping(column, column >= bound)
+
+    lane = lax.broadcasted_iota(jnp.int32, (rows, LANES), 1)
+    edge = jnp.zeros((rows, LANES), F32)
+    if before:
+        edge = jnp.concatenate([b[...].astype(F32) for b in before], axis=0)
     for k in range(count):
-        slot_step(k)
-
-
-def legendre(first, count, pairs, x, basis, last, rates, levs, lon_count, norm):
+        edge = jnp.where(lane == k + first, slot_step(k), edge)
+    for s in range(levs):
+        edge_refs[s][...] = edge[s * part : (s + 1) * part].astype(BF16)
+
+
+def legendre(first, count, pairs, x, basis, last, rates, before, levs, lon_count, norm):
     _, lats, waves = basis.shape
-    cols = waves + 1
+    cols = waves
     part = x.shape[4] // levs
     return pl.pallas_call(
-        functools.partial(legendre_kernel, 1.0 / lon_count, norm, first, count),
-        in_specs=[pl.BlockSpec(memory_space=pltpu.SMEM)] + [VMEM_SPEC] * 4,
-        out_specs=[VMEM_SPEC] * levs,
-        out_shape=[jax.ShapeDtypeStruct((count, part, cols), BF16)] * levs,
+        functools.partial(legendre_kernel, 1.0 / lon_count, norm, levs, first, count),
+        in_specs=[pl.BlockSpec(memory_space=pltpu.SMEM)] + [VMEM_SPEC] * (4 + len(before)),
+        out_specs=[VMEM_SPEC] * (2 * levs),
+        out_shape=[jax.ShapeDtypeStruct((count, part, cols), BF16)] * levs
+        + [jax.ShapeDtypeStruct((part, LANES), BF16)] * levs,
         compiler_params=pltpu.CompilerParams(vmem_limit_bytes=LEGENDRE_VMEM),
         cost_estimate=pl.CostEstimate(
             flops=2 * count * cols * lats * 256,
@@ -355,39 +361,35 @@
             transcendentals=0,
         ),
         name="legendre",
-    )(pairs, x, basis, last, rates)
+    )(pairs, x, basis, last, rates, *before)
 
 
 def assemble_kernel(counts, me_ref, *refs):
-    levs = refs[-2].shape[1]
-    out_ref, sem = refs[-2:]
-    copies, low = [], 0
-    for c, count in enumerate(counts):
-        for s in range(levs):
-            lev = lax.rem(me_ref[0] - s + levs, levs)
-            n = c * levs + s
-            dest = out_ref.at[low : low + count, lev]
-            copies.append(pltpu.make_async_copy(refs[n], dest, sem.at[n]))
-        low += count
-    for copy in copies:
-        copy.start()
-    for copy in copies:
-        copy.wait()
-
-
-def assemble(me, parts):
-    levs = len(parts[0])
-    _, part, cols = parts[0][0].shape
+    out_ref = refs[-1]
+    slots, levs, _, cols = out_ref.shape
+    for s in range(levs):
+        lev = lax.rem(me_ref[0] - s + levs, levs)
+        low = 0
+        for c, count in enumerate(counts):
+            for k in range(count):
+                out_ref[low + k, lev, :, : cols - 1] = refs[c * levs + s][k]
+            low += count
+        edge = refs[len(counts) * levs + s][...]
+        for k in range(slots):
+            out_ref[k, lev, :, cols - 1 :] = edge[:, k : k + 1]
+
+
+def assemble(me, parts, edges):
+    levs = len(edges)
+    _, part, waves = parts[0][0].shape
     counts = [p[0].shape[0] for p in parts]
-    flat = [a for p in parts for a in p]
-    anywhere = pl.BlockSpec(memory_space=pl.ANY)
+    flat = [a for p in parts for a in p] + edges
     return pl.pallas_call(
         functools.partial(assemble_kernel, counts),
-        in_specs=[pl.BlockSpec(memory_space=pltpu.SMEM)] + [anywhere] * len(flat),
-        out_specs=anywhere,
-        scratch_shapes=[pltpu.SemaphoreType.DMA((len(flat),))],
-        out_shape=jax.ShapeDtypeStruct((sum(counts), levs, part, cols), BF16),
-        compiler_params=pltpu.CompilerParams(vmem_limit_bytes=1024 * 1024),
+        in_specs=[pl.BlockSpec(memory_space=pltpu.SMEM)] + [VMEM_SPEC] * len(flat),
+        out_specs=VMEM_SPEC,
+        out_shape=jax.ShapeDtypeStruct((sum(counts), levs, part, waves + 1), BF16),
+        compiler_params=pltpu.CompilerParams(vmem_limit_bytes=LEGENDRE_VMEM),
         name="assemble",
     )(me, *flat)
 
@@ -456,17 +458,20 @@
     received = lax.all_to_all(
         packed, ("lev", "lat"), 0, 0, axis_index_groups=everyone, tiled=True
     ).reshape((levs, nc, ny, nz) + packed.shape[1:])
-    parts = []
+    parts, edges = [], []
     for first, count in CHUNKS:
         norm = float(top * (top + 1))
         x = gather(first, count, me, received, slots, lat_half)
-        outs = legendre(first, count, pairs, x, basis, last, rates, levs, lon_count, norm)
+        outs = legendre(first, count, pairs, x, basis, last, rates, edges, levs, lon_count, norm)
+        edges = list(outs[levs:])
         moved = [outs[0]]
         for s in range(1, levs):
             to = [(i, (i + s) % levs) for i in range(levs)]
             moved.append(lax.ppermute(outs[s], "lev", to))
         parts.append(moved)
-    return assemble(me, parts).reshape(slots, levs, 2, group, cols)
+    for s in range(1, levs):
+        edges[s] = lax.ppermute(edges[s], "lev", [(i, (i + s) % levs) for i in range(levs)])
+    return assemble(me, parts, edges).reshape(slots, levs, 2, group, cols)
 
 
 CHUNKS = ((0, 2), (2, 3))

time: 147 us -> 156 us (1.061)
  starting transfers between devices: 28.5 us -> 36.9 us
    ppermute x0 -> x3, waiting for transfers between devices: none -> 8.65 us  [transform(): lax.ppermute(edges[s], 'lev', [(i, (i + s) % levs) for i in range(levs)])]
    ppermute x6, waiting for transfers between devices: 13.6 us -> 5.96 us  [transform(): moved.append(lax.ppermute(outs[s], 'lev', to))]
    ppermute x0 -> x3, starting transfers between devices: none -> 7.24 us  [transform(): lax.ppermute(edges[s], 'lev', [(i, (i + s) % levs) for i in range(levs)])]
  transfers between devices with their start and end apart: 8 -> 11, of which waited for: 4 -> 7; matrix products, arithmetic and copies ran while one was open for 4% -> 4% of each run, Pallas kernels for 8% -> 7%
where the time goes in v5:
time: 156 us
  waiting for transfers between devices  75.2 us (48%)
  starting transfers between devices  36.9 us (24%)
  Pallas kernels  25.4 us (16%)
  local copies, waits for them, and re-layouts  17.8 us (11%)
    all_to_all x1, waiting for transfers between devices, transform(): lax.all_to_all(packed, ('lev', 'lat'), 0, 0, axis_index_groups=everyone,...  33.8 us
    all_to_all x1, waiting for transfers between devices, transform(): lax.all_to_all(grid_values, ('lev', 'lat'), 0, 0, axis_index_groups=halve...  26.8 us
    unnamed x14, local copies, waits for them, and re-layouts  11.5 us
    ppermute x6, starting transfers between devices, transform(): moved.append(lax.ppermute(outs[s], 'lev', to))  10.7 us
    all_to_all x1, starting transfers between devices, transform(): lax.all_to_all(grid_values, ('lev', 'lat'), 0, 0, axis_index_groups=halve...  10 us
    all_to_all x1, starting transfers between devices, transform(): lax.all_to_all(packed, ('lev', 'lat'), 0, 0, axis_index_groups=everyone,...  8.97 us
    ppermute x3, waiting for transfers between devices, transform(): lax.ppermute(edges[s], 'lev', [(i, (i + s) % levs) for i in range(levs)])  8.65 us
    pallas_call x1, Pallas kernels, fourier(): pl.pallas_call(fourier_kernel, in_specs=[pl.BlockSpec(memory_space=pltpu....  7.88 us
  transfers between devices with their start and end apart: 11, of which 7 were waited for; matrix products, arithmetic and copies ran while one was open for 4% of the time, Pallas kernels for 7%

profile of v5, /device:TPU:0, one launch (start us, length us, event | category | flops | bytes accessed | tf_op | source)
XLA Modules:
  0.0 155.7 jit_solution(10786187528857403690)
XLA Ops:
  0.0 10.0 %all-to-all-start = ((bf16[64,40,640]{2,1,0:T(8,128)(2,1)}), bf16[64,40,640]{2,1,0:T(8,128)(2,1)S(1)}, u32[]{:S(2)}, u32[]{:S(2)}) async-start(bf16[64,40,640]{2,1,0:T(8,128)(2,1)} %param.4), calls=%async_computation | async-start | bytes 6553600 | tf_op jit(solution)/shard_map/all_to_all | solution.py:424
  10.1 0.2 reshape.25
  10.3 0.1 dynamic_slice.7.pairs_ref
  10.4 0.1 reshape.27
  10.5 0.1 broadcast_in_dim.58
  10.7 0.3 copy.7
  11.0 0.1 reshape.26
  11.2 0.1 copy.8
  11.3 0.1 copy.9
  11.4 0.9 broadcast_in_dim.47
  12.3 1.2 reshape_reshape.7
  13.5 0.9 broadcast_in_dim.46
  14.4 1.2 reshape_reshape.6
  15.6 0.1 add_bitcast_fusion
  15.8 0.1 broadcast_in_dim.59.rate_ref
  15.8 0.4 broadcast_in_dim.49.wave_ref
  16.3 0.4 broadcast_in_dim.52.quarter_ref
  16.7 5.2 %circle.1 = bf16[2560,1280]{1,0:T(8,128)(2,1)S(1)} custom-call(s32[2560,128]{1,0:T(8,128)S(1)} %broadcast_in_dim.49.wave_ref, s32[2560,128]{1,0:T(8,128)S(1)} %broadcast_in_dim.52.quarter_ref), custom_call_target="tpu_custom_call" | custom-call | flops 32768000 | bytes 6553600 | tf_op jit(solution)/shard_map/circle/pallas_call | solution.py:60
  21.8 2.7 %copy-done.3 = bf16[2560,1280]{1,0:T(8,128)(2,1)} copy-done((bf16[2560,1280]{1,0:T(8,128)(2,1)}, bf16[2560,1280]{1,0:T(8,128)(2,1)S(1)}, u32[]{:S(2)}) %copy-start.3) | copy-done | bytes 6553624
  24.6 26.8 %all-to-all-done = bf16[64,40,640]{2,1,0:T(8,128)(2,1)S(1)} async-done(((bf16[64,40,640]{2,1,0:T(8,128)(2,1)}), bf16[64,40,640]{2,1,0:T(8,128)(2,1)S(1)}, u32[]{:S(2)}, u32[]{:S(2)}) %all-to-all-start) | async-done | bytes 3276832 | tf_op jit(solution)/shard_map/all_to_all | solution.py:424
  51.3 7.9 %fourier.1 = bf16[128,104,128]{2,1,0:T(8,128)(2,1)S(1)} custom-call(s32[1]{0:T(128)} %bitcast.5.south_ref, bf16[4,2,8,40,640]{4,3,2,1,0:T(8,128)(2,1)S(1)} %bitcast.24, bf16[2,2,640,1280]{3,2,1,0:T(8,128)(2,1)} %bitcast.23, s32[8,128]{1,0:T(8,128)S(1)} %broadcast_in_dim.53.lane_ref), custom_call_target="tpu_custom_call" | custom-call | flops 4194304000 | bytes 13238272 | tf_op jit(solution)/shard_map/fourier/pallas_call | solution.py:162
  59.2 1.8 %copy-done.4 = bf16[128,104,128]{2,1,0:T(8,128)(2,1)} copy-done((bf16[128,104,128]{2,1,0:T(8,128)(2,1)}, bf16[128,104,128]{2,1,0:T(8,128)(2,1)S(1)}, u32[]{:S(2)}) %copy-start.4) | copy-done | bytes 3407896
  61.0 9.0 %all-to-all-start.1 = ((bf16[128,104,128]{2,1,0:T(8,128)(2,1)}), bf16[128,104,128]{2,1,0:T(8,128)(2,1)S(1)}, u32[]{:S(2)}, u32[]{:S(2)}) async-start(bf16[128,104,128]{2,1,0:T(8,128)(2,1)} %copy-done.4), calls=%async_computation.1 | async-start | bytes 6815744 | tf_op jit(solution)/shard_map/all_to_all | solution.py:458
  69.9 0.0 copy-start.2
  70.0 3.3 %copy-done.2 = bf16[640,5,1281]{0,2,1:T(8,128)(2,1)S(1)} copy-done((bf16[640,5,1281]{0,2,1:T(8,128)(2,1)S(1)}, bf16[640,5,1281]{0,2,1:T(8,128)(2,1)}, u32[]{:S(2)}) %copy-start.2) | copy-done | bytes 8198424
  73.3 3.6 %turn.1 = (bf16[5,640,1280]{2,1,0:T(8,128)(2,1)S(1)}, bf16[5,1,640]{2,1,0:T(2,128)(2,1)S(1)}) custom-call(bf16[5,1281,640]{2,1,0:T(8,128)(2,1)S(1)} %bitcast.22), custom_call_target="tpu_custom_call" | custom-call | flops 2098790400 | bytes 16396800 | tf_op jit(solution)/shard_map/turn/pallas_call | solution.py:246
  76.9 3.1 %copy-done = bf16[5,640,1280]{2,1,0:T(8,128)(2,1)} copy-done((bf16[5,640,1280]{2,1,0:T(8,128)(2,1)}, bf16[5,640,1280]{2,1,0:T(8,128)(2,1)S(1)}, u32[]{:S(2)}) %copy-start) | copy-done | bytes 8192024
  80.0 33.8 %all-to-all-done.1 = bf16[128,104,128]{2,1,0:T(8,128)(2,1)S(1)} async-done(((bf16[128,104,128]{2,1,0:T(8,128)(2,1)}), bf16[128,104,128]{2,1,0:T(8,128)(2,1)S(1)}, u32[]{:S(2)}, u32[]{:S(2)}) %all-to-all-start.1) | async-done | bytes 3407904 | tf_op jit(solution)/shard_map/all_to_all | solution.py:458
  113.9 1.2 gather.2.x_ref
  115.1 1.5 gather.3.x_ref
  116.6 0.6 copy-done.1
  117.2 2.0 %legendre.2 = (bf16[2,32,1280]{2,1,0:T(8,128)(2,1)S(1)}, bf16[2,32,1280]{2,1,0:T(8,128)(2,1)S(1)}, bf16[2,32,1280]{2,1,0:T(8,128)(2,1)S(1)}, bf16[2,32,1280]{2,1...) custom-call(s32[5]{0:T(128)S(1)} %dynamic_slice.7.pairs_ref, ...), custom_call_target="tpu_custom_call" | custom-call | flops 838860800 | bytes 3932160 | tf_op jit(solution)/shard_map/legendre/pallas_call | solution.py:351
  119.2 0.3 collective-permute-start
  119.4 2.6 %legendre.3 = (bf16[3,32,1280]{2,1,0:T(8,128)(2,1)S(1)}, bf16[3,32,1280]{2,1,0:T(8,128)(2,1)S(1)}, bf16[3,32,1280]{2,1,0:T(8,128)(2,1)S(1)}, bf16[3,32,1280]{2,1...) custom-call(s32[5]{0:T(128)S(1)} %dynamic_slice.7.pairs_ref, ...), custom_call_target="tpu_custom_call" | custom-call | flops 1258291200 | bytes 5898240 | tf_op jit(solution)/shard_map/legendre/pallas_call | solution.py:351
  122.0 2.0 %collective-permute-start.3 = (bf16[3,32,1280]{2,1,0:T(8,128)(2,1)S(1)}, bf16[3,32,1280]{2,1,0:T(8,128)(2,1)S(1)}, u32[]{:S(2)}, u32[]{:S(2)}) collective-permute-start(bf16[3,32,1280]{2,1,0:T(8,128)(2,1)S(1)} %get-tuple-element.48), channel_id=1, source_target_pairs={{0,32},{32,64},{64,96},{96,0},{1,33},{33,65},{65,97},{97,1},{2,34}... | collective-permute-start | bytes 737288 | tf_op jit(solution)/shard_map/ppermute | solution.py:470
  124.1 2.6 %collective-permute-start.4 = (bf16[3,32,1280]{2,1,0:T(8,128)(2,1)S(1)}, bf16[3,32,1280]{2,1,0:T(8,128)(2,1)S(1)}, u32[]{:S(2)}, u32[]{:S(2)}) collective-permute-start(bf16[3,32,1280]{2,1,0:T(8,128)(2,1)S(1)} %get-tuple-element.49), channel_id=1, source_target_pairs={{0,64},{32,96},{64,0},{96,32},{1,65},{33,97},{65,1},{97,33},{2,66}... | collective-permute-start | bytes 737288 | tf_op jit(solution)/shard_map/ppermute | solution.py:470
  126.6 2.3 %collective-permute-start.5 = (bf16[3,32,1280]{2,1,0:T(8,128)(2,1)S(1)}, bf16[3,32,1280]{2,1,0:T(8,128)(2,1)S(1)}, u32[]{:S(2)}, u32[]{:S(2)}) collective-permute-start(bf16[3,32,1280]{2,1,0:T(8,128)(2,1)S(1)} %get-tuple-element.50), channel_id=1, source_target_pairs={{0,96},{32,0},{64,32},{96,64},{1,97},{33,1},{65,33},{97,65},{2,98}... | collective-permute-start | bytes 737288 | tf_op jit(solution)/shard_map/ppermute | solution.py:470
  128.9 0.0 collective-permute-start.6
  129.0 5.7 %collective-permute-done.6.refs_9_ = bf16[32,128]{1,0:T(8,128)(2,1)S(1)} collective-permute-done((bf16[32,128]{1,0:T(8,128)(2,1)S(1)}, bf16[32,128]{1,0:T(8,128)(2,1)S(1)}, u32[]{:S(2)}, u32[]{:S(2)}) %collective-permute-start.6) | collective-permute-done | bytes 8224 | tf_op jit(solution)/shard_map/ppermute | solution.py:473
  134.6 3.7 %collective-permute-start.7 = (bf16[32,128]{1,0:T(8,128)(2,1)S(1)}, bf16[32,128]{1,0:T(8,128)(2,1)S(1)}, u32[]{:S(2)}, u32[]{:S(2)}) collective-permute-start(bf16[32,128]{1,0:T(8,128)(2,1)S(1)} %get-tuple-element.53), channel_id=1, source_target_pairs={{0,64},{32,96},{64,0},{96,32},{1,65},{33,97},{65,1},{97,33},{2,66}... | collective-permute-start | bytes 24584 | tf_op jit(solution)/shard_map/ppermute | solution.py:473
  138.3 1.6 %collective-permute-done.7.refs_10_ = bf16[32,128]{1,0:T(8,128)(2,1)S(1)} collective-permute-done((bf16[32,128]{1,0:T(8,128)(2,1)S(1)}, bf16[32,128]{1,0:T(8,128)(2,1)S(1)}, u32[]{:S(2)}, u32[]{:S(2)}) %collective-permute-start.7) | collective-permute-done | bytes 8224 | tf_op jit(solution)/shard_map/ppermute | solution.py:473
  139.9 3.5 %collective-permute-start.8 = (bf16[32,128]{1,0:T(8,128)(2,1)S(1)}, bf16[32,128]{1,0:T(8,128)(2,1)S(1)}, u32[]{:S(2)}, u32[]{:S(2)}) collective-permute-start(bf16[32,128]{1,0:T(8,128)(2,1)S(1)} %get-tuple-element.54), channel_id=1, source_target_pairs={{0,96},{32,0},{64,32},{96,64},{1,97},{33,1},{65,33},{97,65},{2,98}... | collective-permute-start | bytes 24584 | tf_op jit(solution)/shard_map/ppermute | solution.py:473
  143.5 1.4 collective-permute-done.8.refs_11_
  144.8 2.3 %collective-permute-start.1 = (bf16[2,32,1280]{2,1,0:T(8,128)(2,1)S(1)}, bf16[2,32,1280]{2,1,0:T(8,128)(2,1)S(1)}, u32[]{:S(2)}, u32[]{:S(2)}) collective-permute-start(bf16[2,32,1280]{2,1,0:T(8,128)(2,1)S(1)} %get-tuple-element.41), channel_id=1, source_target_pairs={{0,64},{32,96},{64,0},{96,32},{1,65},{33,97},{65,1},{97,33},{2,66}... | collective-permute-start | bytes 491528 | tf_op jit(solution)/shard_map/ppermute | solution.py:470
  147.1 1.2 collective-permute-start.2
  148.3 3.3 %collective-permute-done.1.refs_2_ = bf16[2,32,1280]{2,1,0:T(8,128)(2,1)S(1)} collective-permute-done((bf16[2,32,1280]{2,1,0:T(8,128)(2,1)S(1)}, bf16[2,32,1280]{2,1,0:T(8,128)(2,1)S(1)}, u32[]{:S(2)}, u32[]{:S(2)}) %collective-permute-start.1) | collective-permute-done | bytes 163872 | tf_op jit(solution)/shard_map/ppermute | solution.py:470
  151.7 2.6 %collective-permute-done.2.refs_3_ = bf16[2,32,1280]{2,1,0:T(8,128)(2,1)S(1)} collective-permute-done((bf16[2,32,1280]{2,1,0:T(8,128)(2,1)S(1)}, bf16[2,32,1280]{2,1,0:T(8,128)(2,1)S(1)}, u32[]{:S(2)}, u32[]{:S(2)}) %collective-permute-start.2) | collective-permute-done | bytes 163872 | tf_op jit(solution)/shard_map/ppermute | solution.py:470
  154.3 1.4 assemble.1
  (29 shorter events, 0.1 us)
Async XLA Ops:
  0.0 10.1 %copy-start.5 = (s32[640]{0:T(1024)S(1)}, s32[640]{0:T(1024)}, u32[]{:S(2)}) copy-start(s32[640]{0:T(1024)} %param.7) | copy-start | bytes 7684
  0.0 10.4 %copy-start.6 = (f32[64]{0:T(128)S(1)}, f32[64]{0:T(128)}, u32[]{:S(2)}) copy-start(f32[64]{0:T(128)} %param.6) | copy-start | bytes 772
  0.0 51.3 %all-to-all-start = ((bf16[64,40,640]{2,1,0:T(8,128)(2,1)}), bf16[64,40,640]{2,1,0:T(8,128)(2,1)S(1)}, u32[]{:S(2)}, u32[]{:S(2)}) async-start(bf16[64,40,640]{2,1,0:T(8,128)(2,1)} %param.4), calls=%async_computation | async-start | bytes 6553600 | tf_op jit(solution)/shard_map/all_to_all | solution.py:424
  21.8 2.7 %copy-start.3 = (bf16[2560,1280]{1,0:T(8,128)(2,1)}, bf16[2560,1280]{1,0:T(8,128)(2,1)S(1)}, u32[]{:S(2)}) copy-start(bf16[2560,1280]{1,0:T(8,128)(2,1)S(1)} %circle.1) | copy-start | bytes 19660804
  59.2 1.8 %copy-start.4 = (bf16[128,104,128]{2,1,0:T(8,128)(2,1)}, bf16[128,104,128]{2,1,0:T(8,128)(2,1)S(1)}, u32[]{:S(2)}) copy-start(bf16[128,104,128]{2,1,0:T(8,128)(2,1)S(1)} %fourier.1) | copy-start | bytes 10223620
  61.0 52.9 %all-to-all-start.1 = ((bf16[128,104,128]{2,1,0:T(8,128)(2,1)}), bf16[128,104,128]{2,1,0:T(8,128)(2,1)S(1)}, u32[]{:S(2)}, u32[]{:S(2)}) async-start(bf16[128,104,128]{2,1,0:T(8,128)(2,1)} %copy-done.4), calls=%async_computation.1 | async-start | bytes 6815744 | tf_op jit(solution)/shard_map/all_to_all | solution.py:458
  69.9 3.3 %copy-start.2 = (bf16[640,5,1281]{0,2,1:T(8,128)(2,1)S(1)}, bf16[640,5,1281]{0,2,1:T(8,128)(2,1)}, u32[]{:S(2)}) copy-start(bf16[640,5,1281]{0,2,1:T(8,128)(2,1)} %param.5) | copy-start | bytes 24595204
  76.9 3.2 %copy-start = (bf16[5,640,1280]{2,1,0:T(8,128)(2,1)}, bf16[5,640,1280]{2,1,0:T(8,128)(2,1)S(1)}, u32[]{:S(2)}) copy-start(bf16[5,640,1280]{2,1,0:T(8,128)(2,1)S(1)} %get-tuple-element.36.basis_ref) | copy-start | bytes 24576004
  113.9 3.3 %copy-start.1 = (bf16[5,640,1280]{2,1,0:T(8,128)(2,1)S(1)}, bf16[5,640,1280]{2,1,0:T(8,128)(2,1)}, u32[]{:S(2)}) copy-start(bf16[5,640,1280]{2,1,0:T(8,128)(2,1)} %copy-done) | copy-start | bytes 24576004
  119.2 27.9 %collective-permute-start = (bf16[2,32,1280]{2,1,0:T(8,128)(2,1)S(1)}, bf16[2,32,1280]{2,1,0:T(8,128)(2,1)S(1)}, u32[]{:S(2)}, u32[]{:S(2)}) collective-permute-start(bf16[2,32,1280]{2,1,0:T(8,128)(2,1)S(1)} %get-tuple-element.40), channel_id=1, source_target_pairs={{0,32},{32,64},{64,96},{96,0},{1,33},{33,65},{65,97},{97,1},{2,34}... | collective-permute-start | bytes 491528 | tf_op jit(solution)/shard_map/ppermute | solution.py:470
  122.0 32.2 %collective-permute-start.3 = (bf16[3,32,1280]{2,1,0:T(8,128)(2,1)S(1)}, bf16[3,32,1280]{2,1,0:T(8,128)(2,1)S(1)}, u32[]{:S(2)}, u32[]{:S(2)}) collective-permute-start(bf16[3,32,1280]{2,1,0:T(8,128)(2,1)S(1)} %get-tuple-element.48), channel_id=1, source_target_pairs={{0,32},{32,64},{64,96},{96,0},{1,33},{33,65},{65,97},{97,1},{2,34}... | collective-permute-start | bytes 737288 | tf_op jit(solution)/shard_map/ppermute | solution.py:470
  124.1 30.2 %collective-permute-start.4 = (bf16[3,32,1280]{2,1,0:T(8,128)(2,1)S(1)}, bf16[3,32,1280]{2,1,0:T(8,128)(2,1)S(1)}, u32[]{:S(2)}, u32[]{:S(2)}) collective-permute-start(bf16[3,32,1280]{2,1,0:T(8,128)(2,1)S(1)} %get-tuple-element.49), channel_id=1, source_target_pairs={{0,64},{32,96},{64,0},{96,32},{1,65},{33,97},{65,1},{97,33},{2,66}... | collective-permute-start | bytes 737288 | tf_op jit(solution)/shard_map/ppermute | solution.py:470
  126.6 27.7 %collective-permute-start.5 = (bf16[3,32,1280]{2,1,0:T(8,128)(2,1)S(1)}, bf16[3,32,1280]{2,1,0:T(8,128)(2,1)S(1)}, u32[]{:S(2)}, u32[]{:S(2)}) collective-permute-start(bf16[3,32,1280]{2,1,0:T(8,128)(2,1)S(1)} %get-tuple-element.50), channel_id=1, source_target_pairs={{0,96},{32,0},{64,32},{96,64},{1,97},{33,1},{65,33},{97,65},{2,98}... | collective-permute-start | bytes 737288 | tf_op jit(solution)/shard_map/ppermute | solution.py:470
  128.9 5.7 %collective-permute-start.6 = (bf16[32,128]{1,0:T(8,128)(2,1)S(1)}, bf16[32,128]{1,0:T(8,128)(2,1)S(1)}, u32[]{:S(2)}, u32[]{:S(2)}) collective-permute-start(bf16[32,128]{1,0:T(8,128)(2,1)S(1)} %get-tuple-element.52), channel_id=1, source_target_pairs={{0,32},{32,64},{64,96},{96,0},{1,33},{33,65},{65,97},{97,1},{2,34}... | collective-permute-start | bytes 24584 | tf_op jit(solution)/shard_map/ppermute | solution.py:473
  134.6 5.3 %collective-permute-start.7 = (bf16[32,128]{1,0:T(8,128)(2,1)S(1)}, bf16[32,128]{1,0:T(8,128)(2,1)S(1)}, u32[]{:S(2)}, u32[]{:S(2)}) collective-permute-start(bf16[32,128]{1,0:T(8,128)(2,1)S(1)} %get-tuple-element.53), channel_id=1, source_target_pairs={{0,64},{32,96},{64,0},{96,32},{1,65},{33,97},{65,1},{97,33},{2,66}... | collective-permute-start | bytes 24584 | tf_op jit(solution)/shard_map/ppermute | solution.py:473
  139.9 4.9 %collective-permute-start.8 = (bf16[32,128]{1,0:T(8,128)(2,1)S(1)}, bf16[32,128]{1,0:T(8,128)(2,1)S(1)}, u32[]{:S(2)}, u32[]{:S(2)}) collective-permute-start(bf16[32,128]{1,0:T(8,128)(2,1)S(1)} %get-tuple-element.54), channel_id=1, source_target_pairs={{0,96},{32,0},{64,32},{96,64},{1,97},{33,1},{65,33},{97,65},{2,98}... | collective-permute-start | bytes 24584 | tf_op jit(solution)/shard_map/ppermute | solution.py:473
  144.8 6.8 %collective-permute-start.1 = (bf16[2,32,1280]{2,1,0:T(8,128)(2,1)S(1)}, bf16[2,32,1280]{2,1,0:T(8,128)(2,1)S(1)}, u32[]{:S(2)}, u32[]{:S(2)}) collective-permute-start(bf16[2,32,1280]{2,1,0:T(8,128)(2,1)S(1)} %get-tuple-element.41), channel_id=1, source_target_pairs={{0,64},{32,96},{64,0},{96,32},{1,65},{33,97},{65,1},{97,33},{2,66}... | collective-permute-start | bytes 491528 | tf_op jit(solution)/shard_map/ppermute | solution.py:470
  147.1 7.2 %collective-permute-start.2 = (bf16[2,32,1280]{2,1,0:T(8,128)(2,1)S(1)}, bf16[2,32,1280]{2,1,0:T(8,128)(2,1)S(1)}, u32[]{:S(2)}, u32[]{:S(2)}) collective-permute-start(bf16[2,32,1280]{2,1,0:T(8,128)(2,1)S(1)} %get-tuple-element.42), channel_id=1, source_target_pairs={{0,96},{32,0},{64,32},{96,64},{1,97},{33,1},{65,33},{97,65},{2,98}... | collective-permute-start | bytes 491528 | tf_op jit(solution)/shard_map/ppermute | solution.py:470

commit v6 on v5

--- a/solution.py
+++ b/solution.py
@@ -144,7 +144,7 @@
                         tail_ref[spot, :] = value[main + r * dests : main + (r + 1) * dests]
                 rows16 = pl.ds(pl.multiple_of(place * 16, 16), 16)
                 out_ref[span, rows16, :] = jnp.concatenate(both, axis=1).astype(BF16)
-        last = tail_ref[...].reshape(dests, end, LANES)
+        last = tail_ref[: dests * end].reshape(dests, end, LANES)
         out_ref[span, tiles * 16 :, :] = last.astype(BF16)
         return carry
 
@@ -166,7 +166,7 @@
         scratch_shapes=[
             pltpu.VMEM(circle.shape, BF16),
             pltpu.VMEM((2, lat_half, 2 * quarter), BF16),
-            pltpu.VMEM((dests * end, LANES), F32),
+            pltpu.VMEM((dests * end + 8 * end, LANES), F32),
             pltpu.SemaphoreType.DMA((steps,)),
         ],
         out_shape=jax.ShapeDtypeStruct((dev_count, rows, LANES), BF16),
@@ -198,8 +198,8 @@
         def sides(span, height, into):
             n = recv_ref[x, :, : ny // 2, :, span, :].astype(F32).reshape(group * height, LANES)
             s = recv_ref[x, :, ny // 2 :, :, span, :].astype(F32).reshape(group * height, LANES)
-            into[0] = n + s
-            into[1] = n - s
+            into[0, : group * height] = n + s
+            into[1, : group * height] = n - s
 
         def put(slot, kind, tile, r, from_ref, start, stride):
             dest = pl.ds(pl.multiple_of(base + r * group, 16), group)
@@ -273,8 +273,8 @@
         in_specs=[pl.BlockSpec(memory_space=pltpu.SMEM), VMEM_SPEC],
         out_specs=VMEM_SPEC,
         scratch_shapes=[
-            pltpu.VMEM((tiles, 2, group * 16, LANES), F32),
-            pltpu.VMEM((2, group * end, LANES), F32),
+            pltpu.VMEM((tiles, 2, group * 16 + 128, LANES), F32),
+            pltpu.VMEM((2, group * end + 8 * end, LANES), F32),
         ],
         out_shape=jax.ShapeDtypeStruct((count, 2, 2, tiles, levs * 2 * group, LANES), BF16),
         compiler_params=pltpu.CompilerParams(vmem_limit_bytes=LEGENDRE_VMEM),

time: 156 us -> 156 us (level)
  no operation moved by 1% of the time
where the time goes in v6:
time: 156 us
  waiting for transfers between devices  75.2 us (48%)
  starting transfers between devices  36.9 us (24%)
  Pallas kernels  25.4 us (16%)
  local copies, waits for them, and re-layouts  17.8 us (11%)
    all_to_all x1, waiting for transfers between devices, transform(): lax.all_to_all(packed, ('lev', 'lat'), 0, 0, axis_index_groups=everyone,...  33.8 us
    all_to_all x1, waiting for transfers between devices, transform(): lax.all_to_all(grid_values, ('lev', 'lat'), 0, 0, axis_index_groups=halve...  26.8 us
    unnamed x14, local copies, waits for them, and re-layouts  11.5 us
    ppermute x6, starting transfers between devices, transform(): moved.append(lax.ppermute(outs[s], 'lev', to))  10.7 us
    all_to_all x1, starting transfers between devices, transform(): lax.all_to_all(grid_values, ('lev', 'lat'), 0, 0, axis_index_groups=halve...  10 us
    all_to_all x1, starting transfers between devices, transform(): lax.all_to_all(packed, ('lev', 'lat'), 0, 0, axis_index_groups=everyone,...  8.97 us
    ppermute x3, waiting for transfers between devices, transform(): lax.ppermute(edges[s], 'lev', [(i, (i + s) % levs) for i in range(levs)])  8.65 us
    pallas_call x1, Pallas kernels, fourier(): pl.pallas_call(fourier_kernel, in_specs=[pl.BlockSpec(memory_space=pltpu....  7.88 us
  transfers between devices with their start and end apart: 11, of which 7 were waited for; matrix products, arithmetic and copies ran while one was open for 4% of the time, Pallas kernels for 7%

profile of v6, /device:TPU:0, one launch (start us, length us, event | category | flops | bytes accessed | tf_op | source)
XLA Modules:
  0.0 155.7 jit_solution(1146043524380109465)
XLA Ops:
  0.0 10.0 %all-to-all-start = ((bf16[64,40,640]{2,1,0:T(8,128)(2,1)}), bf16[64,40,640]{2,1,0:T(8,128)(2,1)S(1)}, u32[]{:S(2)}, u32[]{:S(2)}) async-start(bf16[64,40,640]{2,1,0:T(8,128)(2,1)} %param.4), calls=%async_computation | async-start | bytes 6553600 | tf_op jit(solution)/shard_map/all_to_all | solution.py:424
  10.1 0.2 reshape.25
  10.3 0.1 dynamic_slice.7.pairs_ref
  10.4 0.1 reshape.27
  10.5 0.1 broadcast_in_dim.58
  10.7 0.3 copy.7
  11.0 0.1 reshape.26
  11.2 0.1 copy.8
  11.3 0.1 copy.9
  11.4 0.9 broadcast_in_dim.47
  12.3 1.2 reshape_reshape.7
  13.5 0.9 broadcast_in_dim.46
  14.4 1.2 reshape_reshape.6
  15.6 0.1 add_bitcast_fusion
  15.8 0.1 broadcast_in_dim.59.rate_ref
  15.8 0.4 broadcast_in_dim.49.wave_ref
  16.3 0.4 broadcast_in_dim.52.quarter_ref
  16.7 5.2 %circle.1 = bf16[2560,1280]{1,0:T(8,128)(2,1)S(1)} custom-call(s32[2560,128]{1,0:T(8,128)S(1)} %broadcast_in_dim.49.wave_ref, s32[2560,128]{1,0:T(8,128)S(1)} %broadcast_in_dim.52.quarter_ref), custom_call_target="tpu_custom_call" | custom-call | flops 32768000 | bytes 6553600 | tf_op jit(solution)/shard_map/circle/pallas_call | solution.py:60
  21.8 2.7 %copy-done.3 = bf16[2560,1280]{1,0:T(8,128)(2,1)} copy-done((bf16[2560,1280]{1,0:T(8,128)(2,1)}, bf16[2560,1280]{1,0:T(8,128)(2,1)S(1)}, u32[]{:S(2)}) %copy-start.3) | copy-done | bytes 6553624
  24.6 26.8 %all-to-all-done = bf16[64,40,640]{2,1,0:T(8,128)(2,1)S(1)} async-done(((bf16[64,40,640]{2,1,0:T(8,128)(2,1)}), bf16[64,40,640]{2,1,0:T(8,128)(2,1)S(1)}, u32[]{:S(2)}, u32[]{:S(2)}) %all-to-all-start) | async-done | bytes 3276832 | tf_op jit(solution)/shard_map/all_to_all | solution.py:424
  51.3 7.9 %fourier.1 = bf16[128,104,128]{2,1,0:T(8,128)(2,1)S(1)} custom-call(s32[1]{0:T(128)} %bitcast.5.south_ref, bf16[4,2,8,40,640]{4,3,2,1,0:T(8,128)(2,1)S(1)} %bitcast.24, bf16[2,2,640,1280]{3,2,1,0:T(8,128)(2,1)} %bitcast.23, s32[8,128]{1,0:T(8,128)S(1)} %broadcast_in_dim.53.lane_ref), custom_call_target="tpu_custom_call" | custom-call | flops 4194304000 | bytes 13238272 | tf_op jit(solution)/shard_map/fourier/pallas_call | solution.py:162
  59.2 1.8 %copy-done.4 = bf16[128,104,128]{2,1,0:T(8,128)(2,1)} copy-done((bf16[128,104,128]{2,1,0:T(8,128)(2,1)}, bf16[128,104,128]{2,1,0:T(8,128)(2,1)S(1)}, u32[]{:S(2)}) %copy-start.4) | copy-done | bytes 3407896
  61.0 9.0 %all-to-all-start.1 = ((bf16[128,104,128]{2,1,0:T(8,128)(2,1)}), bf16[128,104,128]{2,1,0:T(8,128)(2,1)S(1)}, u32[]{:S(2)}, u32[]{:S(2)}) async-start(bf16[128,104,128]{2,1,0:T(8,128)(2,1)} %copy-done.4), calls=%async_computation.1 | async-start | bytes 6815744 | tf_op jit(solution)/shard_map/all_to_all | solution.py:458
  69.9 0.0 copy-start.2
  70.0 3.3 %copy-done.2 = bf16[640,5,1281]{0,2,1:T(8,128)(2,1)S(1)} copy-done((bf16[640,5,1281]{0,2,1:T(8,128)(2,1)S(1)}, bf16[640,5,1281]{0,2,1:T(8,128)(2,1)}, u32[]{:S(2)}) %copy-start.2) | copy-done | bytes 8198424
  73.3 3.6 %turn.1 = (bf16[5,640,1280]{2,1,0:T(8,128)(2,1)S(1)}, bf16[5,1,640]{2,1,0:T(2,128)(2,1)S(1)}) custom-call(bf16[5,1281,640]{2,1,0:T(8,128)(2,1)S(1)} %bitcast.22), custom_call_target="tpu_custom_call" | custom-call | flops 2098790400 | bytes 16396800 | tf_op jit(solution)/shard_map/turn/pallas_call | solution.py:246
  76.9 3.1 %copy-done = bf16[5,640,1280]{2,1,0:T(8,128)(2,1)} copy-done((bf16[5,640,1280]{2,1,0:T(8,128)(2,1)}, bf16[5,640,1280]{2,1,0:T(8,128)(2,1)S(1)}, u32[]{:S(2)}) %copy-start) | copy-done | bytes 8192024
  80.0 33.8 %all-to-all-done.1 = bf16[128,104,128]{2,1,0:T(8,128)(2,1)S(1)} async-done(((bf16[128,104,128]{2,1,0:T(8,128)(2,1)}), bf16[128,104,128]{2,1,0:T(8,128)(2,1)S(1)}, u32[]{:S(2)}, u32[]{:S(2)}) %all-to-all-start.1) | async-done | bytes 3407904 | tf_op jit(solution)/shard_map/all_to_all | solution.py:458
  113.9 1.2 gather.2.x_ref
  115.1 1.5 gather.3.x_ref
  116.6 0.6 copy-done.1
  117.2 2.0 %legendre.2 = (bf16[2,32,1280]{2,1,0:T(8,128)(2,1)S(1)}, bf16[2,32,1280]{2,1,0:T(8,128)(2,1)S(1)}, bf16[2,32,1280]{2,1,0:T(8,128)(2,1)S(1)}, bf16[2,32,1280]{2,1...) custom-call(s32[5]{0:T(128)S(1)} %dynamic_slice.7.pairs_ref, ...), custom_call_target="tpu_custom_call" | custom-call | flops 838860800 | bytes 3932160 | tf_op jit(solution)/shard_map/legendre/pallas_call | solution.py:351
  119.2 0.3 collective-permute-start
  119.4 2.6 %legendre.3 = (bf16[3,32,1280]{2,1,0:T(8,128)(2,1)S(1)}, bf16[3,32,1280]{2,1,0:T(8,128)(2,1)S(1)}, bf16[3,32,1280]{2,1,0:T(8,128)(2,1)S(1)}, bf16[3,32,1280]{2,1...) custom-call(s32[5]{0:T(128)S(1)} %dynamic_slice.7.pairs_ref, ...), custom_call_target="tpu_custom_call" | custom-call | flops 1258291200 | bytes 5898240 | tf_op jit(solution)/shard_map/legendre/pallas_call | solution.py:351
  122.0 2.0 %collective-permute-start.3 = (bf16[3,32,1280]{2,1,0:T(8,128)(2,1)S(1)}, bf16[3,32,1280]{2,1,0:T(8,128)(2,1)S(1)}, u32[]{:S(2)}, u32[]{:S(2)}) collective-permute-start(bf16[3,32,1280]{2,1,0:T(8,128)(2,1)S(1)} %get-tuple-element.48), channel_id=1, source_target_pairs={{0,32},{32,64},{64,96},{96,0},{1,33},{33,65},{65,97},{97,1},{2,34}... | collective-permute-start | bytes 737288 | tf_op jit(solution)/shard_map/ppermute | solution.py:470
  124.1 2.6 %collective-permute-start.4 = (bf16[3,32,1280]{2,1,0:T(8,128)(2,1)S(1)}, bf16[3,32,1280]{2,1,0:T(8,128)(2,1)S(1)}, u32[]{:S(2)}, u32[]{:S(2)}) collective-permute-start(bf16[3,32,1280]{2,1,0:T(8,128)(2,1)S(1)} %get-tuple-element.49), channel_id=1, source_target_pairs={{0,64},{32,96},{64,0},{96,32},{1,65},{33,97},{65,1},{97,33},{2,66}... | collective-permute-start | bytes 737288 | tf_op jit(solution)/shard_map/ppermute | solution.py:470
  126.6 2.3 %collective-permute-start.5 = (bf16[3,32,1280]{2,1,0:T(8,128)(2,1)S(1)}, bf16[3,32,1280]{2,1,0:T(8,128)(2,1)S(1)}, u32[]{:S(2)}, u32[]{:S(2)}) collective-permute-start(bf16[3,32,1280]{2,1,0:T(8,128)(2,1)S(1)} %get-tuple-element.50), channel_id=1, source_target_pairs={{0,96},{32,0},{64,32},{96,64},{1,97},{33,1},{65,33},{97,65},{2,98}... | collective-permute-start | bytes 737288 | tf_op jit(solution)/shard_map/ppermute | solution.py:470
  128.9 0.0 collective-permute-start.6
  129.0 5.7 %collective-permute-done.6.refs_9_ = bf16[32,128]{1,0:T(8,128)(2,1)S(1)} collective-permute-done((bf16[32,128]{1,0:T(8,128)(2,1)S(1)}, bf16[32,128]{1,0:T(8,128)(2,1)S(1)}, u32[]{:S(2)}, u32[]{:S(2)}) %collective-permute-start.6) | collective-permute-done | bytes 8224 | tf_op jit(solution)/shard_map/ppermute | solution.py:473
  134.6 3.7 %collective-permute-start.7 = (bf16[32,128]{1,0:T(8,128)(2,1)S(1)}, bf16[32,128]{1,0:T(8,128)(2,1)S(1)}, u32[]{:S(2)}, u32[]{:S(2)}) collective-permute-start(bf16[32,128]{1,0:T(8,128)(2,1)S(1)} %get-tuple-element.53), channel_id=1, source_target_pairs={{0,64},{32,96},{64,0},{96,32},{1,65},{33,97},{65,1},{97,33},{2,66}... | collective-permute-start | bytes 24584 | tf_op jit(solution)/shard_map/ppermute | solution.py:473
  138.3 1.6 %collective-permute-done.7.refs_10_ = bf16[32,128]{1,0:T(8,128)(2,1)S(1)} collective-permute-done((bf16[32,128]{1,0:T(8,128)(2,1)S(1)}, bf16[32,128]{1,0:T(8,128)(2,1)S(1)}, u32[]{:S(2)}, u32[]{:S(2)}) %collective-permute-start.7) | collective-permute-done | bytes 8224 | tf_op jit(solution)/shard_map/ppermute | solution.py:473
  139.9 3.5 %collective-permute-start.8 = (bf16[32,128]{1,0:T(8,128)(2,1)S(1)}, bf16[32,128]{1,0:T(8,128)(2,1)S(1)}, u32[]{:S(2)}, u32[]{:S(2)}) collective-permute-start(bf16[32,128]{1,0:T(8,128)(2,1)S(1)} %get-tuple-element.54), channel_id=1, source_target_pairs={{0,96},{32,0},{64,32},{96,64},{1,97},{33,1},{65,33},{97,65},{2,98}... | collective-permute-start | bytes 24584 | tf_op jit(solution)/shard_map/ppermute | solution.py:473
  143.5 1.4 collective-permute-done.8.refs_11_
  144.8 2.3 %collective-permute-start.1 = (bf16[2,32,1280]{2,1,0:T(8,128)(2,1)S(1)}, bf16[2,32,1280]{2,1,0:T(8,128)(2,1)S(1)}, u32[]{:S(2)}, u32[]{:S(2)}) collective-permute-start(bf16[2,32,1280]{2,1,0:T(8,128)(2,1)S(1)} %get-tuple-element.41), channel_id=1, source_target_pairs={{0,64},{32,96},{64,0},{96,32},{1,65},{33,97},{65,1},{97,33},{2,66}... | collective-permute-start | bytes 491528 | tf_op jit(solution)/shard_map/ppermute | solution.py:470
  147.1 1.2 collective-permute-start.2
  148.3 3.3 %collective-permute-done.1.refs_2_ = bf16[2,32,1280]{2,1,0:T(8,128)(2,1)S(1)} collective-permute-done((bf16[2,32,1280]{2,1,0:T(8,128)(2,1)S(1)}, bf16[2,32,1280]{2,1,0:T(8,128)(2,1)S(1)}, u32[]{:S(2)}, u32[]{:S(2)}) %collective-permute-start.1) | collective-permute-done | bytes 163872 | tf_op jit(solution)/shard_map/ppermute | solution.py:470
  151.7 2.6 %collective-permute-done.2.refs_3_ = bf16[2,32,1280]{2,1,0:T(8,128)(2,1)S(1)} collective-permute-done((bf16[2,32,1280]{2,1,0:T(8,128)(2,1)S(1)}, bf16[2,32,1280]{2,1,0:T(8,128)(2,1)S(1)}, u32[]{:S(2)}, u32[]{:S(2)}) %collective-permute-start.2) | collective-permute-done | bytes 163872 | tf_op jit(solution)/shard_map/ppermute | solution.py:470
  154.3 1.4 assemble.1
  (29 shorter events, 0.1 us)
Async XLA Ops:
  0.0 10.1 %copy-start.5 = (s32[640]{0:T(1024)S(1)}, s32[640]{0:T(1024)}, u32[]{:S(2)}) copy-start(s32[640]{0:T(1024)} %param.7) | copy-start | bytes 7684
  0.0 10.4 %copy-start.6 = (f32[64]{0:T(128)S(1)}, f32[64]{0:T(128)}, u32[]{:S(2)}) copy-start(f32[64]{0:T(128)} %param.6) | copy-start | bytes 772
  0.0 51.3 %all-to-all-start = ((bf16[64,40,640]{2,1,0:T(8,128)(2,1)}), bf16[64,40,640]{2,1,0:T(8,128)(2,1)S(1)}, u32[]{:S(2)}, u32[]{:S(2)}) async-start(bf16[64,40,640]{2,1,0:T(8,128)(2,1)} %param.4), calls=%async_computation | async-start | bytes 6553600 | tf_op jit(solution)/shard_map/all_to_all | solution.py:424
  21.8 2.7 %copy-start.3 = (bf16[2560,1280]{1,0:T(8,128)(2,1)}, bf16[2560,1280]{1,0:T(8,128)(2,1)S(1)}, u32[]{:S(2)}) copy-start(bf16[2560,1280]{1,0:T(8,128)(2,1)S(1)} %circle.1) | copy-start | bytes 19660804
  59.2 1.8 %copy-start.4 = (bf16[128,104,128]{2,1,0:T(8,128)(2,1)}, bf16[128,104,128]{2,1,0:T(8,128)(2,1)S(1)}, u32[]{:S(2)}) copy-start(bf16[128,104,128]{2,1,0:T(8,128)(2,1)S(1)} %fourier.1) | copy-start | bytes 10223620
  61.0 52.9 %all-to-all-start.1 = ((bf16[128,104,128]{2,1,0:T(8,128)(2,1)}), bf16[128,104,128]{2,1,0:T(8,128)(2,1)S(1)}, u32[]{:S(2)}, u32[]{:S(2)}) async-start(bf16[128,104,128]{2,1,0:T(8,128)(2,1)} %copy-done.4), calls=%async_computation.1 | async-start | bytes 6815744 | tf_op jit(solution)/shard_map/all_to_all | solution.py:458
  69.9 3.3 %copy-start.2 = (bf16[640,5,1281]{0,2,1:T(8,128)(2,1)S(1)}, bf16[640,5,1281]{0,2,1:T(8,128)(2,1)}, u32[]{:S(2)}) copy-start(bf16[640,5,1281]{0,2,1:T(8,128)(2,1)} %param.5) | copy-start | bytes 24595204
  76.9 3.2 %copy-start = (bf16[5,640,1280]{2,1,0:T(8,128)(2,1)}, bf16[5,640,1280]{2,1,0:T(8,128)(2,1)S(1)}, u32[]{:S(2)}) copy-start(bf16[5,640,1280]{2,1,0:T(8,128)(2,1)S(1)} %get-tuple-element.36.basis_ref) | copy-start | bytes 24576004
  113.9 3.3 %copy-start.1 = (bf16[5,640,1280]{2,1,0:T(8,128)(2,1)S(1)}, bf16[5,640,1280]{2,1,0:T(8,128)(2,1)}, u32[]{:S(2)}) copy-start(bf16[5,640,1280]{2,1,0:T(8,128)(2,1)} %copy-done) | copy-start | bytes 24576004
  119.2 27.9 %collective-permute-start = (bf16[2,32,1280]{2,1,0:T(8,128)(2,1)S(1)}, bf16[2,32,1280]{2,1,0:T(8,128)(2,1)S(1)}, u32[]{:S(2)}, u32[]{:S(2)}) collective-permute-start(bf16[2,32,1280]{2,1,0:T(8,128)(2,1)S(1)} %get-tuple-element.40), channel_id=1, source_target_pairs={{0,32},{32,64},{64,96},{96,0},{1,33},{33,65},{65,97},{97,1},{2,34}... | collective-permute-start | bytes 491528 | tf_op jit(solution)/shard_map/ppermute | solution.py:470
  122.0 32.2 %collective-permute-start.3 = (bf16[3,32,1280]{2,1,0:T(8,128)(2,1)S(1)}, bf16[3,32,1280]{2,1,0:T(8,128)(2,1)S(1)}, u32[]{:S(2)}, u32[]{:S(2)}) collective-permute-start(bf16[3,32,1280]{2,1,0:T(8,128)(2,1)S(1)} %get-tuple-element.48), channel_id=1, source_target_pairs={{0,32},{32,64},{64,96},{96,0},{1,33},{33,65},{65,97},{97,1},{2,34}... | collective-permute-start | bytes 737288 | tf_op jit(solution)/shard_map/ppermute | solution.py:470
  124.1 30.2 %collective-permute-start.4 = (bf16[3,32,1280]{2,1,0:T(8,128)(2,1)S(1)}, bf16[3,32,1280]{2,1,0:T(8,128)(2,1)S(1)}, u32[]{:S(2)}, u32[]{:S(2)}) collective-permute-start(bf16[3,32,1280]{2,1,0:T(8,128)(2,1)S(1)} %get-tuple-element.49), channel_id=1, source_target_pairs={{0,64},{32,96},{64,0},{96,32},{1,65},{33,97},{65,1},{97,33},{2,66}... | collective-permute-start | bytes 737288 | tf_op jit(solution)/shard_map/ppermute | solution.py:470
  126.6 27.7 %collective-permute-start.5 = (bf16[3,32,1280]{2,1,0:T(8,128)(2,1)S(1)}, bf16[3,32,1280]{2,1,0:T(8,128)(2,1)S(1)}, u32[]{:S(2)}, u32[]{:S(2)}) collective-permute-start(bf16[3,32,1280]{2,1,0:T(8,128)(2,1)S(1)} %get-tuple-element.50), channel_id=1, source_target_pairs={{0,96},{32,0},{64,32},{96,64},{1,97},{33,1},{65,33},{97,65},{2,98}... | collective-permute-start | bytes 737288 | tf_op jit(solution)/shard_map/ppermute | solution.py:470
  128.9 5.7 %collective-permute-start.6 = (bf16[32,128]{1,0:T(8,128)(2,1)S(1)}, bf16[32,128]{1,0:T(8,128)(2,1)S(1)}, u32[]{:S(2)}, u32[]{:S(2)}) collective-permute-start(bf16[32,128]{1,0:T(8,128)(2,1)S(1)} %get-tuple-element.52), channel_id=1, source_target_pairs={{0,32},{32,64},{64,96},{96,0},{1,33},{33,65},{65,97},{97,1},{2,34}... | collective-permute-start | bytes 24584 | tf_op jit(solution)/shard_map/ppermute | solution.py:473
  134.6 5.3 %collective-permute-start.7 = (bf16[32,128]{1,0:T(8,128)(2,1)S(1)}, bf16[32,128]{1,0:T(8,128)(2,1)S(1)}, u32[]{:S(2)}, u32[]{:S(2)}) collective-permute-start(bf16[32,128]{1,0:T(8,128)(2,1)S(1)} %get-tuple-element.53), channel_id=1, source_target_pairs={{0,64},{32,96},{64,0},{96,32},{1,65},{33,97},{65,1},{97,33},{2,66}... | collective-permute-start | bytes 24584 | tf_op jit(solution)/shard_map/ppermute | solution.py:473
  139.9 4.9 %collective-permute-start.8 = (bf16[32,128]{1,0:T(8,128)(2,1)S(1)}, bf16[32,128]{1,0:T(8,128)(2,1)S(1)}, u32[]{:S(2)}, u32[]{:S(2)}) collective-permute-start(bf16[32,128]{1,0:T(8,128)(2,1)S(1)} %get-tuple-element.54), channel_id=1, source_target_pairs={{0,96},{32,0},{64,32},{96,64},{1,97},{33,1},{65,33},{97,65},{2,98}... | collective-permute-start | bytes 24584 | tf_op jit(solution)/shard_map/ppermute | solution.py:473
  144.8 6.8 %collective-permute-start.1 = (bf16[2,32,1280]{2,1,0:T(8,128)(2,1)S(1)}, bf16[2,32,1280]{2,1,0:T(8,128)(2,1)S(1)}, u32[]{:S(2)}, u32[]{:S(2)}) collective-permute-start(bf16[2,32,1280]{2,1,0:T(8,128)(2,1)S(1)} %get-tuple-element.41), channel_id=1, source_target_pairs={{0,64},{32,96},{64,0},{96,32},{1,65},{33,97},{65,1},{97,33},{2,66}... | collective-permute-start | bytes 491528 | tf_op jit(solution)/shard_map/ppermute | solution.py:470
  147.1 7.2 %collective-permute-start.2 = (bf16[2,32,1280]{2,1,0:T(8,128)(2,1)S(1)}, bf16[2,32,1280]{2,1,0:T(8,128)(2,1)S(1)}, u32[]{:S(2)}, u32[]{:S(2)}) collective-permute-start(bf16[2,32,1280]{2,1,0:T(8,128)(2,1)S(1)} %get-tuple-element.42), channel_id=1, source_target_pairs={{0,96},{32,0},{64,32},{96,64},{1,97},{33,1},{65,33},{97,65},{2,98}... | collective-permute-start | bytes 491528 | tf_op jit(solution)/shard_map/ppermute | solution.py:470
